TPU v7x, 512 devices: a whole 4x8x8 slice. The times are simulated.
512 devices in a mesh: chan: 128 (over y, x_lo, z), pix: 4 (over x_hi, core).
Axes of the slice: x: 4 (x_hi: 2, x_lo: 2; x = x_hi * 2 + x_lo), y: 8, z: 8, core: 2. Of those that a mesh axis runs over, the one named last changes fastest.
Arguments:
- voltages: bfloat16 [256, 2048, 256], P('chan', 'pix'), may hold values from -6 to 6
- fir_taps: float32 [4, 128], replicated, may hold values from -3 to 3
- station_of_slot: int32 [256], replicated, may hold values from 0 to 255, each once
- station_u: int32 [256], replicated, may hold values from 0 to 1023
- station_v: int32 [256], replicated, may hold values from 0 to 1023
- pixel_l: int32 [64], replicated, may hold values from -512 to 511
- pixel_m: int32 [64], replicated, may hold values from -512 to 511
Outputs:
- visibilities: float32 [128, 2, 256, 256], P('chan', None, 'pix')
- image: float32 [128, 4096], P('chan', 'pix')
Inputs may be any that keep to these rules, and one draw needn't show every extreme that they name: `station_of_slot`: each station number stands in exactly one slot.
All inputs are finite; a program needn't handle non-finite values.
Results may differ from a plain program's by a relative error of at most 0.012.
Values may be sent and summed in bfloat16 or wider, within the bound.
No kernel may reach another device: no remote copies, remote signals or barrier semaphores. Data moves between devices by JAX's collectives and lax.ppermute only.
A program may use at most 64 MiB of HBM per device.

v0:
```python
import math

import jax
import jax.numpy as jnp
from jax import lax
from jax.sharding import PartitionSpec as P

POINTS = 128
TAPS = 4
GRID = 1024


def from_behind(block, axis, distance):
    devices = range(lax.axis_size(axis))
    route = [(i - distance, i) for i in devices if i - distance in devices]
    return lax.ppermute(block, axis, route)


def dft_matrix(points):
    counter = jnp.arange(points, dtype=jnp.int32)
    product = jnp.mod(counter[:, None] * counter[None, :], points).astype(jnp.float32)
    phase_angle = product * (2.0 * math.pi / points)
    cosine = jnp.cos(phase_angle)
    sine_part = jnp.sin(phase_angle)
    upper_rows = jnp.concatenate([cosine, sine_part], axis=1)
    lower_rows = jnp.concatenate([-sine_part, cosine], axis=1)
    return (jnp.concatenate([upper_rows, lower_rows], axis=0) * points ** (-0.5)).astype(
        jnp.bfloat16
    )


def steering(channel, station_u, station_v, rows_l, pixel_m):
    grid_phase = (
        station_u[:, None, None] * rows_l[None, :, None]
        + station_v[:, None, None] * pixel_m[None, None, :]
    )
    grid_phase = jnp.mod(grid_phase, GRID).reshape(station_u.shape[0], -1)
    phase_index = jnp.mod((POINTS + channel) * grid_phase, GRID)
    phase_angle = phase_index.astype(jnp.float32) * (2.0 * math.pi / GRID)
    return (jnp.cos(phase_angle).astype(jnp.bfloat16), jnp.sin(phase_angle).astype(jnp.bfloat16))


def flag_rows(visibility):
    row_ids = jnp.arange(visibility.shape[1], dtype=jnp.int32)[:, None]
    columns = jnp.arange(visibility.shape[2], dtype=jnp.int32)[None, :]
    return jnp.where((row_ids == columns)[None], 0.0, visibility).astype(jnp.bfloat16)


def partial_image(flagged, channel, rows_l, pixel_m, station_u, station_v):
    cosine, sine_part = steering(channel, station_u, station_v, rows_l, pixel_m)
    stacked = jnp.concatenate([cosine, sine_part], axis=0)
    upper_rows = jnp.concatenate([flagged[0], flagged[1]], axis=1)
    lower_rows = jnp.concatenate([flagged[1], -flagged[0]], axis=1)
    left_matrix = jnp.concatenate([upper_rows, lower_rows], axis=0)
    weighted = jnp.dot(left_matrix, stacked, preferred_element_type=jnp.float32)
    row_count = flagged.shape[1]
    cos_rows = cosine.astype(jnp.float32)
    sin_rows = sine_part.astype(jnp.float32)
    return jnp.sum(cos_rows * weighted[:row_count] - sin_rows * weighted[row_count:], axis=0)


def on_device(voltages, fir_taps, station_of_slot, station_u, station_v, pixel_l, pixel_m):
    local_stations, spec_dev, sample_width = voltages.shape
    points = sample_width // 2
    history = from_behind(voltages[:, spec_dev - (TAPS - 1) :, :], "pix", 1)
    extended = jnp.concatenate([history, voltages], axis=1).astype(jnp.float32)
    taps_full = jnp.concatenate([fir_taps, fir_taps], axis=1)
    filtered = taps_full[0] * extended[:, TAPS - 1 : TAPS - 1 + spec_dev, :]
    for tap_index in range(1, TAPS):
        filtered = (
            filtered
            + taps_full[tap_index]
            * extended[:, TAPS - 1 - tap_index : TAPS - 1 - tap_index + spec_dev, :]
        )
    filtered = filtered.astype(jnp.bfloat16)
    dft_table = dft_matrix(points)
    spectra = jnp.einsum(
        "ok,stk->ost", dft_table, filtered, preferred_element_type=jnp.float32
    ).astype(jnp.bfloat16)
    spectra = spectra.reshape(2, points, local_stations, spec_dev)
    stations = local_stations * lax.axis_size("chan")
    slot_of_station = (
        jnp.zeros((stations,), jnp.int32)
        .at[station_of_slot]
        .set(jnp.arange(stations, dtype=jnp.int32))
    )
    ordered = jnp.take(
        lax.all_to_all(spectra, "chan", split_axis=1, concat_axis=2, tiled=True),
        slot_of_station,
        axis=2,
    )
    gram_real = jnp.einsum("rcst,rcut->csu", ordered, ordered, preferred_element_type=jnp.float32)
    cross_gram = jnp.einsum(
        "cst,cut->csu", ordered[1], ordered[0], preferred_element_type=jnp.float32
    )
    partial_value = jnp.stack([gram_real, cross_gram - jnp.swapaxes(cross_gram, 1, 2)], axis=1)
    chan_count = partial_value.shape[0]
    pix_count = lax.axis_size("pix")
    pix_index = lax.axis_index("pix")
    spectra_total = spec_dev * pix_count
    inv_total = 1.0 / spectra_total
    image_scale = math.sqrt(spectra_total) / stations
    channels = lax.axis_index("chan") * chan_count + jnp.arange(chan_count, dtype=jnp.int32)
    rows_l = pixel_l.shape[0] // pix_count
    summed = lax.psum(partial_value.astype(jnp.bfloat16), "pix").astype(jnp.float32) * inv_total
    row_count = stations // pix_count
    visibilities = lax.dynamic_slice_in_dim(summed, pix_index * row_count, row_count, 2)
    block_l = lax.dynamic_slice_in_dim(pixel_l, pix_index * rows_l, rows_l, 0)

    def whole_channel(channel_pair):
        visibility, channel = channel_pair
        return partial_image(flag_rows(visibility), channel, block_l, pixel_m, station_u, station_v)

    image = lax.map(whole_channel, (summed, channels)) * image_scale
    return (visibilities, image)


def solution(mesh):
    in_specs = (P("chan", "pix", None), P(), P(), P(), P(), P(), P())
    out_specs = (P("chan", None, "pix", None), P("chan", "pix"))
    return jax.shard_map(
        on_device, mesh=mesh, in_specs=in_specs, out_specs=out_specs, check_vma=False
    )
```

profile of v0, /device:TPU:1, one launch (start us, length us, event | category | flops | bytes accessed | tf_op | source)
XLA Modules:
  0.0 119.6 jit_solution(533256342638013136)
XLA Ops:
  7.2 0.8 slice.52
  7.9 6.0 %collective-permute-start = (bf16[2,3,256]{2,1,0:T(4,128)(2,1)S(1)}, bf16[2,3,256]{2,1,0:T(4,128)(2,1)S(1)}, u32[]{:S(2)}, u32[]{:S(2)}) collective-permute-start(bf16[2,3,256]{2,1,0:T(4,128)(2,1)S(1)} %slice.52), channel_id=1, source_target_pairs={{0,1},{1,2},{2,3},{4,5},{5,6},{6,7},{8,9},{9,10},{10,11},{12,13},{... | collective-permute-start | bytes 9224 | tf_op jit(solution)/shard_map/ppermute | solution.py:16
  14.0 0.3 fusion.44
  14.3 0.7 constant_dynamic-update-slice_fusion.1
  14.9 0.7 constant_dynamic-update-slice_fusion
  15.6 0.7 dynamic_slice.13
  16.4 0.7 broadcast_multiply_fusion.1
  17.1 0.8 broadcast_multiply_fusion
  18.0 0.3 fusion.46
  18.3 0.1 maximum_convert_fusion
  18.4 0.7 convolution_convert_fusion
  19.1 1.3 %copy.19 = bf16[2,128,2,512]{3,0,2,1:T(2,128)(2,1)} copy(bf16[2,128,2,512]{3,1,0,2:T(8,128)(2,1)S(1)} %bitcast.57) | data formatting | bytes 1048576 | tf_op jit(solution)/shard_map/reshape | solution.py:80
  20.4 17.6 %all-to-all-start = ((bf16[2,128,2,512]{3,0,2,1:T(2,128)(2,1)}), bf16[2,128,2,512]{3,0,2,1:T(2,128)(2,1)S(1)}, u32[]{:S(2)}, u32[]{:S(2)}) async-start(bf16[2,128,2,512]{3,0,2,1:T(2,128)(2,1)} %copy.19), calls=%async_computation | async-start | bytes 1048576 | tf_op jit(solution)/shard_map/all_to_all | solution.py:88
  38.1 0.3 copy.24
  38.4 1.6 %scatter_custom_fusion = s32[256]{0:T(256)S(1)} fusion(s32[256]{0:T(256)S(1)} %compare_select_fusion.1, s32[256]{0:T(256)S(1)} %iota.27, s32[]{:T(128)} %constant.76.clone.1), kind=kCustom, calls=%fused_computation.86 | custom fusion | bytes 1028 | tf_op jit(solution)/shard_map/scatter | solution.py:85
  40.1 4.3 %cosine_convert_fusion = (bf16[256,1024]{1,0:T(8,128)(2,1)S(1)}, f32[256,1024]{1,0:T(8,128)S(1)}) fusion(s32[256,1024]{1,0:T(8,128)S(1)} %copy.24, s32[]{:T(128)S(6)} %add.95), kind=kLoop, calls=%fused_computation.34 | loop fusion | flops 6815744 | bytes 2621444 | tf_op jit(solution)/shard_map/while/body/eval_jaxpr/convert_element_type | solution.py:40
  44.4 12.9 %all-to-all-done = bf16[2,128,2,512]{3,0,2,1:T(2,128)(2,1)S(1)} async-done(((bf16[2,128,2,512]{3,0,2,1:T(2,128)(2,1)}), bf16[2,128,2,512]{3,0,2,1:T(2,128)(2,1)S(1)}, u32[]{:S(2)}, u32[]{:S(2)}) %all-to-all-start) | async-done | bytes 524320 | tf_op jit(solution)/shard_map/all_to_all | solution.py:88
  57.3 1.7 %gather_fusion = bf16[256,2,512]{2,1,0:T(2,128)(2,1)S(1)} fusion(bf16[2,256,512]{2,0,1:T(2,128)(2,1)S(1)} %bitcast.56, s32[1024]{0:T(1024)S(1)} %pad_clamp_fusion), kind=kCustom, calls=%fused_computation | custom fusion | bytes 1049600 | tf_op jit(solution)/shard_map/jit(_take)/gather | solution.py:87
  59.0 1.0 fusion.56
  60.1 1.0 broadcast_select_fusion
  61.2 0.3 fusion.1
  61.5 0.7 fusion.54
  62.2 0.3 fusion.28
  62.5 0.1 copy.23
  62.7 0.7 pad_maximum_fusion
  63.5 3.4 %sine_convert_fusion = bf16[256,1024]{1,0:T(8,128)(2,1)S(1)} fusion(f32[256,1024]{1,0:T(8,128)S(1)} %get-tuple-element.19), kind=kLoop, calls=%fused_computation.33 | loop fusion | flops 262144 | bytes 1572864 | tf_op jit(solution)/shard_map/while/body/eval_jaxpr/convert_element_type | solution.py:40
  66.9 39.1 %all-reduce.2.cloned.1.call-done = bf16[1,2,256,256]{3,2,1,0:T(8,128)(2,1)} async-done(((bf16[1,2,256,256]{3,2,1,0:T(8,128)(2,1)}), bf16[1,2,256,256]{3,2,1,0:T(8,128)(2,1)}) %all-reduce.2.cloned.1.call-update) | async-done | bytes 262160 | tf_op jit(solution)/shard_map/psum | solution.py:105
  106.0 1.0 fusion.24
  107.1 0.7 fusion.13
  107.8 3.6 %fusion.8 = f32[1024]{0:T(1024)S(1)} fusion(f32[512,1024]{1,0:T(8,128)S(1)} %fusion.13, bf16[256,1024]{1,0:T(8,128)(2,1)S(1)} %get-tuple-element.18, f32[256,1024]{1,0:T(8,128)S(1)} %get-tuple-element.19), kind=kLoop, calls=%fused_computation.19 | loop fusion | flops 1833984 | bytes 3674112 | tf_op jit(solution)/shard_map/while/body/eval_jaxpr/reduce_sum | solution.py:59
  111.4 0.6 broadcast_multiply_fusion.2
  112.0 0.7 constant_dynamic-slice_fusion
  (21 shorter events, 0.3 us)
Async XLA Ops:
  7.2 11.1 %copy-start.1 = (bf16[2,512,256]{2,1,0:T(8,128)(2,1)S(1)}, bf16[2,512,256]{2,1,0:T(8,128)(2,1)}, u32[]{:S(2)}) copy-start(bf16[2,512,256]{2,1,0:T(8,128)(2,1)} %param.7) | copy-start | bytes 1572868
  7.9 10.3 %collective-permute-start = (bf16[2,3,256]{2,1,0:T(4,128)(2,1)S(1)}, bf16[2,3,256]{2,1,0:T(4,128)(2,1)S(1)}, u32[]{:S(2)}, u32[]{:S(2)}) collective-permute-start(bf16[2,3,256]{2,1,0:T(4,128)(2,1)S(1)} %slice.52), channel_id=1, source_target_pairs={{0,1},{1,2},{2,3},{4,5},{5,6},{6,7},{8,9},{9,10},{10,11},{12,13},{... | collective-permute-start | bytes 9224 | tf_op jit(solution)/shard_map/ppermute | solution.py:16
  19.1 19.0 %copy-start.2 = (s32[256]{0:T(256)S(1)}, s32[256]{0:T(256)}, u32[]{:S(2)}) copy-start(s32[256]{0:T(256)} %param.9) | copy-start | bytes 3076
  20.4 36.9 %all-to-all-start = ((bf16[2,128,2,512]{3,0,2,1:T(2,128)(2,1)}), bf16[2,128,2,512]{3,0,2,1:T(2,128)(2,1)S(1)}, u32[]{:S(2)}, u32[]{:S(2)}) async-start(bf16[2,128,2,512]{3,0,2,1:T(2,128)(2,1)} %copy.19), calls=%async_computation | async-start | bytes 1048576 | tf_op jit(solution)/shard_map/all_to_all | solution.py:88
  38.0 68.0 %all-reduce.2.cloned.1.call-start = ((), (), s32[]{:S(2)}) async-start(), calls=%async_computation.1 | async-start | bytes 524288 | tf_op jit(solution)/shard_map/psum | solution.py:105
  107.8 4.2 %copy-start = (bf16[1,2,256,256]{3,2,1,0:T(8,128)(2,1)S(1)}, bf16[1,2,256,256]{3,2,1,0:T(8,128)(2,1)}, u32[]{:S(2)}) copy-start(bf16[1,2,256,256]{3,2,1,0:T(8,128)(2,1)} %all-reduce.2.cloned.1.call-done) | copy-start | bytes 786436
Sparse Core Ops, SparseCore 0:
  63.6 42.3 all-reduce.1
where the time goes:
time: 120 us
  waiting for transfers between devices  52.1 us (43%)
  starting transfers between devices  23.6 us (20%)
  other arithmetic  18.1 us (15%)
  between operations  14.3 us (12%)
  local copies, waits for them, and re-layouts  9.43 us (8%)
  matrix products  2.01 us (2%)
    psum x1, waiting for transfers between devices, on_device(): lax.psum(partial_value.astype(jnp.bfloat16), 'pix').astype(jnp.float32)  39.1 us
    all_to_all x1, starting transfers between devices, on_device(): lax.all_to_all(spectra, 'chan', split_axis=1, concat_axis=2, tiled=True)  17.6 us
    all_to_all x1, waiting for transfers between devices, on_device(): lax.all_to_all(spectra, 'chan', split_axis=1, concat_axis=2, tiled=True)  12.9 us
    ppermute x1, starting transfers between devices, from_behind(): return lax.ppermute(block, axis, route)  6.02 us
    convert_element_type x1, other arithmetic, steering(): jnp.cos(phase_angle).astype(jnp.bfloat16)  4.27 us
    reduce_sum x1, other arithmetic, partial_image(): jnp.sum(cos_rows * weighted[:row_count] - sin_rows * weighted[row_count:]...  3.6 us
    convert_element_type x1, other arithmetic, steering(): jnp.sin(phase_angle).astype(jnp.bfloat16)  3.39 us
  transfers between devices with their start and end apart: 3, of which 2 were waited for; matrix products, arithmetic and copies ran while one was open for 12% of the time, Pallas kernels for 0%

commit v1 on v0

v1 whole, which is shorter than its diff:
```python
import math

import jax
import jax.numpy as jnp
import numpy as np
from jax import lax
from jax.experimental import pallas as pl
from jax.experimental.pallas import tpu as pltpu
from jax.sharding import PartitionSpec as P

POINTS = 128
TAPS = 4
GRID = 1024
LANES = 128
STATIONS = 256
HALO = 8

VMEM = pl.BlockSpec(memory_space=pltpu.VMEM)
SMEM = pl.BlockSpec(memory_space=pltpu.SMEM)
F32 = jnp.float32
BF16 = jnp.bfloat16


def dft_matrix(points):
    counter = np.arange(points)
    angle = np.mod(counter[:, None] * counter[None, :], points) * (2.0 * math.pi / points)
    cosine, sine = np.cos(angle), np.sin(angle)
    table = np.block([[cosine, sine], [-sine, cosine]]) * points ** (-0.5)
    return jnp.asarray(table, dtype=F32).astype(BF16)


def params(flops, moved):
    return dict(
        compiler_params=pltpu.CompilerParams(vmem_limit_bytes=40 * 1024 * 1024),
        cost_estimate=pl.CostEstimate(flops=flops, bytes_accessed=moved, transcendentals=0),
    )


def filter_kernel(v_ref, hist_ref, taps_ref, dft_ref, out_ref, ext, wide):
    spec_dev = v_ref.shape[1]
    taps = jnp.concatenate([taps_ref[...], taps_ref[...]], axis=1)
    step = 256
    for s in range(2):
        ext[s, 0:HALO, :] = hist_ref[s].astype(F32)
        ext[s, HALO:, :] = v_ref[s].astype(F32)
    for s in range(2):
        for t in range(0, spec_dev, step):
            total = taps[0:1] * ext[s, HALO + t : HALO + t + step, :]
            for k in range(1, TAPS):
                total = total + taps[k : k + 1] * ext[s, HALO - k + t : HALO - k + t + step, :]
            spectra = lax.dot_general(
                dft_ref[...], total.astype(BF16), (((1,), (1,)), ((), ())), preferred_element_type=F32
            )
            for r in range(2):
                for part in range(step // LANES):
                    row = s * 8 + r * 4 + t // LANES + part
                    wide[pl.ds(row, POINTS, stride=16), :] = spectra[
                        r * POINTS : (r + 1) * POINTS, part * LANES : (part + 1) * LANES
                    ]
    for c in range(0, POINTS, 16):
        out_ref[c : c + 16] = wide[c * 16 : (c + 16) * 16, :].astype(BF16).reshape(16, 16, LANES)


def filter_bank(voltages, history, fir_taps):
    return pl.pallas_call(
        filter_kernel,
        out_shape=jax.ShapeDtypeStruct((POINTS, 16, LANES), BF16),
        in_specs=[VMEM] * 4,
        out_specs=VMEM,
        scratch_shapes=[
            pltpu.VMEM((2, HALO + voltages.shape[1], 2 * POINTS), F32),
            pltpu.VMEM((POINTS * 16, LANES), F32),
        ],
        name="filter_bank",
        **params(2 * 256 * 256 * 1024, 1 << 20),
    )(voltages, history, fir_taps, dft_matrix(POINTS))


def steering_kernel(chan_ref, u_ref, v_ref, l_ref, m_ref, cos_ref, sin_ref):
    freq = POINTS + chan_ref[0]
    rows = lax.broadcasted_iota(jnp.int32, (STATIONS, STATIONS), 0)
    cols = lax.broadcasted_iota(jnp.int32, (STATIONS, STATIONS), 1)
    eye = rows == cols

    def column(ref):
        return jnp.sum(jnp.where(eye, ref[...], 0), axis=1, keepdims=True)

    def phases(station, pixel):
        index = (freq * ((station * pixel) & (GRID - 1))) & (GRID - 1)
        angle = index.astype(F32) * (2.0 * math.pi / GRID)
        return jnp.cos(angle), jnp.sin(angle)

    l_cos, l_sin = phases(column(u_ref), l_ref[...])
    m_cos, m_sin = phases(column(v_ref), m_ref[...])
    first = lax.broadcasted_iota(jnp.int32, (STATIONS, LANES), 1) < 64
    for q in range(cos_ref.shape[1] // LANES):
        a_cos = jnp.where(first, l_cos[:, 2 * q : 2 * q + 1], l_cos[:, 2 * q + 1 : 2 * q + 2])
        a_sin = jnp.where(first, l_sin[:, 2 * q : 2 * q + 1], l_sin[:, 2 * q + 1 : 2 * q + 2])
        cos_ref[:, q * LANES : (q + 1) * LANES] = (a_cos * m_cos - a_sin * m_sin).astype(BF16)
        sin_ref[:, q * LANES : (q + 1) * LANES] = (a_sin * m_cos + a_cos * m_sin).astype(BF16)


def steering(channel, station_u, station_v, rows_l, pixel_m, pixels):
    out = jax.ShapeDtypeStruct((STATIONS, pixels), BF16)
    return pl.pallas_call(
        steering_kernel,
        out_shape=(out, out),
        in_specs=[SMEM] + [VMEM] * 4,
        out_specs=(VMEM, VMEM),
        name="steering",
        **params(6 * STATIONS * pixels, 4 * STATIONS * pixels),
    )(channel, station_u, station_v, rows_l, pixel_m)


def gram_kernel(recv_ref, station_ref, out_ref, wide, slots):
    for c in range(0, POINTS, 16):
        wide[c * 16 : (c + 16) * 16, :] = recv_ref[c : c + 16].reshape(256, LANES).astype(F32)
    for s in range(2):
        for q in range(8):
            slots[s * POINTS : (s + 1) * POINTS, q * LANES : (q + 1) * LANES] = wide[
                pl.ds(s * 8 + q, POINTS, stride=16), :
            ].astype(BF16)
    rows = lax.broadcasted_iota(jnp.int32, (STATIONS, STATIONS), 0)
    select = jnp.where(rows == station_ref[...], 1.0, 0.0).astype(BF16)
    ordered = jnp.dot(select, slots[...], preferred_element_type=F32).astype(BF16)
    half = ordered.shape[1] // 2
    turned = jnp.concatenate([ordered[:, half:], -ordered[:, :half]], axis=1)
    contract = (((1,), (1,)), ((), ()))
    out_ref[0] = lax.dot_general(ordered, ordered, contract, preferred_element_type=F32).astype(BF16)
    out_ref[1] = lax.dot_general(turned, ordered, contract, preferred_element_type=F32).astype(BF16)


def gram(received, station_row):
    return pl.pallas_call(
        gram_kernel,
        out_shape=jax.ShapeDtypeStruct((2, STATIONS, STATIONS), BF16),
        in_specs=[VMEM] * 2,
        out_specs=VMEM,
        scratch_shapes=[
            pltpu.VMEM((POINTS * 16, LANES), F32),
            pltpu.VMEM((STATIONS, 1024), BF16),
        ],
        name="gram",
        **params(6 * 256 * 256 * 1024, 1 << 20),
    )(received, station_row)


def image_kernel(place_ref, own_ref, other_ref, cos_ref, sin_ref, rows_ref, pixels_ref, send_ref, real, imag):
    rows = lax.broadcasted_iota(jnp.int32, (STATIONS, STATIONS), 0)
    cols = lax.broadcasted_iota(jnp.int32, (STATIONS, STATIONS), 1)
    real[...] = own_ref[0].astype(F32) + other_ref[0].astype(F32)
    imag[...] = own_ref[1].astype(F32) + other_ref[1].astype(F32)
    count = rows_ref.shape[1]
    here = pl.ds(pl.multiple_of(place_ref[0] * count, count), count)
    across = pl.ds(pl.multiple_of(place_ref[1] * count, count), count)
    rows_ref[0] = real[here, :]
    rows_ref[1] = imag[here, :]
    send_ref[0:count, :] = real[across, :].astype(BF16)
    send_ref[count : 2 * count, :] = imag[across, :].astype(BF16)
    flag_real = jnp.where(rows == cols, 0.0, real[...]).astype(BF16)
    flag_imag = jnp.where(rows == cols, 0.0, imag[...]).astype(BF16)
    width = 256
    groups = cos_ref.shape[1] // width
    for q in range(groups):
        cosine = cos_ref[:, q * width : (q + 1) * width]
        sine = sin_ref[:, q * width : (q + 1) * width]
        upper = jnp.dot(flag_real, cosine, preferred_element_type=F32) + 2.0 * jnp.dot(
            flag_imag, sine, preferred_element_type=F32
        )
        lower = jnp.dot(flag_real, sine, preferred_element_type=F32)
        pixel = jnp.sum(cosine.astype(F32) * upper + sine.astype(F32) * lower, axis=0, keepdims=True)
        if q < groups // 2:
            pixels_ref[q : q + 1, :] = pixel
        else:
            at = 2 * count + q - groups // 2
            send_ref[at : at + 1, :] = pixel.astype(BF16)
    send_ref[2 * count + groups // 2 :, :] = jnp.zeros_like(send_ref[2 * count + groups // 2 :, :])


def image_rows(place, own, other, cosine, sine, count):
    groups = cosine.shape[1] // 512
    return pl.pallas_call(
        image_kernel,
        out_shape=(
            jax.ShapeDtypeStruct((2, count, STATIONS), F32),
            jax.ShapeDtypeStruct((groups, STATIONS), F32),
            jax.ShapeDtypeStruct((2 * count + 16, STATIONS), BF16),
        ),
        in_specs=[SMEM] + [VMEM] * 4,
        out_specs=(VMEM, VMEM, VMEM),
        scratch_shapes=[pltpu.VMEM((STATIONS, STATIONS), F32)] * 2,
        name="image_rows",
        **params(6 * 256 * 256 * 2048, 1 << 21),
    )(place, own, other, cosine, sine)


def finish_kernel(inv_total, image_scale, rows_ref, pixels_ref, got_ref, vis_ref, image_ref):
    count = rows_ref.shape[1]
    for part in range(2):
        got = got_ref[part * count : (part + 1) * count, :].astype(F32)
        vis_ref[0, part] = (rows_ref[part] + got) * inv_total
    for q in range(pixels_ref.shape[0]):
        got = got_ref[2 * count + q : 2 * count + q + 1, :].astype(F32)
        image_ref[:, q * STATIONS : (q + 1) * STATIONS] = (pixels_ref[q : q + 1, :] + got) * (
            inv_total * image_scale
        )


def finish(rows, pixels, got, inv_total, image_scale):
    count = rows.shape[1]
    return pl.pallas_call(
        lambda *refs: finish_kernel(inv_total, image_scale, *refs),
        out_shape=(
            jax.ShapeDtypeStruct((1, 2, count, STATIONS), F32),
            jax.ShapeDtypeStruct((1, pixels.size), F32),
        ),
        in_specs=[VMEM] * 3,
        out_specs=(VMEM, VMEM),
        name="finish",
        **params(1 << 16, 1 << 18),
    )(rows, pixels, got)


def on_device(voltages, fir_taps, station_of_slot, station_u, station_v, pixel_l, pixel_m):
    spec_dev = voltages.shape[1]
    pix_count = lax.axis_size("pix")
    spectra_total = spec_dev * pix_count
    pix = lax.axis_index("pix")
    across = jnp.where(pix < 2, pix + 2, pix - 2)
    rows_l = pixel_l.shape[0] // pix_count
    history = lax.ppermute(
        voltages[:, spec_dev - HALO :, :], "pix", [(i, i + 1) for i in range(pix_count - 1)]
    )
    sent = filter_bank(voltages, history, fir_taps)
    received = lax.all_to_all(sent, "chan", split_axis=0, concat_axis=0, tiled=True)

    block_l = jnp.concatenate(
        [
            lax.dynamic_slice_in_dim(pixel_l, pix * rows_l, rows_l, 0),
            lax.dynamic_slice_in_dim(pixel_l, across * rows_l, rows_l, 0),
            jnp.zeros((LANES - 2 * rows_l,), jnp.int32),
        ]
    )[None]
    cosine, sine = steering(
        lax.axis_index("chan")[None].astype(jnp.int32),
        station_u[None],
        station_v[None],
        block_l,
        jnp.concatenate([pixel_m, pixel_m])[None],
        2 * rows_l * pixel_m.shape[0],
    )
    station_row = station_of_slot.reshape(POINTS, 2).T.reshape(1, STATIONS)
    own = gram(received, station_row)
    other = lax.ppermute(own, "pix", [(0, 1), (1, 0), (2, 3), (3, 2)])
    place = jnp.stack([pix, across]).astype(jnp.int32)
    rows, pixels, send = image_rows(place, own, other, cosine, sine, STATIONS // pix_count)
    got = lax.ppermute(send, "pix", [(0, 2), (2, 0), (1, 3), (3, 1)])
    return finish(rows, pixels, got, 1.0 / spectra_total, math.sqrt(spectra_total) / STATIONS)


def solution(mesh):
    in_specs = (P("chan", "pix", None), P(), P(), P(), P(), P(), P())
    out_specs = (P("chan", None, "pix", None), P("chan", "pix"))
    return jax.shard_map(
        on_device, mesh=mesh, in_specs=in_specs, out_specs=out_specs, check_vma=False
    )
```

time: 120 us -> 65.8 us (0.55)
  waiting for transfers between devices: 52.1 us -> 23.5 us
  other arithmetic: 18.1 us -> 0.15 us
  between operations: 14.3 us -> 0.73 us
  Pallas kernels: 0 us -> 8.24 us
  local copies, waits for them, and re-layouts: 9.43 us -> 4.94 us
  starting transfers between devices: 23.6 us -> 27.8 us
  matrix products: 2.01 us -> 0 us
    psum x1 -> x0, waiting for transfers between devices: 39.1 us -> none  [on_device(): lax.psum(partial_value.astype(jnp.bfloat16), 'pix').astype(jnp.float32)]
    convert_element_type x4 -> x0, other arithmetic: 8.81 us -> none  [the longest x1 4.27 us: steering(): jnp.cos(phase_angle).astype(jnp.bfloat16)]
    pallas_call x0 -> x5, Pallas kernels: none -> 8.24 us  [the longest x1 3.33 us: steering(): pl.pallas_call(steering_kernel, out_shape=(out, out), in_specs=[SMEM] + [...]
    ppermute x1 -> x3, starting transfers between devices: 6.02 us -> 12.2 us  [the longest x1 6.02 us: on_device(): lax.ppermute(voltages[:, spec_dev - HALO:, :], 'pix', [(i, i + 1) for i i...]
    all_to_all x1, waiting for transfers between devices: 12.9 us -> 18.4 us  [on_device(): lax.all_to_all(sent, 'chan', split_axis=0, concat_axis=0, tiled=True)]
    ppermute x1 -> x3, waiting for transfers between devices: 0.01 us -> 5.09 us  [the longest x1 2.74 us: on_device(): lax.ppermute(voltages[:, spec_dev - HALO:, :], 'pix', [(i, i + 1) for i i...]
    reduce_sum x1 -> x0, other arithmetic: 3.6 us -> none  [partial_image(): jnp.sum(cos_rows * weighted[:row_count] - sin_rows * weighted[row_count:]...]
    unnamed x7 -> x16, local copies, waits for them, and re-layouts: 0.7 us -> 3.96 us
  transfers between devices with their start and end apart: 3 -> 4, of which waited for: 2 -> 3; matrix products, arithmetic and copies ran while one was open for 12% -> 1% of each run, Pallas kernels for 0% -> 5%
where the time goes in v1:
time: 65.8 us; the launch traced here: 65.4 us
  starting transfers between devices  27.8 us (42%)
  waiting for transfers between devices  23.5 us (36%)
  Pallas kernels  8.24 us (13%)
  local copies, waits for them, and re-layouts  4.94 us (8%)
  between operations  0.73 us (1%)
    all_to_all x1, waiting for transfers between devices, on_device(): lax.all_to_all(sent, 'chan', split_axis=0, concat_axis=0, tiled=True)  18.4 us
    all_to_all x1, starting transfers between devices, on_device(): lax.all_to_all(sent, 'chan', split_axis=0, concat_axis=0, tiled=True)  15.6 us
    ppermute x1, starting transfers between devices, on_device(): lax.ppermute(voltages[:, spec_dev - HALO:, :], 'pix', [(i, i + 1) for i i...  6.02 us
    ppermute x1, starting transfers between devices, on_device(): got = lax.ppermute(send, 'pix', [(0, 2), (2, 0), (1, 3), (3, 1)])  4.24 us
    unnamed x16, local copies, waits for them, and re-layouts  3.96 us
    pallas_call x1, Pallas kernels, steering(): pl.pallas_call(steering_kernel, out_shape=(out, out), in_specs=[SMEM] + [...  3.33 us
    ppermute x1, waiting for transfers between devices, on_device(): lax.ppermute(voltages[:, spec_dev - HALO:, :], 'pix', [(i, i + 1) for i i...  2.74 us
    ppermute x1, waiting for transfers between devices, on_device(): got = lax.ppermute(send, 'pix', [(0, 2), (2, 0), (1, 3), (3, 1)])  2.35 us
  transfers between devices with their start and end apart: 4, of which 3 were waited for; matrix products, arithmetic and copies ran while one was open for 1% of the time, Pallas kernels for 5%

profile of v1, /device:TPU:1, one launch (start us, length us, event | category | flops | bytes accessed | tf_op | source)
XLA Modules:
  0.0 65.4 jit_solution(7638585393888837751)
XLA Ops:
  0.6 0.0 copy-start.2
  0.6 0.7 %slice.3 = bf16[2,8,256]{2,1,0:T(8,128)(2,1)S(1)} slice(bf16[2,512,256]{2,1,0:T(8,128)(2,1)} %v_ref.1), slice={[0:2], [504:512], [0:256]} | slice | bytes 16384 | tf_op jit(solution)/shard_map/slice | solution.py:232
  1.3 6.0 %collective-permute-start = (bf16[2,8,256]{2,1,0:T(8,128)(2,1)S(1)}, bf16[2,8,256]{2,1,0:T(8,128)(2,1)S(1)}, u32[]{:S(2)}, u32[]{:S(2)}) collective-permute-start(bf16[2,8,256]{2,1,0:T(8,128)(2,1)S(1)} %slice.3), channel_id=1, source_target_pairs={{0,1},{1,2},{2,3},{4,5},{5,6},{6,7},{8,9},{9,10},{10,11},{12,13},{... | collective-permute-start | bytes 24584 | tf_op jit(solution)/shard_map/ppermute | solution.py:231
  7.4 2.7 %collective-permute-done.hist_ref = bf16[2,8,256]{2,1,0:T(8,128)(2,1)S(1)} collective-permute-done((bf16[2,8,256]{2,1,0:T(8,128)(2,1)S(1)}, bf16[2,8,256]{2,1,0:T(8,128)(2,1)S(1)}, u32[]{:S(2)}, u32[]{:S(2)}) %collective-permute-start) | collective-permute-done | bytes 8224 | tf_op jit(solution)/shard_map/ppermute | solution.py:231
  10.1 0.0 copy-done.2
  10.1 0.0 copy-start
  10.1 1.0 %copy-done = bf16[2,512,256]{2,1,0:T(8,128)(2,1)S(1)} copy-done((bf16[2,512,256]{2,1,0:T(8,128)(2,1)S(1)}, bf16[2,512,256]{2,1,0:T(8,128)(2,1)}, u32[]{:S(2)}) %copy-start) | copy-done | bytes 524312
  11.2 0.0 copy-start.1
  11.2 0.9 %copy-done.1 = bf16[256,256]{1,0:T(8,128)(2,1)S(1)} copy-done((bf16[256,256]{1,0:T(8,128)(2,1)S(1)}, bf16[256,256]{1,0:T(8,128)(2,1)}, u32[]{:S(2)}) %copy-start.1) | copy-done | bytes 131096
  12.1 1.7 %filter_bank.1 = bf16[128,16,128]{2,1,0:T(8,128)(2,1)} custom-call(bf16[2,512,256]{2,1,0:T(8,128)(2,1)S(1)} %copy-done, bf16[2,8,256]{2,1,0:T(8,128)(2,1)S(1)} %collective-permute-done.hist_ref, f32[4,128]{1,0:T(4,128)S(1)} %copy-done.2, bf16[256,256]{1,0:T(8,128)(2,1)S(1)} %copy-done.1), custom_call_target="tpu_custom_call" | custom-call | flops 134217728 | bytes 1048576 | tf_op jit(solution)/shard_map/filter_bank/pallas_call | solution.py:65
  13.7 15.6 %all-to-all-start = ((bf16[128,16,128]{2,1,0:T(8,128)(2,1)}), bf16[128,16,128]{2,1,0:T(8,128)(2,1)S(1)}, u32[]{:S(2)}, u32[]{:S(2)}) async-start(bf16[128,16,128]{2,1,0:T(8,128)(2,1)} %filter_bank.1), calls=%async_computation | async-start | bytes 1048576 | tf_op jit(solution)/shard_map/all_to_all | solution.py:235
  29.3 0.0 copy-start.6
  29.3 0.7 %copy-done.6 = s32[256]{0:T(256)S(1)} copy-done((s32[256]{0:T(256)S(1)}, s32[256]{0:T(256)}, u32[]{:S(2)}) %copy-start.6) | copy-done | bytes 1048
  30.0 0.1 reshape.10
  30.1 0.1 copy.10
  30.2 18.4 %all-to-all-done.recv_ref = bf16[128,16,128]{2,1,0:T(8,128)(2,1)S(1)} async-done(((bf16[128,16,128]{2,1,0:T(8,128)(2,1)}), bf16[128,16,128]{2,1,0:T(8,128)(2,1)S(1)}, u32[]{:S(2)}, u32[]{:S(2)}) %all-to-all-start) | async-done | bytes 524320 | tf_op jit(solution)/shard_map/all_to_all | solution.py:235
  48.7 0.0 copy-start.5
  48.7 0.9 %gram.1.own_ref = bf16[2,256,256]{2,1,0:T(8,128)(2,1)S(1)} custom-call(bf16[128,16,128]{2,1,0:T(8,128)(2,1)S(1)} %all-to-all-done.recv_ref, s32[1,256]{1,0:T(1,128)S(1)} %bitcast.11), custom_call_target="tpu_custom_call" | custom-call | flops 402653184 | bytes 1048576 | tf_op jit(solution)/shard_map/gram/pallas_call | solution.py:134
  49.6 1.9 %collective-permute-start.1 = (bf16[2,256,256]{2,1,0:T(8,128)(2,1)S(1)}, bf16[2,256,256]{2,1,0:T(8,128)(2,1)S(1)}, u32[]{:S(2)}, u32[]{:S(2)}) collective-permute-start(bf16[2,256,256]{2,1,0:T(8,128)(2,1)S(1)} %gram.1.own_ref), channel_id=1, source_target_pairs={{0,1},{1,0},{2,3},{3,2},{4,5},{5,4},{6,7},{7,6},{8,9},{9,8},{10,11... | collective-permute-start | bytes 786440 | tf_op jit(solution)/shard_map/ppermute | solution.py:254
  51.5 0.0 copy-done.5
  51.5 0.1 fusion
  51.6 0.7 copy-done.7
  52.3 0.1 add_bitcast_fusion
  52.4 0.0 copy-done.4
  52.4 0.7 %copy-done.3 = s32[256]{0:T(256)S(1)} copy-done((s32[256]{0:T(256)S(1)}, s32[256]{0:T(256)}, u32[]{:S(2)}) %copy-start.3) | copy-done | bytes 1048
  53.0 3.3 %steering.1 = (bf16[256,2048]{1,0:T(8,128)(2,1)S(1)}, bf16[256,2048]{1,0:T(8,128)(2,1)S(1)}) custom-call(s32[1]{0:T(128)} %bitcast.4.chan_ref, s32[1,256]{1,0:T(1,128)S(1)} %bitcast.12, s32[1,256]{1,0:T(1,128)S(1)} %bitcast.13, s32[1,128]{1,0:T(1,128)S(1)} %get-tuple-element.14.l_ref, s32[1,128]{1,0:T(1,128)S(1)} %get-tuple-element.15.m_ref), custom_call_target="tpu_custom_call" | custom-call | flops 3145728 | bytes 2097152 | tf_op jit(solution)/shard_map/steering/pallas_call | solution.py:105
  56.4 0.1 pad_add_fusion.place_ref
  56.4 0.0 collective-permute-done.1.other_ref
  56.4 1.6 %image_rows.1 = (f32[2,64,256]{2,1,0:T(8,128)S(1)}, f32[4,256]{1,0:T(4,128)S(1)}, bf16[144,256]{1,0:T(8,128)(2,1)S(1)}) custom-call(s32[2]{0:T(128)S(1)} %pad_add_fusion.place_ref, bf16[2,256,256]{2,1,0:T(8,128)(2,1)S(1)} %gram.1.own_ref, bf16[2,256,256]{2,1,0:T(8,128)(2,1)S(1)} %collective-permute-done.1.other_ref, ...), custom_call_target="tpu_custom_call" | custom-call | flops 805306368 | bytes 2097152 | tf_op jit(solution)/shard_map/image_rows/pallas_call | solution.py:182
  58.1 4.2 %collective-permute-start.2 = (bf16[144,256]{1,0:T(8,128)(2,1)S(1)}, bf16[144,256]{1,0:T(8,128)(2,1)S(1)}, u32[]{:S(2)}, u32[]{:S(2)}) collective-permute-start(bf16[144,256]{1,0:T(8,128)(2,1)S(1)} %get-tuple-element.11), channel_id=1, source_target_pairs={{0,2},{2,0},{1,3},{3,1},{4,6},{6,4},{5,7},{7,5},{8,10},{10,8},{9,1... | collective-permute-start | bytes 221192 | tf_op jit(solution)/shard_map/ppermute | solution.py:257
  62.3 2.3 %collective-permute-done.2.refs_2_ = bf16[144,256]{1,0:T(8,128)(2,1)S(1)} collective-permute-done((bf16[144,256]{1,0:T(8,128)(2,1)S(1)}, bf16[144,256]{1,0:T(8,128)(2,1)S(1)}, u32[]{:S(2)}, u32[]{:S(2)}) %collective-permute-start.2) | collective-permute-done | bytes 73760 | tf_op jit(solution)/shard_map/ppermute | solution.py:257
  64.7 0.7 %finish.1 = (f32[1,2,64,256]{3,2,1,0:T(8,128)}, f32[1,1024]{1,0:T(1,128)}) custom-call(f32[2,64,256]{2,1,0:T(8,128)S(1)} %get-tuple-element.9.refs_0_, f32[4,256]{1,0:T(4,128)S(1)} %get-tuple-element.10.refs_1_, bf16[144,256]{1,0:T(8,128)(2,1)S(1)} %collective-permute-done.2.refs_2_), custom_call_target="tpu_custom_call" | custom-call | flops 65536 | bytes 262144 | tf_op jit(solution)/shard_map/finish/pallas_call | solution.py:211
  (4 shorter events, 0.0 us)
Async XLA Ops:
  0.6 9.5 %copy-start.2 = (f32[4,128]{1,0:T(4,128)S(1)}, f32[4,128]{1,0:T(4,128)}, u32[]{:S(2)}) copy-start(f32[4,128]{1,0:T(4,128)} %taps_ref.1) | copy-start | bytes 6148
  1.3 8.8 %collective-permute-start = (bf16[2,8,256]{2,1,0:T(8,128)(2,1)S(1)}, bf16[2,8,256]{2,1,0:T(8,128)(2,1)S(1)}, u32[]{:S(2)}, u32[]{:S(2)}) collective-permute-start(bf16[2,8,256]{2,1,0:T(8,128)(2,1)S(1)} %slice.3), channel_id=1, source_target_pairs={{0,1},{1,2},{2,3},{4,5},{5,6},{6,7},{8,9},{9,10},{10,11},{12,13},{... | collective-permute-start | bytes 24584 | tf_op jit(solution)/shard_map/ppermute | solution.py:231
  10.1 1.0 %copy-start = (bf16[2,512,256]{2,1,0:T(8,128)(2,1)S(1)}, bf16[2,512,256]{2,1,0:T(8,128)(2,1)}, u32[]{:S(2)}) copy-start(bf16[2,512,256]{2,1,0:T(8,128)(2,1)} %v_ref.1) | copy-start | bytes 1572868
  11.2 0.9 %copy-start.1 = (bf16[256,256]{1,0:T(8,128)(2,1)S(1)}, bf16[256,256]{1,0:T(8,128)(2,1)}, u32[]{:S(2)}) copy-start(bf16[256,256]{1,0:T(8,128)(2,1)} %constant.24.dft_ref) | copy-start | bytes 393220
  13.7 34.9 %all-to-all-start = ((bf16[128,16,128]{2,1,0:T(8,128)(2,1)}), bf16[128,16,128]{2,1,0:T(8,128)(2,1)S(1)}, u32[]{:S(2)}, u32[]{:S(2)}) async-start(bf16[128,16,128]{2,1,0:T(8,128)(2,1)} %filter_bank.1), calls=%async_computation | async-start | bytes 1048576 | tf_op jit(solution)/shard_map/all_to_all | solution.py:235
  29.3 0.7 %copy-start.6 = (s32[256]{0:T(256)S(1)}, s32[256]{0:T(256)}, u32[]{:S(2)}) copy-start(s32[256]{0:T(256)} %param.10) | copy-start | bytes 3076
  48.7 2.9 %copy-start.5 = (s32[64]{0:T(128)S(1)}, s32[64]{0:T(128)}, u32[]{:S(2)}) copy-start(s32[64]{0:T(128)} %param.13) | copy-start | bytes 772
  48.7 3.7 %copy-start.4 = (s32[256]{0:T(256)S(1)}, s32[256]{0:T(256)}, u32[]{:S(2)}) copy-start(s32[256]{0:T(256)} %param.12) | copy-start | bytes 3076
  49.6 6.9 %collective-permute-start.1 = (bf16[2,256,256]{2,1,0:T(8,128)(2,1)S(1)}, bf16[2,256,256]{2,1,0:T(8,128)(2,1)S(1)}, u32[]{:S(2)}, u32[]{:S(2)}) collective-permute-start(bf16[2,256,256]{2,1,0:T(8,128)(2,1)S(1)} %gram.1.own_ref), channel_id=1, source_target_pairs={{0,1},{1,0},{2,3},{3,2},{4,5},{5,4},{6,7},{7,6},{8,9},{9,8},{10,11... | collective-permute-start | bytes 786440 | tf_op jit(solution)/shard_map/ppermute | solution.py:254
  51.6 0.7 %copy-start.7 = (s32[64]{0:T(128)S(1)}, s32[64]{0:T(128)}, u32[]{:S(2)}) copy-start(s32[64]{0:T(128)} %param.14) | copy-start | bytes 772
  52.3 0.7 %copy-start.3 = (s32[256]{0:T(256)S(1)}, s32[256]{0:T(256)}, u32[]{:S(2)}) copy-start(s32[256]{0:T(256)} %param.11) | copy-start | bytes 3076
  58.1 6.6 %collective-permute-start.2 = (bf16[144,256]{1,0:T(8,128)(2,1)S(1)}, bf16[144,256]{1,0:T(8,128)(2,1)S(1)}, u32[]{:S(2)}, u32[]{:S(2)}) collective-permute-start(bf16[144,256]{1,0:T(8,128)(2,1)S(1)} %get-tuple-element.11), channel_id=1, source_target_pairs={{0,2},{2,0},{1,3},{3,1},{4,6},{6,4},{5,7},{7,5},{8,10},{10,8},{9,1... | collective-permute-start | bytes 221192 | tf_op jit(solution)/shard_map/ppermute | solution.py:257

commit v2 on v1

--- a/solution.py
+++ b/solution.py
@@ -16,6 +16,8 @@
 HALO = 8
 
 VMEM = pl.BlockSpec(memory_space=pltpu.VMEM)
+HBM = pl.BlockSpec(memory_space=pltpu.HBM)
+ANY = pl.BlockSpec(memory_space=pl.ANY)
 SMEM = pl.BlockSpec(memory_space=pltpu.SMEM)
 F32 = jnp.float32
 BF16 = jnp.bfloat16
@@ -36,14 +38,20 @@
     )
 
 
-def filter_kernel(v_ref, hist_ref, taps_ref, dft_ref, out_ref, ext, wide):
+def filter_kernel(v_hbm, hist_ref, taps_ref, dft_hbm, out_ref, v_ref, dft_ref, ext, wide, sems):
     spec_dev = v_ref.shape[1]
+    copies = [pltpu.make_async_copy(v_hbm.at[s], v_ref.at[s], sems.at[s]) for s in range(2)]
+    copies.append(pltpu.make_async_copy(dft_hbm, dft_ref, sems.at[2]))
+    for copy in copies:
+        copy.start()
     taps = jnp.concatenate([taps_ref[...], taps_ref[...]], axis=1)
     step = 256
     for s in range(2):
         ext[s, 0:HALO, :] = hist_ref[s].astype(F32)
+        copies[s].wait()
         ext[s, HALO:, :] = v_ref[s].astype(F32)
-    for s in range(2):
+        if s == 0:
+            copies[2].wait()
         for t in range(0, spec_dev, step):
             total = taps[0:1] * ext[s, HALO + t : HALO + t + step, :]
             for k in range(1, TAPS):
@@ -65,11 +73,14 @@
     return pl.pallas_call(
         filter_kernel,
         out_shape=jax.ShapeDtypeStruct((POINTS, 16, LANES), BF16),
-        in_specs=[VMEM] * 4,
+        in_specs=[HBM, VMEM, VMEM, HBM],
         out_specs=VMEM,
         scratch_shapes=[
+            pltpu.VMEM(voltages.shape, BF16),
+            pltpu.VMEM((2 * POINTS, 2 * POINTS), BF16),
             pltpu.VMEM((2, HALO + voltages.shape[1], 2 * POINTS), F32),
             pltpu.VMEM((POINTS * 16, LANES), F32),
+            pltpu.SemaphoreType.DMA((3,)),
         ],
         name="filter_bank",
         **params(2 * 256 * 256 * 1024, 1 << 20),
@@ -112,7 +123,7 @@
     )(channel, station_u, station_v, rows_l, pixel_m)
 
 
-def gram_kernel(recv_ref, station_ref, out_ref, wide, slots):
+def gram_kernel(recv_ref, station_ref, after_ref, out_ref, wide, slots):
     for c in range(0, POINTS, 16):
         wide[c * 16 : (c + 16) * 16, :] = recv_ref[c : c + 16].reshape(256, LANES).astype(F32)
     for s in range(2):
@@ -130,11 +141,11 @@
     out_ref[1] = lax.dot_general(turned, ordered, contract, preferred_element_type=F32).astype(BF16)
 
 
-def gram(received, station_row):
+def gram(received, station_row, after):
     return pl.pallas_call(
         gram_kernel,
         out_shape=jax.ShapeDtypeStruct((2, STATIONS, STATIONS), BF16),
-        in_specs=[VMEM] * 2,
+        in_specs=[VMEM, VMEM, ANY],
         out_specs=VMEM,
         scratch_shapes=[
             pltpu.VMEM((POINTS * 16, LANES), F32),
@@ -142,7 +153,7 @@
         ],
         name="gram",
         **params(6 * 256 * 256 * 1024, 1 << 20),
-    )(received, station_row)
+    )(received, station_row, after)
 
 
 def image_kernel(place_ref, own_ref, other_ref, cos_ref, sin_ref, rows_ref, pixels_ref, send_ref, real, imag):
@@ -250,7 +261,7 @@
         2 * rows_l * pixel_m.shape[0],
     )
     station_row = station_of_slot.reshape(POINTS, 2).T.reshape(1, STATIONS)
-    own = gram(received, station_row)
+    own = gram(received, station_row, cosine)
     other = lax.ppermute(own, "pix", [(0, 1), (1, 0), (2, 3), (3, 2)])
     place = jnp.stack([pix, across]).astype(jnp.int32)
     rows, pixels, send = image_rows(place, own, other, cosine, sine, STATIONS // pix_count)

time: 65.8 us -> 63.3 us (0.962)
  waiting for transfers between devices: 23.5 us -> 20.3 us
  local copies, waits for them, and re-layouts: 4.94 us -> 5.61 us
    all_to_all x1, waiting for transfers between devices: 18.4 us -> 12.9 us  [on_device(): lax.all_to_all(sent, 'chan', split_axis=0, concat_axis=0, tiled=True)]
    ppermute x1, waiting for transfers between devices: 0.01 us -> 1.42 us  [on_device(): other = lax.ppermute(own, 'pix', [(0, 1), (1, 0), (2, 3), (3, 2)])]
    ppermute x1, waiting for transfers between devices: 2.35 us -> 3.19 us  [on_device(): got = lax.ppermute(send, 'pix', [(0, 2), (2, 0), (1, 3), (3, 1)])]
    unnamed x16, local copies, waits for them, and re-layouts: 3.96 us -> 4.64 us
  transfers between devices with their start and end apart: 4 -> 4, of which waited for: 3 -> 4; matrix products, arithmetic and copies ran while one was open for 1% -> 1% of each run, Pallas kernels for 5% -> 5%
where the time goes in v2:
time: 63.3 us; the launch traced here: 62.9 us
  starting transfers between devices  27.4 us (43%)
  waiting for transfers between devices  20.3 us (32%)
  Pallas kernels  8.72 us (14%)
  local copies, waits for them, and re-layouts  5.61 us (9%)
  between operations  0.74 us (1%)
    all_to_all x1, starting transfers between devices, on_device(): lax.all_to_all(sent, 'chan', split_axis=0, concat_axis=0, tiled=True)  15.6 us
    all_to_all x1, waiting for transfers between devices, on_device(): lax.all_to_all(sent, 'chan', split_axis=0, concat_axis=0, tiled=True)  12.9 us
    ppermute x1, starting transfers between devices, on_device(): lax.ppermute(voltages[:, spec_dev - HALO:, :], 'pix', [(i, i + 1) for i i...  6.02 us
    unnamed x16, local copies, waits for them, and re-layouts  4.64 us
    ppermute x1, starting transfers between devices, on_device(): got = lax.ppermute(send, 'pix', [(0, 2), (2, 0), (1, 3), (3, 1)])  3.89 us
    pallas_call x1, Pallas kernels, steering(): pl.pallas_call(steering_kernel, out_shape=(out, out), in_specs=[SMEM] + [...  3.33 us
    ppermute x1, waiting for transfers between devices, on_device(): got = lax.ppermute(send, 'pix', [(0, 2), (2, 0), (1, 3), (3, 1)])  3.19 us
    ppermute x1, waiting for transfers between devices, on_device(): lax.ppermute(voltages[:, spec_dev - HALO:, :], 'pix', [(i, i + 1) for i i...  2.74 us
  transfers between devices with their start and end apart: 4, of which 4 were waited for; matrix products, arithmetic and copies ran while one was open for 1% of the time, Pallas kernels for 5%

profile of v2, /device:TPU:1, one launch (start us, length us, event | category | flops | bytes accessed | tf_op | source)
XLA Modules:
  0.0 62.9 jit_solution(2870710604019210993)
XLA Ops:
  0.6 0.0 copy-start.2
  0.6 0.7 %slice.3 = bf16[2,8,256]{2,1,0:T(8,128)(2,1)S(1)} slice(bf16[2,512,256]{2,1,0:T(8,128)(2,1)} %v_hbm.1), slice={[0:2], [504:512], [0:256]} | slice | bytes 16384 | tf_op jit(solution)/shard_map/slice | solution.py:243
  1.3 6.0 %collective-permute-start = (bf16[2,8,256]{2,1,0:T(8,128)(2,1)S(1)}, bf16[2,8,256]{2,1,0:T(8,128)(2,1)S(1)}, u32[]{:S(2)}, u32[]{:S(2)}) collective-permute-start(bf16[2,8,256]{2,1,0:T(8,128)(2,1)S(1)} %slice.3), channel_id=1, source_target_pairs={{0,1},{1,2},{2,3},{4,5},{5,6},{6,7},{8,9},{9,10},{10,11},{12,13},{... | collective-permute-start | bytes 24584 | tf_op jit(solution)/shard_map/ppermute | solution.py:242
  7.4 2.7 %collective-permute-done.hist_ref = bf16[2,8,256]{2,1,0:T(8,128)(2,1)S(1)} collective-permute-done((bf16[2,8,256]{2,1,0:T(8,128)(2,1)S(1)}, bf16[2,8,256]{2,1,0:T(8,128)(2,1)S(1)}, u32[]{:S(2)}, u32[]{:S(2)}) %collective-permute-start) | collective-permute-done | bytes 8224 | tf_op jit(solution)/shard_map/ppermute | solution.py:242
  10.1 0.0 copy-done.2
  10.1 0.0 copy-start
  10.1 1.0 %copy-done = bf16[2,512,256]{2,1,0:T(8,128)(2,1)S(1)} copy-done((bf16[2,512,256]{2,1,0:T(8,128)(2,1)S(1)}, bf16[2,512,256]{2,1,0:T(8,128)(2,1)}, u32[]{:S(2)}) %copy-start) | copy-done | bytes 524312
  11.2 0.0 copy-start.1
  11.2 0.9 %copy-done.1 = bf16[256,256]{1,0:T(8,128)(2,1)S(1)} copy-done((bf16[256,256]{1,0:T(8,128)(2,1)S(1)}, bf16[256,256]{1,0:T(8,128)(2,1)}, u32[]{:S(2)}) %copy-start.1) | copy-done | bytes 131096
  12.1 2.1 %filter_bank.1 = bf16[128,16,128]{2,1,0:T(8,128)(2,1)} custom-call(bf16[2,512,256]{2,1,0:T(8,128)(2,1)S(1)} %copy-done, bf16[2,8,256]{2,1,0:T(8,128)(2,1)S(1)} %collective-permute-done.hist_ref, f32[4,128]{1,0:T(4,128)S(1)} %copy-done.2, bf16[256,256]{1,0:T(8,128)(2,1)S(1)} %copy-done.1), custom_call_target="tpu_custom_call" | custom-call | flops 134217728 | bytes 1048576 | tf_op jit(solution)/shard_map/filter_bank/pallas_call | solution.py:73
  14.2 15.6 %all-to-all-start = ((bf16[128,16,128]{2,1,0:T(8,128)(2,1)}), bf16[128,16,128]{2,1,0:T(8,128)(2,1)S(1)}, u32[]{:S(2)}, u32[]{:S(2)}) async-start(bf16[128,16,128]{2,1,0:T(8,128)(2,1)} %filter_bank.1), calls=%async_computation | async-start | bytes 1048576 | tf_op jit(solution)/shard_map/all_to_all | solution.py:246
  29.8 0.0 copy-start.6
  29.8 0.7 %copy-done.6 = s32[256]{0:T(256)S(1)} copy-done((s32[256]{0:T(256)S(1)}, s32[256]{0:T(256)}, u32[]{:S(2)}) %copy-start.6) | copy-done | bytes 1048
  30.5 0.1 reshape.10
  30.7 0.0 copy-start.4
  30.7 0.1 copy.10
  30.7 0.7 %copy-done.5 = s32[64]{0:T(128)S(1)} copy-done((s32[64]{0:T(128)S(1)}, s32[64]{0:T(128)}, u32[]{:S(2)}) %copy-start.5) | copy-done | bytes 280
  31.4 0.1 fusion
  31.5 0.7 %copy-done.7 = s32[64]{0:T(128)S(1)} copy-done((s32[64]{0:T(128)S(1)}, s32[64]{0:T(128)}, u32[]{:S(2)}) %copy-start.7) | copy-done | bytes 280
  32.1 0.1 add_bitcast_fusion
  32.2 0.0 copy-done.4
  32.2 0.7 %copy-done.3 = s32[256]{0:T(256)S(1)} copy-done((s32[256]{0:T(256)S(1)}, s32[256]{0:T(256)}, u32[]{:S(2)}) %copy-start.3) | copy-done | bytes 1048
  32.9 3.3 %steering.1 = (bf16[256,2048]{1,0:T(8,128)(2,1)S(1)}, bf16[256,2048]{1,0:T(8,128)(2,1)S(1)}) custom-call(s32[1]{0:T(128)} %bitcast.4.chan_ref, s32[1,256]{1,0:T(1,128)S(1)} %bitcast.12, s32[1,256]{1,0:T(1,128)S(1)} %bitcast.13, s32[1,128]{1,0:T(1,128)S(1)} %get-tuple-element.14.l_ref, s32[1,128]{1,0:T(1,128)S(1)} %get-tuple-element.15.m_ref), custom_call_target="tpu_custom_call" | custom-call | flops 3145728 | bytes 2097152 | tf_op jit(solution)/shard_map/steering/pallas_call | solution.py:116
  36.2 12.9 %all-to-all-done.recv_ref = bf16[128,16,128]{2,1,0:T(8,128)(2,1)S(1)} async-done(((bf16[128,16,128]{2,1,0:T(8,128)(2,1)}), bf16[128,16,128]{2,1,0:T(8,128)(2,1)S(1)}, u32[]{:S(2)}, u32[]{:S(2)}) %all-to-all-start) | async-done | bytes 524320 | tf_op jit(solution)/shard_map/all_to_all | solution.py:246
  49.1 0.9 %gram.1.own_ref = bf16[2,256,256]{2,1,0:T(8,128)(2,1)S(1)} custom-call(bf16[128,16,128]{2,1,0:T(8,128)(2,1)S(1)} %all-to-all-done.recv_ref, s32[1,256]{1,0:T(1,128)S(1)} %bitcast.11, bf16[256,2048]{1,0:T(8,128)(2,1)S(1)} %get-tuple-element.7.after_ref.cos_ref), custom_call_target="tpu_custom_call" | custom-call | flops 402653184 | bytes 1048576 | tf_op jit(solution)/shard_map/gram/pallas_call | solution.py:145
  50.1 1.9 %collective-permute-start.1 = (bf16[2,256,256]{2,1,0:T(8,128)(2,1)S(1)}, bf16[2,256,256]{2,1,0:T(8,128)(2,1)S(1)}, u32[]{:S(2)}, u32[]{:S(2)}) collective-permute-start(bf16[2,256,256]{2,1,0:T(8,128)(2,1)S(1)} %gram.1.own_ref), channel_id=1, source_target_pairs={{0,1},{1,0},{2,3},{3,2},{4,5},{5,4},{6,7},{7,6},{8,9},{9,8},{10,11... | collective-permute-start | bytes 786440 | tf_op jit(solution)/shard_map/ppermute | solution.py:265
  52.0 0.1 pad_add_fusion.place_ref
  52.1 1.4 %collective-permute-done.1.other_ref = bf16[2,256,256]{2,1,0:T(8,128)(2,1)S(1)} collective-permute-done((bf16[2,256,256]{2,1,0:T(8,128)(2,1)S(1)}, bf16[2,256,256]{2,1,0:T(8,128)(2,1)S(1)}, u32[]{:S(2)}, u32[]{:S(2)}) %collective-permute-start.1) | collective-permute-done | bytes 262176 | tf_op jit(solution)/shard_map/ppermute | solution.py:265
  53.5 1.6 %image_rows.1 = (f32[2,64,256]{2,1,0:T(8,128)S(1)}, f32[4,256]{1,0:T(4,128)S(1)}, bf16[144,256]{1,0:T(8,128)(2,1)S(1)}) custom-call(s32[2]{0:T(128)S(1)} %pad_add_fusion.place_ref, bf16[2,256,256]{2,1,0:T(8,128)(2,1)S(1)} %gram.1.own_ref, bf16[2,256,256]{2,1,0:T(8,128)(2,1)S(1)} %collective-permute-done.1.other_ref, ...), custom_call_target="tpu_custom_call" | custom-call | flops 805306368 | bytes 2097152 | tf_op jit(solution)/shard_map/image_rows/pallas_call | solution.py:193
  55.2 3.9 %collective-permute-start.2 = (bf16[144,256]{1,0:T(8,128)(2,1)S(1)}, bf16[144,256]{1,0:T(8,128)(2,1)S(1)}, u32[]{:S(2)}, u32[]{:S(2)}) collective-permute-start(bf16[144,256]{1,0:T(8,128)(2,1)S(1)} %get-tuple-element.11), channel_id=1, source_target_pairs={{0,2},{2,0},{1,3},{3,1},{4,6},{6,4},{5,7},{7,5},{8,10},{10,8},{9,1... | collective-permute-start | bytes 221192 | tf_op jit(solution)/shard_map/ppermute | solution.py:268
  59.0 3.2 %collective-permute-done.2.refs_2_ = bf16[144,256]{1,0:T(8,128)(2,1)S(1)} collective-permute-done((bf16[144,256]{1,0:T(8,128)(2,1)S(1)}, bf16[144,256]{1,0:T(8,128)(2,1)S(1)}, u32[]{:S(2)}, u32[]{:S(2)}) %collective-permute-start.2) | collective-permute-done | bytes 73760 | tf_op jit(solution)/shard_map/ppermute | solution.py:268
  62.2 0.7 %finish.1 = (f32[1,2,64,256]{3,2,1,0:T(8,128)}, f32[1,1024]{1,0:T(1,128)}) custom-call(f32[2,64,256]{2,1,0:T(8,128)S(1)} %get-tuple-element.9.refs_0_, f32[4,256]{1,0:T(4,128)S(1)} %get-tuple-element.10.refs_1_, bf16[144,256]{1,0:T(8,128)(2,1)S(1)} %collective-permute-done.2.refs_2_), custom_call_target="tpu_custom_call" | custom-call | flops 65536 | bytes 262144 | tf_op jit(solution)/shard_map/finish/pallas_call | solution.py:222
  (4 shorter events, 0.0 us)
Async XLA Ops:
  0.6 9.5 %copy-start.2 = (f32[4,128]{1,0:T(4,128)S(1)}, f32[4,128]{1,0:T(4,128)}, u32[]{:S(2)}) copy-start(f32[4,128]{1,0:T(4,128)} %taps_ref.1) | copy-start | bytes 6148
  1.3 8.8 %collective-permute-start = (bf16[2,8,256]{2,1,0:T(8,128)(2,1)S(1)}, bf16[2,8,256]{2,1,0:T(8,128)(2,1)S(1)}, u32[]{:S(2)}, u32[]{:S(2)}) collective-permute-start(bf16[2,8,256]{2,1,0:T(8,128)(2,1)S(1)} %slice.3), channel_id=1, source_target_pairs={{0,1},{1,2},{2,3},{4,5},{5,6},{6,7},{8,9},{9,10},{10,11},{12,13},{... | collective-permute-start | bytes 24584 | tf_op jit(solution)/shard_map/ppermute | solution.py:242
  10.1 1.0 %copy-start = (bf16[2,512,256]{2,1,0:T(8,128)(2,1)S(1)}, bf16[2,512,256]{2,1,0:T(8,128)(2,1)}, u32[]{:S(2)}) copy-start(bf16[2,512,256]{2,1,0:T(8,128)(2,1)} %v_hbm.1) | copy-start | bytes 1572868
  11.2 0.9 %copy-start.1 = (bf16[256,256]{1,0:T(8,128)(2,1)S(1)}, bf16[256,256]{1,0:T(8,128)(2,1)}, u32[]{:S(2)}) copy-start(bf16[256,256]{1,0:T(8,128)(2,1)} %constant.24.dft_hbm) | copy-start | bytes 393220
  14.2 34.9 %all-to-all-start = ((bf16[128,16,128]{2,1,0:T(8,128)(2,1)}), bf16[128,16,128]{2,1,0:T(8,128)(2,1)S(1)}, u32[]{:S(2)}, u32[]{:S(2)}) async-start(bf16[128,16,128]{2,1,0:T(8,128)(2,1)} %filter_bank.1), calls=%async_computation | async-start | bytes 1048576 | tf_op jit(solution)/shard_map/all_to_all | solution.py:246
  29.8 0.7 %copy-start.6 = (s32[256]{0:T(256)S(1)}, s32[256]{0:T(256)}, u32[]{:S(2)}) copy-start(s32[256]{0:T(256)} %param.10) | copy-start | bytes 3076
  30.7 1.6 %copy-start.4 = (s32[256]{0:T(256)S(1)}, s32[256]{0:T(256)}, u32[]{:S(2)}) copy-start(s32[256]{0:T(256)} %param.12) | copy-start | bytes 3076
  30.7 0.7 %copy-start.5 = (s32[64]{0:T(128)S(1)}, s32[64]{0:T(128)}, u32[]{:S(2)}) copy-start(s32[64]{0:T(128)} %param.13) | copy-start | bytes 772
  31.5 0.7 %copy-start.7 = (s32[64]{0:T(128)S(1)}, s32[64]{0:T(128)}, u32[]{:S(2)}) copy-start(s32[64]{0:T(128)} %param.14) | copy-start | bytes 772
  32.2 0.7 %copy-start.3 = (s32[256]{0:T(256)S(1)}, s32[256]{0:T(256)}, u32[]{:S(2)}) copy-start(s32[256]{0:T(256)} %param.11) | copy-start | bytes 3076
  50.1 3.4 %collective-permute-start.1 = (bf16[2,256,256]{2,1,0:T(8,128)(2,1)S(1)}, bf16[2,256,256]{2,1,0:T(8,128)(2,1)S(1)}, u32[]{:S(2)}, u32[]{:S(2)}) collective-permute-start(bf16[2,256,256]{2,1,0:T(8,128)(2,1)S(1)} %gram.1.own_ref), channel_id=1, source_target_pairs={{0,1},{1,0},{2,3},{3,2},{4,5},{5,4},{6,7},{7,6},{8,9},{9,8},{10,11... | collective-permute-start | bytes 786440 | tf_op jit(solution)/shard_map/ppermute | solution.py:265
  55.2 7.1 %collective-permute-start.2 = (bf16[144,256]{1,0:T(8,128)(2,1)S(1)}, bf16[144,256]{1,0:T(8,128)(2,1)S(1)}, u32[]{:S(2)}, u32[]{:S(2)}) collective-permute-start(bf16[144,256]{1,0:T(8,128)(2,1)S(1)} %get-tuple-element.11), channel_id=1, source_target_pairs={{0,2},{2,0},{1,3},{3,1},{4,6},{6,4},{5,7},{7,5},{8,10},{10,8},{9,1... | collective-permute-start | bytes 221192 | tf_op jit(solution)/shard_map/ppermute | solution.py:268

commit v3 on v2

v3 whole, which is shorter than its diff:
```python
import math

import jax
import jax.numpy as jnp
import numpy as np
from jax import lax
from jax.experimental import pallas as pl
from jax.experimental.pallas import tpu as pltpu
from jax.sharding import PartitionSpec as P

POINTS = 128
TAPS = 4
GRID = 1024
LANES = 128
STATIONS = 256
EDGE = 8
ROWS = 18

VMEM = pl.BlockSpec(memory_space=pltpu.VMEM)
HBM = pl.BlockSpec(memory_space=pltpu.HBM)
ANY = pl.BlockSpec(memory_space=pl.ANY)
SMEM = pl.BlockSpec(memory_space=pltpu.SMEM)
F32 = jnp.float32
BF16 = jnp.bfloat16


def dft_matrix(points):
    counter = np.arange(points)
    angle = np.mod(counter[:, None] * counter[None, :], points) * (2.0 * math.pi / points)
    cosine, sine = np.cos(angle), np.sin(angle)
    table = np.block([[cosine, sine], [-sine, cosine]]) * points ** (-0.5)
    return jnp.asarray(table, dtype=F32).astype(BF16)


def params(flops, moved, limit=40 * 1024 * 1024):
    return dict(
        compiler_params=pltpu.CompilerParams(vmem_limit_bytes=limit),
        cost_estimate=pl.CostEstimate(flops=flops, bytes_accessed=moved, transcendentals=0),
    )


def filter_kernel(v_hbm, taps_ref, dft_hbm, out_hbm, v_ref, dft_ref, ext, tail, wide, packed, sems):
    spec_dev = v_hbm.shape[1]
    copies = [pltpu.make_async_copy(v_hbm.at[s], v_ref.at[s], sems.at[s]) for s in range(2)]
    copies.append(pltpu.make_async_copy(dft_hbm, dft_ref, sems.at[2]))
    for copy in copies:
        copy.start()
    taps = jnp.concatenate([taps_ref[...], taps_ref[...]], axis=1)
    step = 256
    contract = (((1,), (1,)), ((), ()))
    for s in range(2):
        ext[s, 0:EDGE, :] = jnp.zeros((EDGE, 2 * POINTS), F32)
        ext[s, EDGE + spec_dev :, :] = jnp.zeros((EDGE, 2 * POINTS), F32)
    tail[2 * EDGE :, :] = jnp.zeros((LANES - 2 * EDGE, 2 * POINTS), BF16)

    def filtered(s, start, count):
        total = taps[0:1] * ext[s, EDGE + start : EDGE + start + count, :]
        for k in range(1, TAPS):
            total = total + taps[k : k + 1] * ext[s, EDGE - k + start : EDGE - k + start + count, :]
        return total

    for s in range(2):
        copies[s].wait()
        ext[s, EDGE : EDGE + spec_dev, :] = v_ref[s].astype(F32)
        if s == 0:
            copies[2].wait()
        for t in range(0, spec_dev, step):
            spectra = lax.dot_general(
                dft_ref[...], filtered(s, t, step).astype(BF16), contract, preferred_element_type=F32
            )
            for r in range(2):
                for part in range(step // LANES):
                    row = s * 8 + r * 4 + t // LANES + part
                    wide[pl.ds(row, POINTS, stride=ROWS), :] = spectra[
                        r * POINTS : (r + 1) * POINTS, part * LANES : (part + 1) * LANES
                    ]
    edges = jnp.concatenate([filtered(s, spec_dev, EDGE) for s in range(2)], axis=0)
    tail[0 : 2 * EDGE, :] = edges.astype(BF16)
    spectra = lax.dot_general(dft_ref[...], tail[...], contract, preferred_element_type=F32)
    for r in range(2):
        wide[pl.ds(16 + r, POINTS, stride=ROWS), :] = spectra[r * POINTS : (r + 1) * POINTS]
    chunk = POINTS * ROWS // 8
    writes = []
    for c in range(8):
        here = pl.ds(c * chunk // 2, chunk // 2)
        packed[here] = wide[c * chunk : (c + 1) * chunk, :].astype(BF16).reshape(chunk // 2, 2, LANES)
        writes.append(pltpu.make_async_copy(packed.at[here], out_hbm.at[here], sems.at[3 + c]))
        writes[-1].start()
    for write in writes:
        write.wait()


def filter_bank(voltages, fir_taps):
    pairs = POINTS * ROWS // 2
    return pl.pallas_call(
        filter_kernel,
        out_shape=jax.ShapeDtypeStruct((pairs, 2, LANES), BF16),
        in_specs=[HBM, VMEM, HBM],
        out_specs=HBM,
        scratch_shapes=[
            pltpu.VMEM(voltages.shape, BF16),
            pltpu.VMEM((2 * POINTS, 2 * POINTS), BF16),
            pltpu.VMEM((2, 2 * EDGE + voltages.shape[1], 2 * POINTS), F32),
            pltpu.VMEM((LANES, 2 * POINTS), BF16),
            pltpu.VMEM((2 * pairs, LANES), F32),
            pltpu.VMEM((pairs, 2, LANES), BF16),
            pltpu.SemaphoreType.DMA((11,)),
        ],
        name="filter_bank",
        **params(2 * 256 * 256 * 1024, 1 << 20, 66_000_000),
    )(voltages, fir_taps, dft_matrix(POINTS))


def steering_kernel(chan_ref, u_ref, v_ref, l_ref, m_ref, cos_ref, sin_ref):
    freq = POINTS + chan_ref[0]
    rows = lax.broadcasted_iota(jnp.int32, (STATIONS, STATIONS), 0)
    cols = lax.broadcasted_iota(jnp.int32, (STATIONS, STATIONS), 1)
    eye = rows == cols

    def column(ref):
        return jnp.sum(jnp.where(eye, ref[...], 0), axis=1, keepdims=True)

    def phases(station, pixel):
        index = (freq * ((station * pixel) & (GRID - 1))) & (GRID - 1)
        angle = index.astype(F32) * (2.0 * math.pi / GRID)
        return jnp.cos(angle), jnp.sin(angle)

    l_cos, l_sin = phases(column(u_ref), l_ref[...])
    m_cos, m_sin = phases(column(v_ref), m_ref[...])
    first = lax.broadcasted_iota(jnp.int32, (STATIONS, LANES), 1) < 64
    for q in range(cos_ref.shape[1] // LANES):
        a_cos = jnp.where(first, l_cos[:, 2 * q : 2 * q + 1], l_cos[:, 2 * q + 1 : 2 * q + 2])
        a_sin = jnp.where(first, l_sin[:, 2 * q : 2 * q + 1], l_sin[:, 2 * q + 1 : 2 * q + 2])
        cos_ref[:, q * LANES : (q + 1) * LANES] = (a_cos * m_cos - a_sin * m_sin).astype(BF16)
        sin_ref[:, q * LANES : (q + 1) * LANES] = (a_sin * m_cos + a_cos * m_sin).astype(BF16)


def steering(channel, station_u, station_v, rows_l, pixel_m, pixels):
    out = jax.ShapeDtypeStruct((STATIONS, pixels), BF16)
    return pl.pallas_call(
        steering_kernel,
        out_shape=(out, out),
        in_specs=[SMEM] + [VMEM] * 4,
        out_specs=(VMEM, VMEM),
        name="steering",
        **params(6 * STATIONS * pixels, 4 * STATIONS * pixels),
    )(channel, station_u, station_v, rows_l, pixel_m)


def gram_kernel(place_ref, recv_ref, station_ref, after_ref, out_ref, wide, slots):
    chunk = 256
    for c in range(0, POINTS * ROWS, chunk):
        wide[c : c + chunk, :] = recv_ref[c // 2 : (c + chunk) // 2].reshape(chunk, LANES).astype(F32)
    lane = lax.broadcasted_iota(jnp.int32, (POINTS, LANES), 1)
    head = lane < TAPS - 1
    edge = lane < EDGE
    left_out = jnp.logical_and(head, place_ref[0] > 0)

    def column(row):
        return wide[pl.ds(row, POINTS, stride=ROWS), :]

    for s in range(2):
        rows = slice(s * POINTS, (s + 1) * POINTS)
        for q in range(8):
            values = column(s * 8 + q)
            if q % 4 == 0:
                values = jnp.where(left_out, 0.0, values)
            slots[rows, q * LANES : (q + 1) * LANES] = values.astype(BF16)
        pieces = [
            pltpu.roll(column(16 + r), LANES - EDGE, 1) if s else column(16 + r) for r in range(2)
        ]
        pieces = [jnp.where(edge, piece, 0.0) for piece in pieces]
        pieces += [jnp.where(head, column(s * 8 + r * 4), 0.0) for r in range(2)]
        total = pieces[0]
        for i in range(1, 4):
            total = total + pltpu.roll(pieces[i], i * EDGE, 1)
        slots[rows, 8 * LANES :] = total.astype(BF16)
    rows = lax.broadcasted_iota(jnp.int32, (STATIONS, STATIONS), 0)
    select = jnp.where(rows == station_ref[...], 1.0, 0.0).astype(BF16)
    ordered = jnp.dot(select, slots[...], preferred_element_type=F32).astype(BF16)
    half = 4 * LANES
    spectra = ordered[:, : 2 * half]
    turned = jnp.concatenate([ordered[:, half : 2 * half], -ordered[:, :half]], axis=1)
    contract = (((1,), (1,)), ((), ()))
    real = lax.dot_general(spectra, spectra, contract, preferred_element_type=F32)
    imag = lax.dot_general(turned, spectra, contract, preferred_element_type=F32)
    out_ref[:, 0:STATIONS] = real.astype(BF16)
    out_ref[:, STATIONS : 2 * STATIONS] = imag.astype(BF16)
    out_ref[:, 2 * STATIONS :] = ordered[:, 2 * half :]


def gram(place, received, station_row, after):
    return pl.pallas_call(
        gram_kernel,
        out_shape=jax.ShapeDtypeStruct((STATIONS, 2 * STATIONS + LANES), BF16),
        in_specs=[SMEM, VMEM, VMEM, ANY],
        out_specs=VMEM,
        scratch_shapes=[
            pltpu.VMEM((POINTS * ROWS, LANES), F32),
            pltpu.VMEM((STATIONS, 9 * LANES), BF16),
        ],
        name="gram",
        **params(6 * 256 * 256 * 1024, 1 << 20),
    )(place, received, station_row, after)


def image_kernel(place_ref, own_ref, other_ref, cos_ref, sin_ref, rows_ref, extra_ref, send_ref, real, imag):
    count = rows_ref.shape[1]
    lane = lax.broadcasted_iota(jnp.int32, (STATIONS, LANES), 1)
    contract = (((1,), (1,)), ((), ()))
    upper_core = (place_ref[0] & 1) == 1
    second_chip = place_ref[0] >= 2
    own_edge = own_ref[:, 2 * STATIONS :].astype(F32)
    other_edge = other_ref[:, 2 * STATIONS :].astype(F32)
    low = jnp.where(upper_core, other_edge, own_edge)
    high = jnp.where(upper_core, own_edge, other_edge)
    inner = jnp.where(lane < 16, low + pltpu.roll(high, LANES - 16, 1), 0.0)
    turned = jnp.where(lane < 8, pltpu.roll(inner, LANES - 8, 1), -pltpu.roll(inner, 8, 1))
    turned = jnp.where(lane < 16, turned, 0.0).astype(BF16)
    inner = inner.astype(BF16)
    real[...] = (
        own_ref[:, 0:STATIONS].astype(F32)
        + other_ref[:, 0:STATIONS].astype(F32)
        + lax.dot_general(inner, inner, contract, preferred_element_type=F32)
    )
    imag[...] = (
        own_ref[:, STATIONS : 2 * STATIONS].astype(F32)
        + other_ref[:, STATIONS : 2 * STATIONS].astype(F32)
        + lax.dot_general(turned, inner, contract, preferred_element_type=F32)
    )
    here = pl.ds(pl.multiple_of(place_ref[0] * count, count), count)
    across = pl.ds(pl.multiple_of(place_ref[1] * count, count), count)
    rows_ref[0] = real[here, :]
    rows_ref[1] = imag[here, :]
    send_ref[0:count, :] = real[across, :].astype(BF16)
    send_ref[count : 2 * count, :] = imag[across, :].astype(BF16)

    outer = jnp.where(second_chip, pltpu.roll(low, LANES - 16, 1), high)
    outer = jnp.where(lane < 16, outer, 0.0).T[0:16]
    edge_rows = outer[0:8] + pltpu.roll(outer[8:16], 4, 0)

    rows = lax.broadcasted_iota(jnp.int32, (STATIONS, STATIONS), 0)
    cols = lax.broadcasted_iota(jnp.int32, (STATIONS, STATIONS), 1)
    flag_real = jnp.where(rows == cols, 0.0, real[...]).astype(BF16)
    flag_real = jnp.concatenate([flag_real, outer.astype(BF16)], axis=0)
    flag_imag = jnp.where(rows == cols, 0.0, imag[...]).astype(BF16)
    width = STATIONS
    groups = cos_ref.shape[1] // width // 2
    for q in range(2 * groups):
        cosine = cos_ref[:, q * width : (q + 1) * width]
        sine = sin_ref[:, q * width : (q + 1) * width]
        by_cos = jnp.dot(flag_real, cosine, preferred_element_type=F32)
        by_sin = jnp.dot(flag_real, sine, preferred_element_type=F32)
        cross = jnp.dot(flag_imag, sine, preferred_element_type=F32)
        upper = by_cos[:STATIONS] + 2.0 * cross
        pixel = jnp.sum(
            cosine.astype(F32) * upper + sine.astype(F32) * by_sin[:STATIONS], axis=0, keepdims=True
        )
        first = by_cos[STATIONS : STATIONS + 8] - by_sin[STATIONS + 8 :]
        second = by_cos[STATIONS + 8 :] + by_sin[STATIONS : STATIONS + 8]
        beams = first + pltpu.roll(second, 4, 0)
        if q < groups:
            extra_ref[8 * q : 8 * q + 8, :] = beams
            extra_ref[8 * groups + 8 + q : 8 * groups + 9 + q, :] = pixel
        else:
            at = 2 * count + 8 * (q - groups)
            send_ref[at : at + 8, :] = beams.astype(BF16)
            at = 2 * count + 8 * groups + 8 + q - groups
            send_ref[at : at + 1, :] = pixel.astype(BF16)
    extra_ref[8 * groups : 8 * groups + 8, :] = edge_rows
    at = 2 * count + 8 * groups
    send_ref[at : at + 8, :] = edge_rows.astype(BF16)
    end = at + 8 + groups
    send_ref[end:, :] = jnp.zeros((send_ref.shape[0] - end, width), BF16)


def image_rows(place, own, other, cosine, sine, count):
    groups = cosine.shape[1] // 512
    return pl.pallas_call(
        image_kernel,
        out_shape=(
            jax.ShapeDtypeStruct((2, count, STATIONS), F32),
            jax.ShapeDtypeStruct((9 * groups + 8, STATIONS), F32),
            jax.ShapeDtypeStruct((2 * count + 8 * groups + 16, STATIONS), BF16),
        ),
        in_specs=[SMEM] + [VMEM] * 4,
        out_specs=(VMEM, VMEM, VMEM),
        scratch_shapes=[pltpu.VMEM((STATIONS, STATIONS), F32)] * 2,
        name="image_rows",
        **params(6 * 256 * 256 * 2048, 1 << 21),
    )(place, own, other, cosine, sine)


def finish_kernel(inv_total, image_scale, place_ref, rows_ref, extra_ref, got_ref, vis_ref, image_ref, turn):
    count = rows_ref.shape[1]
    groups = image_ref.shape[1] // STATIONS
    at = 8 * groups
    edge = extra_ref[at : at + 8, :] + got_ref[2 * count + at : 2 * count + at + 8, :].astype(F32)
    swapped = pltpu.roll(edge, 4, 0)
    low = lax.broadcasted_iota(jnp.int32, (8, STATIONS), 0) < 4
    swapped = jnp.where(low, swapped, -swapped)
    blank = jnp.zeros((LANES - 16, STATIONS), F32)
    turn[...] = jnp.concatenate([edge, swapped, blank], axis=0).T
    left = turn[pl.ds(pl.multiple_of(place_ref[0] * count, count), count), :]
    right = jnp.concatenate([edge, edge, blank], axis=0).astype(BF16)
    lane = lax.broadcasted_iota(jnp.int32, (count, LANES), 1)
    for part in range(2):
        got = got_ref[part * count : (part + 1) * count, :].astype(F32)
        chosen = jnp.where((lane < 8) if part == 0 else (lane >= 8), left, 0.0).astype(BF16)
        update = jnp.dot(chosen, right, preferred_element_type=F32)
        vis_ref[0, part] = (rows_ref[part] + got + update) * inv_total
    own_power = jnp.sum(jnp.sum(edge * edge, axis=1, keepdims=True), axis=0, keepdims=True)
    for q in range(groups):
        got = got_ref[2 * count + at + 8 + q : 2 * count + at + 9 + q, :].astype(F32)
        beams = extra_ref[8 * q : 8 * q + 8, :] + got_ref[
            2 * count + 8 * q : 2 * count + 8 * q + 8, :
        ].astype(F32)
        power = jnp.sum(beams * beams, axis=0, keepdims=True) - own_power
        image_ref[:, q * STATIONS : (q + 1) * STATIONS] = (
            extra_ref[at + 8 + q : at + 9 + q, :] + got + power
        ) * (inv_total * image_scale)


def finish(place, rows, extra, got, pixels, inv_total, image_scale):
    count = rows.shape[1]
    return pl.pallas_call(
        lambda *refs: finish_kernel(inv_total, image_scale, *refs),
        out_shape=(
            jax.ShapeDtypeStruct((1, 2, count, STATIONS), F32),
            jax.ShapeDtypeStruct((1, pixels), F32),
        ),
        in_specs=[SMEM] + [VMEM] * 3,
        out_specs=(VMEM, VMEM),
        scratch_shapes=[pltpu.VMEM((STATIONS, LANES), F32)],
        name="finish",
        **params(1 << 20, 1 << 18),
    )(place, rows, extra, got)


def on_device(voltages, fir_taps, station_of_slot, station_u, station_v, pixel_l, pixel_m):
    spec_dev = voltages.shape[1]
    pix_count = lax.axis_size("pix")
    spectra_total = spec_dev * pix_count
    pix = lax.axis_index("pix")
    across = jnp.where(pix < 2, pix + 2, pix - 2)
    place = jnp.stack([pix, across]).astype(jnp.int32)
    rows_l = pixel_l.shape[0] // pix_count
    sent = filter_bank(voltages, fir_taps).reshape(POINTS, ROWS // 2, 2, LANES)
    received = lax.all_to_all(sent, "chan", split_axis=0, concat_axis=0, tiled=True)

    block_l = jnp.concatenate(
        [
            lax.dynamic_slice_in_dim(pixel_l, pix * rows_l, rows_l, 0),
            lax.dynamic_slice_in_dim(pixel_l, across * rows_l, rows_l, 0),
            jnp.zeros((LANES - 2 * rows_l,), jnp.int32),
        ]
    )[None]
    pixels = rows_l * pixel_m.shape[0]
    cosine, sine = steering(
        lax.axis_index("chan")[None].astype(jnp.int32),
        station_u[None],
        station_v[None],
        block_l,
        jnp.concatenate([pixel_m, pixel_m])[None],
        2 * pixels,
    )
    station_row = station_of_slot.reshape(POINTS, 2).T.reshape(1, STATIONS)
    own = gram(place, received.reshape(-1, 2, LANES), station_row, cosine)
    other = lax.ppermute(own, "pix", [(0, 1), (1, 0), (2, 3), (3, 2)])
    rows, extra, send = image_rows(place, own, other, cosine, sine, STATIONS // pix_count)
    got = lax.ppermute(send, "pix", [(0, 2), (2, 0), (1, 3), (3, 1)])
    return finish(
        place, rows, extra, got, pixels, 1.0 / spectra_total, math.sqrt(spectra_total) / STATIONS
    )


def solution(mesh):
    in_specs = (P("chan", "pix", None), P(), P(), P(), P(), P(), P())
    out_specs = (P("chan", None, "pix", None), P("chan", "pix"))
    return jax.shard_map(
        on_device, mesh=mesh, in_specs=in_specs, out_specs=out_specs, check_vma=False
    )
```

time: 63.3 us -> 61.7 us (0.975)
  waiting for transfers between devices: 20.3 us -> 16.3 us
  Pallas kernels: 8.72 us -> 12.2 us
  local copies, waits for them, and re-layouts: 5.61 us -> 2.96 us
  starting transfers between devices: 27.4 us -> 29 us
    ppermute x1 -> x0, starting transfers between devices: 6.02 us -> none  [on_device(): lax.ppermute(voltages[:, spec_dev - HALO:, :], 'pix', [(i, i + 1) for i i...]
    all_to_all x1, starting transfers between devices: 15.6 us -> 19.3 us  [on_device(): lax.all_to_all(sent, 'chan', split_axis=0, concat_axis=0, tiled=True)]
    ppermute x1, starting transfers between devices: 1.92 us -> 5.39 us  [on_device(): other = lax.ppermute(own, 'pix', [(0, 1), (1, 0), (2, 3), (3, 2)])]
    ppermute x1 -> x0, waiting for transfers between devices: 2.74 us -> none  [on_device(): lax.ppermute(voltages[:, spec_dev - HALO:, :], 'pix', [(i, i + 1) for i i...]
    pallas_call x2, Pallas kernels: 3.07 us -> 5.48 us  [the longest x1 3.78 us: filter_bank(): pl.pallas_call(filter_kernel, out_shape=jax.ShapeDtypeStruct((pairs, 2, L...]
    unnamed x16 -> x10, local copies, waits for them, and re-layouts: 4.64 us -> 2.69 us
    pallas_call x1, Pallas kernels: 0.68 us -> 1.44 us  [finish(): pl.pallas_call(lambda *refs: finish_kernel(inv_total, image_scale, *refs)...]
    slice x1 -> x0, local copies, waits for them, and re-layouts: 0.7 us -> none  [on_device(): voltages[:, spec_dev - HALO:, :]]
  transfers between devices with their start and end apart: 4 -> 3, of which waited for: 4 -> 3; matrix products, arithmetic and copies ran while one was open for 1% -> 1% of each run, Pallas kernels for 5% -> 5%
where the time goes in v3:
time: 61.7 us; the launch traced here: 61.4 us
  starting transfers between devices  29 us (47%)
  waiting for transfers between devices  16.3 us (26%)
  Pallas kernels  12.2 us (20%)
  local copies, waits for them, and re-layouts  2.96 us (5%)
  between operations  0.73 us (1%)
    all_to_all x1, starting transfers between devices, on_device(): lax.all_to_all(sent, 'chan', split_axis=0, concat_axis=0, tiled=True)  19.3 us
    all_to_all x1, waiting for transfers between devices, on_device(): lax.all_to_all(sent, 'chan', split_axis=0, concat_axis=0, tiled=True)  12.3 us
    ppermute x1, starting transfers between devices, on_device(): other = lax.ppermute(own, 'pix', [(0, 1), (1, 0), (2, 3), (3, 2)])  5.39 us
    ppermute x1, starting transfers between devices, on_device(): got = lax.ppermute(send, 'pix', [(0, 2), (2, 0), (1, 3), (3, 1)])  4.36 us
    pallas_call x1, Pallas kernels, filter_bank(): pl.pallas_call(filter_kernel, out_shape=jax.ShapeDtypeStruct((pairs, 2, L...  3.78 us
    pallas_call x1, Pallas kernels, steering(): pl.pallas_call(steering_kernel, out_shape=(out, out), in_specs=[SMEM] + [...  3.35 us
    ppermute x1, waiting for transfers between devices, on_device(): got = lax.ppermute(send, 'pix', [(0, 2), (2, 0), (1, 3), (3, 1)])  2.84 us
    unnamed x10, local copies, waits for them, and re-layouts  2.69 us
  transfers between devices with their start and end apart: 3, of which 3 were waited for; matrix products, arithmetic and copies ran while one was open for 1% of the time, Pallas kernels for 5%

profile of v3, /device:TPU:1, one launch (start us, length us, event | category | flops | bytes accessed | tf_op | source)
XLA Modules:
  0.0 61.4 jit_solution(14259811009471941548)
XLA Ops:
  0.6 3.8 %filter_bank.1 = bf16[1152,2,128]{2,1,0:T(2,128)(2,1)} custom-call(bf16[2,512,256]{2,1,0:T(8,128)(2,1)} %v_hbm.1, f32[4,128]{1,0:T(4,128)} %taps_ref.1, bf16[256,256]{1,0:T(8,128)(2,1)} %constant.24.dft_hbm), custom_call_target="tpu_custom_call" | custom-call | flops 134217728 | bytes 1048576 | tf_op jit(solution)/shard_map/filter_bank/pallas_call | solution.py:95
  4.4 19.3 %all-to-all-start = ((bf16[128,9,2,128]{3,2,1,0:T(2,128)(2,1)}), bf16[128,9,2,128]{3,2,1,0:T(2,128)(2,1)S(1)}, u32[]{:S(2)}, u32[]{:S(2)}) async-start(bf16[128,9,2,128]{3,2,1,0:T(2,128)(2,1)} %bitcast.17), calls=%async_computation | async-start | bytes 1179648 | tf_op jit(solution)/shard_map/all_to_all | solution.py:349
  23.7 0.0 copy-start.3
  23.7 0.7 %copy-done.3 = s32[256]{0:T(256)S(1)} copy-done((s32[256]{0:T(256)S(1)}, s32[256]{0:T(256)}, u32[]{:S(2)}) %copy-start.3) | copy-done | bytes 1048
  24.4 0.1 reshape.18
  24.5 0.0 copy-start.1
  24.6 0.1 copy.10
  24.6 0.0 copy-start.2
  24.6 0.7 %copy-done.2 = s32[64]{0:T(128)S(1)} copy-done((s32[64]{0:T(128)S(1)}, s32[64]{0:T(128)}, u32[]{:S(2)}) %copy-start.2) | copy-done | bytes 280
  25.3 0.1 fusion
  25.4 0.0 copy-start.4
  25.4 0.7 %copy-done.4 = s32[64]{0:T(128)S(1)} copy-done((s32[64]{0:T(128)S(1)}, s32[64]{0:T(128)}, u32[]{:S(2)}) %copy-start.4) | copy-done | bytes 280
  26.0 0.1 add_bitcast_fusion
  26.1 0.0 copy-start
  26.1 0.0 copy-done.1
  26.1 0.7 %copy-done = s32[256]{0:T(256)S(1)} copy-done((s32[256]{0:T(256)S(1)}, s32[256]{0:T(256)}, u32[]{:S(2)}) %copy-start) | copy-done | bytes 1048
  26.8 3.3 %steering.1 = (bf16[256,2048]{1,0:T(8,128)(2,1)S(1)}, bf16[256,2048]{1,0:T(8,128)(2,1)S(1)}) custom-call(s32[1]{0:T(128)} %bitcast.6.chan_ref, s32[1,256]{1,0:T(1,128)S(1)} %bitcast.15, s32[1,256]{1,0:T(1,128)S(1)} %bitcast.16, s32[1,128]{1,0:T(1,128)S(1)} %get-tuple-element.14.l_ref, s32[1,128]{1,0:T(1,128)S(1)} %get-tuple-element.15.m_ref), custom_call_target="tpu_custom_call" | custom-call | flops 3145728 | bytes 2097152 | tf_op jit(solution)/shard_map/steering/pallas_call | solution.py:140
  30.1 0.1 pad_add_fusion.place_ref.refs_0_
  30.2 12.3 %all-to-all-done = bf16[128,9,2,128]{3,2,1,0:T(2,128)(2,1)S(1)} async-done(((bf16[128,9,2,128]{3,2,1,0:T(2,128)(2,1)}), bf16[128,9,2,128]{3,2,1,0:T(2,128)(2,1)S(1)}, u32[]{:S(2)}, u32[]{:S(2)}) %all-to-all-start) | async-done | bytes 589856 | tf_op jit(solution)/shard_map/all_to_all | solution.py:349
  42.5 1.7 %gram.1.own_ref = bf16[256,640]{1,0:T(8,128)(2,1)S(1)} custom-call(s32[2]{0:T(128)S(1)} %pad_add_fusion.place_ref.refs_0_, bf16[1152,2,128]{2,1,0:T(2,128)(2,1)S(1)} %bitcast.13, s32[1,256]{1,0:T(1,128)S(1)} %bitcast.14, bf16[256,2048]{1,0:T(8,128)(2,1)S(1)} %get-tuple-element.7.after_ref.cos_ref), custom_call_target="tpu_custom_call" | custom-call | flops 402653184 | bytes 1048576 | tf_op jit(solution)/shard_map/gram/pallas_call | solution.py:193
  44.2 5.4 %collective-permute-start = (bf16[256,640]{1,0:T(8,128)(2,1)S(1)}, bf16[256,640]{1,0:T(8,128)(2,1)S(1)}, u32[]{:S(2)}, u32[]{:S(2)}) collective-permute-start(bf16[256,640]{1,0:T(8,128)(2,1)S(1)} %gram.1.own_ref), channel_id=1, source_target_pairs={{0,1},{1,0},{2,3},{3,2},{4,5},{5,4},{6,7},{7,6},{8,9},{9,8},{10,11... | collective-permute-start | bytes 983048 | tf_op jit(solution)/shard_map/ppermute | solution.py:369
  49.6 1.2 %collective-permute-done.other_ref = bf16[256,640]{1,0:T(8,128)(2,1)S(1)} collective-permute-done((bf16[256,640]{1,0:T(8,128)(2,1)S(1)}, bf16[256,640]{1,0:T(8,128)(2,1)S(1)}, u32[]{:S(2)}, u32[]{:S(2)}) %collective-permute-start) | collective-permute-done | bytes 327712 | tf_op jit(solution)/shard_map/ppermute | solution.py:369
  50.8 1.9 %image_rows.1 = (f32[2,64,256]{2,1,0:T(8,128)S(1)}, f32[44,256]{1,0:T(8,128)S(1)}, bf16[176,256]{1,0:T(8,128)(2,1)S(1)}) custom-call(s32[2]{0:T(128)S(1)} %pad_add_fusion.place_ref.refs_0_, bf16[256,640]{1,0:T(8,128)(2,1)S(1)} %gram.1.own_ref, bf16[256,640]{1,0:T(8,128)(2,1)S(1)} %collective-permute-done.other_ref, ...), custom_call_target="tpu_custom_call" | custom-call | flops 805306368 | bytes 2097152 | tf_op jit(solution)/shard_map/image_rows/pallas_call | solution.py:279
  52.7 4.4 %collective-permute-start.1 = (bf16[176,256]{1,0:T(8,128)(2,1)S(1)}, bf16[176,256]{1,0:T(8,128)(2,1)S(1)}, u32[]{:S(2)}, u32[]{:S(2)}) collective-permute-start(bf16[176,256]{1,0:T(8,128)(2,1)S(1)} %get-tuple-element.11), channel_id=1, source_target_pairs={{0,2},{2,0},{1,3},{3,1},{4,6},{6,4},{5,7},{7,5},{8,10},{10,8},{9,1... | collective-permute-start | bytes 270344 | tf_op jit(solution)/shard_map/ppermute | solution.py:371
  57.1 2.8 %collective-permute-done.1.refs_3_ = bf16[176,256]{1,0:T(8,128)(2,1)S(1)} collective-permute-done((bf16[176,256]{1,0:T(8,128)(2,1)S(1)}, bf16[176,256]{1,0:T(8,128)(2,1)S(1)}, u32[]{:S(2)}, u32[]{:S(2)}) %collective-permute-start.1) | collective-permute-done | bytes 90144 | tf_op jit(solution)/shard_map/ppermute | solution.py:371
  59.9 1.4 %finish.1 = (f32[1,2,64,256]{3,2,1,0:T(8,128)}, f32[1,1024]{1,0:T(1,128)}) custom-call(s32[2]{0:T(128)S(1)} %pad_add_fusion.place_ref.refs_0_, f32[2,64,256]{2,1,0:T(8,128)S(1)} %get-tuple-element.9.refs_1_, f32[44,256]{1,0:T(8,128)S(1)} %get-tuple-element.10.refs_2_, bf16[176,256]{1,0:T(8,128)(2,1)S(1)} %collective-permute-done.1.refs_3_), custom_call_target="tpu_custom_call" | custom-call | flops 1048576 | bytes 262144 | tf_op jit(solution)/shard_map/finish/pallas_call | solution.py:326
  (1 shorter events, 0.0 us)
Async XLA Ops:
  4.4 38.1 %all-to-all-start = ((bf16[128,9,2,128]{3,2,1,0:T(2,128)(2,1)}), bf16[128,9,2,128]{3,2,1,0:T(2,128)(2,1)S(1)}, u32[]{:S(2)}, u32[]{:S(2)}) async-start(bf16[128,9,2,128]{3,2,1,0:T(2,128)(2,1)} %bitcast.17), calls=%async_computation | async-start | bytes 1179648 | tf_op jit(solution)/shard_map/all_to_all | solution.py:349
  23.7 0.7 %copy-start.3 = (s32[256]{0:T(256)S(1)}, s32[256]{0:T(256)}, u32[]{:S(2)}) copy-start(s32[256]{0:T(256)} %param.10) | copy-start | bytes 3076
  24.5 1.6 %copy-start.1 = (s32[256]{0:T(256)S(1)}, s32[256]{0:T(256)}, u32[]{:S(2)}) copy-start(s32[256]{0:T(256)} %param.12) | copy-start | bytes 3076
  24.6 0.7 %copy-start.2 = (s32[64]{0:T(128)S(1)}, s32[64]{0:T(128)}, u32[]{:S(2)}) copy-start(s32[64]{0:T(128)} %param.13) | copy-start | bytes 772
  25.4 0.7 %copy-start.4 = (s32[64]{0:T(128)S(1)}, s32[64]{0:T(128)}, u32[]{:S(2)}) copy-start(s32[64]{0:T(128)} %param.14) | copy-start | bytes 772
  26.1 0.7 %copy-start = (s32[256]{0:T(256)S(1)}, s32[256]{0:T(256)}, u32[]{:S(2)}) copy-start(s32[256]{0:T(256)} %param.11) | copy-start | bytes 3076
  44.2 6.6 %collective-permute-start = (bf16[256,640]{1,0:T(8,128)(2,1)S(1)}, bf16[256,640]{1,0:T(8,128)(2,1)S(1)}, u32[]{:S(2)}, u32[]{:S(2)}) collective-permute-start(bf16[256,640]{1,0:T(8,128)(2,1)S(1)} %gram.1.own_ref), channel_id=1, source_target_pairs={{0,1},{1,0},{2,3},{3,2},{4,5},{5,4},{6,7},{7,6},{8,9},{9,8},{10,11... | collective-permute-start | bytes 983048 | tf_op jit(solution)/shard_map/ppermute | solution.py:369
  52.7 7.2 %collective-permute-start.1 = (bf16[176,256]{1,0:T(8,128)(2,1)S(1)}, bf16[176,256]{1,0:T(8,128)(2,1)S(1)}, u32[]{:S(2)}, u32[]{:S(2)}) collective-permute-start(bf16[176,256]{1,0:T(8,128)(2,1)S(1)} %get-tuple-element.11), channel_id=1, source_target_pairs={{0,2},{2,0},{1,3},{3,1},{4,6},{6,4},{5,7},{7,5},{8,10},{10,8},{9,1... | collective-permute-start | bytes 270344 | tf_op jit(solution)/shard_map/ppermute | solution.py:371

commit v4 on v3

--- a/solution.py
+++ b/solution.py
@@ -39,19 +39,22 @@
     )
 
 
-def filter_kernel(v_hbm, taps_ref, dft_hbm, out_hbm, v_ref, dft_ref, ext, tail, wide, packed, sems):
+def filter_kernel(v_hbm, taps_hbm, dft_hbm, out_hbm, v_ref, taps_ref, dft_ref, ext, tail, wide, packed, sems):
     spec_dev = v_hbm.shape[1]
     copies = [pltpu.make_async_copy(v_hbm.at[s], v_ref.at[s], sems.at[s]) for s in range(2)]
     copies.append(pltpu.make_async_copy(dft_hbm, dft_ref, sems.at[2]))
-    for copy in copies:
-        copy.start()
-    taps = jnp.concatenate([taps_ref[...], taps_ref[...]], axis=1)
+    copies.append(pltpu.make_async_copy(taps_hbm, taps_ref, sems.at[3]))
+    for i in (0, 3, 2, 1):
+        copies[i].start()
     step = 256
     contract = (((1,), (1,)), ((), ()))
     for s in range(2):
         ext[s, 0:EDGE, :] = jnp.zeros((EDGE, 2 * POINTS), F32)
         ext[s, EDGE + spec_dev :, :] = jnp.zeros((EDGE, 2 * POINTS), F32)
     tail[2 * EDGE :, :] = jnp.zeros((LANES - 2 * EDGE, 2 * POINTS), BF16)
+
+    copies[3].wait()
+    taps = jnp.concatenate([taps_ref[...], taps_ref[...]], axis=1)
 
     def filtered(s, start, count):
         total = taps[0:1] * ext[s, EDGE + start : EDGE + start + count, :]
@@ -84,7 +87,7 @@
     for c in range(8):
         here = pl.ds(c * chunk // 2, chunk // 2)
         packed[here] = wide[c * chunk : (c + 1) * chunk, :].astype(BF16).reshape(chunk // 2, 2, LANES)
-        writes.append(pltpu.make_async_copy(packed.at[here], out_hbm.at[here], sems.at[3 + c]))
+        writes.append(pltpu.make_async_copy(packed.at[here], out_hbm.at[here], sems.at[4 + c]))
         writes[-1].start()
     for write in writes:
         write.wait()
@@ -95,16 +98,17 @@
     return pl.pallas_call(
         filter_kernel,
         out_shape=jax.ShapeDtypeStruct((pairs, 2, LANES), BF16),
-        in_specs=[HBM, VMEM, HBM],
+        in_specs=[HBM, HBM, HBM],
         out_specs=HBM,
         scratch_shapes=[
             pltpu.VMEM(voltages.shape, BF16),
+            pltpu.VMEM(fir_taps.shape, F32),
             pltpu.VMEM((2 * POINTS, 2 * POINTS), BF16),
             pltpu.VMEM((2, 2 * EDGE + voltages.shape[1], 2 * POINTS), F32),
             pltpu.VMEM((LANES, 2 * POINTS), BF16),
             pltpu.VMEM((2 * pairs, LANES), F32),
             pltpu.VMEM((pairs, 2, LANES), BF16),
-            pltpu.SemaphoreType.DMA((11,)),
+            pltpu.SemaphoreType.DMA((12,)),
         ],
         name="filter_bank",
         **params(2 * 256 * 256 * 1024, 1 << 20, 66_000_000),
@@ -147,14 +151,14 @@
     )(channel, station_u, station_v, rows_l, pixel_m)
 
 
-def gram_kernel(place_ref, recv_ref, station_ref, after_ref, out_ref, wide, slots):
+def gram_kernel(recv_ref, station_ref, after_ref, out_ref, wide, slots):
     chunk = 256
     for c in range(0, POINTS * ROWS, chunk):
         wide[c : c + chunk, :] = recv_ref[c // 2 : (c + chunk) // 2].reshape(chunk, LANES).astype(F32)
     lane = lax.broadcasted_iota(jnp.int32, (POINTS, LANES), 1)
     head = lane < TAPS - 1
     edge = lane < EDGE
-    left_out = jnp.logical_and(head, place_ref[0] > 0)
+    left_out = jnp.logical_and(head, lax.axis_index("pix") > 0)
 
     def column(row):
         return wide[pl.ds(row, POINTS, stride=ROWS), :]
@@ -189,11 +193,11 @@
     out_ref[:, 2 * STATIONS :] = ordered[:, 2 * half :]
 
 
-def gram(place, received, station_row, after):
+def gram(received, station_row, after):
     return pl.pallas_call(
         gram_kernel,
         out_shape=jax.ShapeDtypeStruct((STATIONS, 2 * STATIONS + LANES), BF16),
-        in_specs=[SMEM, VMEM, VMEM, ANY],
+        in_specs=[VMEM, VMEM, ANY],
         out_specs=VMEM,
         scratch_shapes=[
             pltpu.VMEM((POINTS * ROWS, LANES), F32),
@@ -201,15 +205,16 @@
         ],
         name="gram",
         **params(6 * 256 * 256 * 1024, 1 << 20),
-    )(place, received, station_row, after)
-
-
-def image_kernel(place_ref, own_ref, other_ref, cos_ref, sin_ref, rows_ref, extra_ref, send_ref, real, imag):
+    )(received, station_row, after)
+
+
+def image_kernel(own_ref, other_ref, cos_ref, sin_ref, rows_ref, extra_ref, send_ref, real, imag):
     count = rows_ref.shape[1]
     lane = lax.broadcasted_iota(jnp.int32, (STATIONS, LANES), 1)
     contract = (((1,), (1,)), ((), ()))
-    upper_core = (place_ref[0] & 1) == 1
-    second_chip = place_ref[0] >= 2
+    pix = lax.axis_index("pix")
+    upper_core = (pix & 1) == 1
+    second_chip = pix >= 2
     own_edge = own_ref[:, 2 * STATIONS :].astype(F32)
     other_edge = other_ref[:, 2 * STATIONS :].astype(F32)
     low = jnp.where(upper_core, other_edge, own_edge)
@@ -228,8 +233,8 @@
         + other_ref[:, STATIONS : 2 * STATIONS].astype(F32)
         + lax.dot_general(turned, inner, contract, preferred_element_type=F32)
     )
-    here = pl.ds(pl.multiple_of(place_ref[0] * count, count), count)
-    across = pl.ds(pl.multiple_of(place_ref[1] * count, count), count)
+    here = pl.ds(pl.multiple_of(pix * count, count), count)
+    across = pl.ds(pl.multiple_of((pix ^ 2) * count, count), count)
     rows_ref[0] = real[here, :]
     rows_ref[1] = imag[here, :]
     send_ref[0:count, :] = real[across, :].astype(BF16)
@@ -274,7 +279,7 @@
     send_ref[end:, :] = jnp.zeros((send_ref.shape[0] - end, width), BF16)
 
 
-def image_rows(place, own, other, cosine, sine, count):
+def image_rows(own, other, cosine, sine, count):
     groups = cosine.shape[1] // 512
     return pl.pallas_call(
         image_kernel,
@@ -283,15 +288,16 @@
             jax.ShapeDtypeStruct((9 * groups + 8, STATIONS), F32),
             jax.ShapeDtypeStruct((2 * count + 8 * groups + 16, STATIONS), BF16),
         ),
-        in_specs=[SMEM] + [VMEM] * 4,
+        in_specs=[VMEM] * 4,
         out_specs=(VMEM, VMEM, VMEM),
         scratch_shapes=[pltpu.VMEM((STATIONS, STATIONS), F32)] * 2,
         name="image_rows",
         **params(6 * 256 * 256 * 2048, 1 << 21),
-    )(place, own, other, cosine, sine)
-
-
-def finish_kernel(inv_total, image_scale, place_ref, rows_ref, extra_ref, got_ref, vis_ref, image_ref, turn):
+    )(own, other, cosine, sine)
+
+
+def finish_kernel(inv_total, image_scale, rows_ref, extra_ref, got_ref, vis_ref, image_ref, turn):
+    pix = lax.axis_index("pix")
     count = rows_ref.shape[1]
     groups = image_ref.shape[1] // STATIONS
     at = 8 * groups
@@ -301,7 +307,7 @@
     swapped = jnp.where(low, swapped, -swapped)
     blank = jnp.zeros((LANES - 16, STATIONS), F32)
     turn[...] = jnp.concatenate([edge, swapped, blank], axis=0).T
-    left = turn[pl.ds(pl.multiple_of(place_ref[0] * count, count), count), :]
+    left = turn[pl.ds(pl.multiple_of(pix * count, count), count), :]
     right = jnp.concatenate([edge, edge, blank], axis=0).astype(BF16)
     lane = lax.broadcasted_iota(jnp.int32, (count, LANES), 1)
     for part in range(2):
@@ -321,7 +327,7 @@
         ) * (inv_total * image_scale)
 
 
-def finish(place, rows, extra, got, pixels, inv_total, image_scale):
+def finish(rows, extra, got, pixels, inv_total, image_scale):
     count = rows.shape[1]
     return pl.pallas_call(
         lambda *refs: finish_kernel(inv_total, image_scale, *refs),
@@ -329,12 +335,12 @@
             jax.ShapeDtypeStruct((1, 2, count, STATIONS), F32),
             jax.ShapeDtypeStruct((1, pixels), F32),
         ),
-        in_specs=[SMEM] + [VMEM] * 3,
+        in_specs=[VMEM] * 3,
         out_specs=(VMEM, VMEM),
         scratch_shapes=[pltpu.VMEM((STATIONS, LANES), F32)],
         name="finish",
         **params(1 << 20, 1 << 18),
-    )(place, rows, extra, got)
+    )(rows, extra, got)
 
 
 def on_device(voltages, fir_taps, station_of_slot, station_u, station_v, pixel_l, pixel_m):
@@ -343,7 +349,6 @@
     spectra_total = spec_dev * pix_count
     pix = lax.axis_index("pix")
     across = jnp.where(pix < 2, pix + 2, pix - 2)
-    place = jnp.stack([pix, across]).astype(jnp.int32)
     rows_l = pixel_l.shape[0] // pix_count
     sent = filter_bank(voltages, fir_taps).reshape(POINTS, ROWS // 2, 2, LANES)
     received = lax.all_to_all(sent, "chan", split_axis=0, concat_axis=0, tiled=True)
@@ -365,13 +370,11 @@
         2 * pixels,
     )
     station_row = station_of_slot.reshape(POINTS, 2).T.reshape(1, STATIONS)
-    own = gram(place, received.reshape(-1, 2, LANES), station_row, cosine)
+    own = gram(received.reshape(-1, 2, LANES), station_row, cosine)
     other = lax.ppermute(own, "pix", [(0, 1), (1, 0), (2, 3), (3, 2)])
-    rows, extra, send = image_rows(place, own, other, cosine, sine, STATIONS // pix_count)
+    rows, extra, send = image_rows(own, other, cosine, sine, STATIONS // pix_count)
     got = lax.ppermute(send, "pix", [(0, 2), (2, 0), (1, 3), (3, 1)])
-    return finish(
-        place, rows, extra, got, pixels, 1.0 / spectra_total, math.sqrt(spectra_total) / STATIONS
-    )
+    return finish(rows, extra, got, pixels, 1.0 / spectra_total, math.sqrt(spectra_total) / STATIONS)
 
 
 def solution(mesh):

time: 61.7 us -> 59.4 us (0.963)
  Pallas kernels: 12.2 us -> 9.87 us
    pallas_call x1, Pallas kernels: 3.78 us -> 3.04 us  [filter_bank(): pl.pallas_call(filter_kernel, out_shape=jax.ShapeDtypeStruct((pairs, 2, L...]
  transfers between devices with their start and end apart: 3 -> 3, of which waited for: 3 -> 3; matrix products, arithmetic and copies ran while one was open for 1% -> 1% of each run, Pallas kernels for 5% -> 6%
where the time goes in v4:
time: 59.4 us; the launch traced here: 59.1 us
  starting transfers between devices  29 us (49%)
  waiting for transfers between devices  16.4 us (28%)
  Pallas kernels  9.87 us (17%)
  local copies, waits for them, and re-layouts  2.96 us (5%)
  between operations  0.72 us (1%)
    all_to_all x1, starting transfers between devices, on_device(): lax.all_to_all(sent, 'chan', split_axis=0, concat_axis=0, tiled=True)  19.3 us
    all_to_all x1, waiting for transfers between devices, on_device(): lax.all_to_all(sent, 'chan', split_axis=0, concat_axis=0, tiled=True)  12.3 us
    ppermute x1, starting transfers between devices, on_device(): other = lax.ppermute(own, 'pix', [(0, 1), (1, 0), (2, 3), (3, 2)])  5.39 us
    ppermute x1, starting transfers between devices, on_device(): got = lax.ppermute(send, 'pix', [(0, 2), (2, 0), (1, 3), (3, 1)])  4.36 us
    pallas_call x1, Pallas kernels, steering(): pl.pallas_call(steering_kernel, out_shape=(out, out), in_specs=[SMEM] + [...  3.35 us
    pallas_call x1, Pallas kernels, filter_bank(): pl.pallas_call(filter_kernel, out_shape=jax.ShapeDtypeStruct((pairs, 2, L...  3.04 us
    ppermute x1, waiting for transfers between devices, on_device(): got = lax.ppermute(send, 'pix', [(0, 2), (2, 0), (1, 3), (3, 1)])  2.83 us
    unnamed x10, local copies, waits for them, and re-layouts  2.69 us
  transfers between devices with their start and end apart: 3, of which 3 were waited for; matrix products, arithmetic and copies ran while one was open for 1% of the time, Pallas kernels for 6%

profile of v4, /device:TPU:1, one launch (start us, length us, event | category | flops | bytes accessed | tf_op | source)
XLA Modules:
  0.0 59.1 jit_solution(11848480071520832004)
XLA Ops:
  0.6 3.0 %filter_bank.1 = bf16[1152,2,128]{2,1,0:T(2,128)(2,1)} custom-call(bf16[2,512,256]{2,1,0:T(8,128)(2,1)} %v_hbm.1, f32[4,128]{1,0:T(4,128)} %taps_hbm.1, bf16[256,256]{1,0:T(8,128)(2,1)} %constant.24.dft_hbm), custom_call_target="tpu_custom_call" | custom-call | flops 134217728 | bytes 1048576 | tf_op jit(solution)/shard_map/filter_bank/pallas_call | solution.py:98
  3.7 19.3 %all-to-all-start = ((bf16[128,9,2,128]{3,2,1,0:T(2,128)(2,1)}), bf16[128,9,2,128]{3,2,1,0:T(2,128)(2,1)S(1)}, u32[]{:S(2)}, u32[]{:S(2)}) async-start(bf16[128,9,2,128]{3,2,1,0:T(2,128)(2,1)} %bitcast.15), calls=%async_computation | async-start | bytes 1179648 | tf_op jit(solution)/shard_map/all_to_all | solution.py:354
  23.0 0.0 copy-start.3
  23.0 0.7 %copy-done.3 = s32[256]{0:T(256)S(1)} copy-done((s32[256]{0:T(256)S(1)}, s32[256]{0:T(256)}, u32[]{:S(2)}) %copy-start.3) | copy-done | bytes 1048
  23.7 0.1 reshape.18
  23.8 0.0 copy-start.1
  23.8 0.1 copy.10
  23.9 0.0 copy-start.2
  23.9 0.7 %copy-done.2 = s32[64]{0:T(128)S(1)} copy-done((s32[64]{0:T(128)S(1)}, s32[64]{0:T(128)}, u32[]{:S(2)}) %copy-start.2) | copy-done | bytes 280
  24.6 0.1 fusion
  24.6 0.0 copy-start.4
  24.6 0.7 %copy-done.4 = s32[64]{0:T(128)S(1)} copy-done((s32[64]{0:T(128)S(1)}, s32[64]{0:T(128)}, u32[]{:S(2)}) %copy-start.4) | copy-done | bytes 280
  25.3 0.1 add_bitcast_fusion
  25.4 0.0 copy-start
  25.4 0.0 copy-done.1
  25.4 0.7 %copy-done = s32[256]{0:T(256)S(1)} copy-done((s32[256]{0:T(256)S(1)}, s32[256]{0:T(256)}, u32[]{:S(2)}) %copy-start) | copy-done | bytes 1048
  26.1 3.3 %steering.1 = (bf16[256,2048]{1,0:T(8,128)(2,1)S(1)}, bf16[256,2048]{1,0:T(8,128)(2,1)S(1)}) custom-call(s32[1]{0:T(128)} %bitcast.4.chan_ref, s32[1,256]{1,0:T(1,128)S(1)} %bitcast.13, s32[1,256]{1,0:T(1,128)S(1)} %bitcast.14, s32[1,128]{1,0:T(1,128)S(1)} %get-tuple-element.14.l_ref, s32[1,128]{1,0:T(1,128)S(1)} %get-tuple-element.15.m_ref), custom_call_target="tpu_custom_call" | custom-call | flops 3145728 | bytes 2097152 | tf_op jit(solution)/shard_map/steering/pallas_call | solution.py:144
  29.4 12.3 %all-to-all-done = bf16[128,9,2,128]{3,2,1,0:T(2,128)(2,1)S(1)} async-done(((bf16[128,9,2,128]{3,2,1,0:T(2,128)(2,1)}), bf16[128,9,2,128]{3,2,1,0:T(2,128)(2,1)S(1)}, u32[]{:S(2)}, u32[]{:S(2)}) %all-to-all-start) | async-done | bytes 589856 | tf_op jit(solution)/shard_map/all_to_all | solution.py:354
  41.7 1.2 %gram.1.own_ref = bf16[256,640]{1,0:T(8,128)(2,1)S(1)} custom-call(bf16[1152,2,128]{2,1,0:T(2,128)(2,1)S(1)} %bitcast.11, s32[1,256]{1,0:T(1,128)S(1)} %bitcast.12, bf16[256,2048]{1,0:T(8,128)(2,1)S(1)} %get-tuple-element.7.after_ref.cos_ref), custom_call_target="tpu_custom_call" | custom-call | flops 402653184 | bytes 1048576 | tf_op jit(solution)/shard_map/gram/pallas_call | solution.py:197
  42.9 5.4 %collective-permute-start = (bf16[256,640]{1,0:T(8,128)(2,1)S(1)}, bf16[256,640]{1,0:T(8,128)(2,1)S(1)}, u32[]{:S(2)}, u32[]{:S(2)}) collective-permute-start(bf16[256,640]{1,0:T(8,128)(2,1)S(1)} %gram.1.own_ref), channel_id=1, source_target_pairs={{0,1},{1,0},{2,3},{3,2},{4,5},{5,4},{6,7},{7,6},{8,9},{9,8},{10,11... | collective-permute-start | bytes 983048 | tf_op jit(solution)/shard_map/ppermute | solution.py:374
  48.3 1.2 %collective-permute-done.other_ref = bf16[256,640]{1,0:T(8,128)(2,1)S(1)} collective-permute-done((bf16[256,640]{1,0:T(8,128)(2,1)S(1)}, bf16[256,640]{1,0:T(8,128)(2,1)S(1)}, u32[]{:S(2)}, u32[]{:S(2)}) %collective-permute-start) | collective-permute-done | bytes 327712 | tf_op jit(solution)/shard_map/ppermute | solution.py:374
  49.5 1.4 %image_rows.1 = (f32[2,64,256]{2,1,0:T(8,128)S(1)}, f32[44,256]{1,0:T(8,128)S(1)}, bf16[176,256]{1,0:T(8,128)(2,1)S(1)}) custom-call(bf16[256,640]{1,0:T(8,128)(2,1)S(1)} %gram.1.own_ref, bf16[256,640]{1,0:T(8,128)(2,1)S(1)} %collective-permute-done.other_ref, bf16[256,2048]{1,0:T(8,128)(2,1)S(1)} %get-tuple-element.7.after_ref.cos_ref, ...), custom_call_target="tpu_custom_call" | custom-call | flops 805306368 | bytes 2097152 | tf_op jit(solution)/shard_map/image_rows/pallas_call | solution.py:284
  51.0 4.4 %collective-permute-start.1 = (bf16[176,256]{1,0:T(8,128)(2,1)S(1)}, bf16[176,256]{1,0:T(8,128)(2,1)S(1)}, u32[]{:S(2)}, u32[]{:S(2)}) collective-permute-start(bf16[176,256]{1,0:T(8,128)(2,1)S(1)} %get-tuple-element.11), channel_id=1, source_target_pairs={{0,2},{2,0},{1,3},{3,1},{4,6},{6,4},{5,7},{7,5},{8,10},{10,8},{9,1... | collective-permute-start | bytes 270344 | tf_op jit(solution)/shard_map/ppermute | solution.py:376
  55.3 2.8 %collective-permute-done.1.refs_2_ = bf16[176,256]{1,0:T(8,128)(2,1)S(1)} collective-permute-done((bf16[176,256]{1,0:T(8,128)(2,1)S(1)}, bf16[176,256]{1,0:T(8,128)(2,1)S(1)}, u32[]{:S(2)}, u32[]{:S(2)}) %collective-permute-start.1) | collective-permute-done | bytes 90144 | tf_op jit(solution)/shard_map/ppermute | solution.py:376
  58.2 0.9 %finish.1 = (f32[1,2,64,256]{3,2,1,0:T(8,128)}, f32[1,1024]{1,0:T(1,128)}) custom-call(f32[2,64,256]{2,1,0:T(8,128)S(1)} %get-tuple-element.9.refs_0_, f32[44,256]{1,0:T(8,128)S(1)} %get-tuple-element.10.refs_1_, bf16[176,256]{1,0:T(8,128)(2,1)S(1)} %collective-permute-done.1.refs_2_), custom_call_target="tpu_custom_call" | custom-call | flops 1048576 | bytes 262144 | tf_op jit(solution)/shard_map/finish/pallas_call | solution.py:332
  (1 shorter events, 0.0 us)
Async XLA Ops:
  3.7 38.1 %all-to-all-start = ((bf16[128,9,2,128]{3,2,1,0:T(2,128)(2,1)}), bf16[128,9,2,128]{3,2,1,0:T(2,128)(2,1)S(1)}, u32[]{:S(2)}, u32[]{:S(2)}) async-start(bf16[128,9,2,128]{3,2,1,0:T(2,128)(2,1)} %bitcast.15), calls=%async_computation | async-start | bytes 1179648 | tf_op jit(solution)/shard_map/all_to_all | solution.py:354
  23.0 0.7 %copy-start.3 = (s32[256]{0:T(256)S(1)}, s32[256]{0:T(256)}, u32[]{:S(2)}) copy-start(s32[256]{0:T(256)} %param.10) | copy-start | bytes 3076
  23.8 1.6 %copy-start.1 = (s32[256]{0:T(256)S(1)}, s32[256]{0:T(256)}, u32[]{:S(2)}) copy-start(s32[256]{0:T(256)} %param.12) | copy-start | bytes 3076
  23.9 0.7 %copy-start.2 = (s32[64]{0:T(128)S(1)}, s32[64]{0:T(128)}, u32[]{:S(2)}) copy-start(s32[64]{0:T(128)} %param.13) | copy-start | bytes 772
  24.6 0.7 %copy-start.4 = (s32[64]{0:T(128)S(1)}, s32[64]{0:T(128)}, u32[]{:S(2)}) copy-start(s32[64]{0:T(128)} %param.14) | copy-start | bytes 772
  25.4 0.7 %copy-start = (s32[256]{0:T(256)S(1)}, s32[256]{0:T(256)}, u32[]{:S(2)}) copy-start(s32[256]{0:T(256)} %param.11) | copy-start | bytes 3076
  42.9 6.6 %collective-permute-start = (bf16[256,640]{1,0:T(8,128)(2,1)S(1)}, bf16[256,640]{1,0:T(8,128)(2,1)S(1)}, u32[]{:S(2)}, u32[]{:S(2)}) collective-permute-start(bf16[256,640]{1,0:T(8,128)(2,1)S(1)} %gram.1.own_ref), channel_id=1, source_target_pairs={{0,1},{1,0},{2,3},{3,2},{4,5},{5,4},{6,7},{7,6},{8,9},{9,8},{10,11... | collective-permute-start | bytes 983048 | tf_op jit(solution)/shard_map/ppermute | solution.py:374
  51.0 7.2 %collective-permute-start.1 = (bf16[176,256]{1,0:T(8,128)(2,1)S(1)}, bf16[176,256]{1,0:T(8,128)(2,1)S(1)}, u32[]{:S(2)}, u32[]{:S(2)}) collective-permute-start(bf16[176,256]{1,0:T(8,128)(2,1)S(1)} %get-tuple-element.11), channel_id=1, source_target_pairs={{0,2},{2,0},{1,3},{3,1},{4,6},{6,4},{5,7},{7,5},{8,10},{10,8},{9,1... | collective-permute-start | bytes 270344 | tf_op jit(solution)/shard_map/ppermute | solution.py:376

commit v5 on v4

--- a/solution.py
+++ b/solution.py
@@ -41,52 +41,60 @@
 
 def filter_kernel(v_hbm, taps_hbm, dft_hbm, out_hbm, v_ref, taps_ref, dft_ref, ext, tail, wide, packed, sems):
     spec_dev = v_hbm.shape[1]
+    step = 256
+    pieces = [(s, t) for s in range(2) for t in range(0, spec_dev, step)]
     copies = [pltpu.make_async_copy(v_hbm.at[s], v_ref.at[s], sems.at[s]) for s in range(2)]
-    copies.append(pltpu.make_async_copy(dft_hbm, dft_ref, sems.at[2]))
-    copies.append(pltpu.make_async_copy(taps_hbm, taps_ref, sems.at[3]))
-    for i in (0, 3, 2, 1):
+    copies.append(pltpu.make_async_copy(taps_hbm, taps_ref, sems.at[2]))
+    copies.append(pltpu.make_async_copy(dft_hbm, dft_ref, sems.at[3]))
+    for i in (2, 0, 3, 1):
         copies[i].start()
-    step = 256
     contract = (((1,), (1,)), ((), ()))
+    blank = jnp.zeros((EDGE, POINTS), F32)
     for s in range(2):
-        ext[s, 0:EDGE, :] = jnp.zeros((EDGE, 2 * POINTS), F32)
-        ext[s, EDGE + spec_dev :, :] = jnp.zeros((EDGE, 2 * POINTS), F32)
+        for half in range(2):
+            ext[s, half, 0:EDGE, :] = blank
+            ext[s, half, EDGE + spec_dev :, :] = blank
     tail[2 * EDGE :, :] = jnp.zeros((LANES - 2 * EDGE, 2 * POINTS), BF16)
-
-    copies[3].wait()
-    taps = jnp.concatenate([taps_ref[...], taps_ref[...]], axis=1)
+    copies[2].wait()
+    taps = taps_ref[...]
 
     def filtered(s, start, count):
-        total = taps[0:1] * ext[s, EDGE + start : EDGE + start + count, :]
-        for k in range(1, TAPS):
-            total = total + taps[k : k + 1] * ext[s, EDGE - k + start : EDGE - k + start + count, :]
-        return total
-
-    for s in range(2):
-        copies[s].wait()
-        ext[s, EDGE : EDGE + spec_dev, :] = v_ref[s].astype(F32)
-        if s == 0:
-            copies[2].wait()
-        for t in range(0, spec_dev, step):
-            spectra = lax.dot_general(
-                dft_ref[...], filtered(s, t, step).astype(BF16), contract, preferred_element_type=F32
-            )
-            for r in range(2):
-                for part in range(step // LANES):
-                    row = s * 8 + r * 4 + t // LANES + part
-                    wide[pl.ds(row, POINTS, stride=ROWS), :] = spectra[
-                        r * POINTS : (r + 1) * POINTS, part * LANES : (part + 1) * LANES
-                    ]
-    edges = jnp.concatenate([filtered(s, spec_dev, EDGE) for s in range(2)], axis=0)
-    tail[0 : 2 * EDGE, :] = edges.astype(BF16)
+        halves = []
+        for half in range(2):
+            total = taps[0:1] * ext[s, half, EDGE + start : EDGE + start + count, :]
+            for k in range(1, TAPS):
+                first = EDGE - k + start
+                total = total + taps[k : k + 1] * ext[s, half, first : first + count, :]
+            halves.append(total.astype(BF16))
+        return jnp.concatenate(halves, axis=1)
+
+    for i, (s, t) in enumerate(pieces):
+        if t == 0:
+            copies[s].wait()
+            for half in range(2):
+                ext[s, half, EDGE : EDGE + spec_dev, :] = v_ref[
+                    s, :, half * POINTS : (half + 1) * POINTS
+                ].astype(F32)
+        if i == 0:
+            copies[3].wait()
+        spectra = lax.dot_general(
+            dft_ref[...], filtered(s, t, step), contract, preferred_element_type=F32
+        )
+        for r in range(2):
+            for part in range(step // LANES):
+                row = s * 8 + r * 4 + t // LANES + part
+                wide[pl.ds(row, POINTS, stride=ROWS), :] = spectra[
+                    r * POINTS : (r + 1) * POINTS, part * LANES : (part + 1) * LANES
+                ]
+    tail[0 : 2 * EDGE, :] = jnp.concatenate([filtered(s, spec_dev, EDGE) for s in range(2)], axis=0)
     spectra = lax.dot_general(dft_ref[...], tail[...], contract, preferred_element_type=F32)
     for r in range(2):
         wide[pl.ds(16 + r, POINTS, stride=ROWS), :] = spectra[r * POINTS : (r + 1) * POINTS]
     chunk = POINTS * ROWS // 8
     writes = []
     for c in range(8):
-        here = pl.ds(c * chunk // 2, chunk // 2)
-        packed[here] = wide[c * chunk : (c + 1) * chunk, :].astype(BF16).reshape(chunk // 2, 2, LANES)
+        here = pl.ds(c * chunk, chunk)
+        packed[here] = wide[c * chunk : (c + 1) * chunk, :].astype(BF16)
         writes.append(pltpu.make_async_copy(packed.at[here], out_hbm.at[here], sems.at[4 + c]))
         writes[-1].start()
     for write in writes:
@@ -94,20 +102,20 @@
 
 
 def filter_bank(voltages, fir_taps):
-    pairs = POINTS * ROWS // 2
+    rows = POINTS * ROWS
     return pl.pallas_call(
         filter_kernel,
-        out_shape=jax.ShapeDtypeStruct((pairs, 2, LANES), BF16),
+        out_shape=jax.ShapeDtypeStruct((rows, LANES), BF16),
         in_specs=[HBM, HBM, HBM],
         out_specs=HBM,
         scratch_shapes=[
             pltpu.VMEM(voltages.shape, BF16),
             pltpu.VMEM(fir_taps.shape, F32),
             pltpu.VMEM((2 * POINTS, 2 * POINTS), BF16),
-            pltpu.VMEM((2, 2 * EDGE + voltages.shape[1], 2 * POINTS), F32),
+            pltpu.VMEM((2, 2, 2 * EDGE + voltages.shape[1], POINTS), F32),
             pltpu.VMEM((LANES, 2 * POINTS), BF16),
-            pltpu.VMEM((2 * pairs, LANES), F32),
-            pltpu.VMEM((pairs, 2, LANES), BF16),
+            pltpu.VMEM((rows, LANES), F32),
+            pltpu.VMEM((rows, LANES), BF16),
             pltpu.SemaphoreType.DMA((12,)),
         ],
         name="filter_bank",
@@ -115,7 +123,7 @@
     )(voltages, fir_taps, dft_matrix(POINTS))
 
 
-def steering_kernel(chan_ref, u_ref, v_ref, l_ref, m_ref, cos_ref, sin_ref):
+def steering_kernel(chan_ref, u_ref, v_ref, l_ref, m_ref, *out_refs):
     freq = POINTS + chan_ref[0]
     rows = lax.broadcasted_iota(jnp.int32, (STATIONS, STATIONS), 0)
     cols = lax.broadcasted_iota(jnp.int32, (STATIONS, STATIONS), 1)
@@ -132,29 +140,32 @@
     l_cos, l_sin = phases(column(u_ref), l_ref[...])
     m_cos, m_sin = phases(column(v_ref), m_ref[...])
     first = lax.broadcasted_iota(jnp.int32, (STATIONS, LANES), 1) < 64
-    for q in range(cos_ref.shape[1] // LANES):
+    blocks = out_refs[0].shape[1] // LANES
+    for q in range(2 * blocks):
+        cos_ref, sin_ref = out_refs[2 * (q // blocks) : 2 * (q // blocks) + 2]
+        at = q % blocks * LANES
         a_cos = jnp.where(first, l_cos[:, 2 * q : 2 * q + 1], l_cos[:, 2 * q + 1 : 2 * q + 2])
         a_sin = jnp.where(first, l_sin[:, 2 * q : 2 * q + 1], l_sin[:, 2 * q + 1 : 2 * q + 2])
-        cos_ref[:, q * LANES : (q + 1) * LANES] = (a_cos * m_cos - a_sin * m_sin).astype(BF16)
-        sin_ref[:, q * LANES : (q + 1) * LANES] = (a_sin * m_cos + a_cos * m_sin).astype(BF16)
+        cos_ref[:, at : at + LANES] = (a_cos * m_cos - a_sin * m_sin).astype(BF16)
+        sin_ref[:, at : at + LANES] = (a_sin * m_cos + a_cos * m_sin).astype(BF16)
 
 
 def steering(channel, station_u, station_v, rows_l, pixel_m, pixels):
     out = jax.ShapeDtypeStruct((STATIONS, pixels), BF16)
     return pl.pallas_call(
         steering_kernel,
-        out_shape=(out, out),
+        out_shape=(out,) * 4,
         in_specs=[SMEM] + [VMEM] * 4,
-        out_specs=(VMEM, VMEM),
+        out_specs=(VMEM,) * 4,
         name="steering",
-        **params(6 * STATIONS * pixels, 4 * STATIONS * pixels),
+        **params(12 * STATIONS * pixels, 8 * STATIONS * pixels),
     )(channel, station_u, station_v, rows_l, pixel_m)
 
 
 def gram_kernel(recv_ref, station_ref, after_ref, out_ref, wide, slots):
     chunk = 256
     for c in range(0, POINTS * ROWS, chunk):
-        wide[c : c + chunk, :] = recv_ref[c // 2 : (c + chunk) // 2].reshape(chunk, LANES).astype(F32)
+        wide[c : c + chunk, :] = recv_ref[c : c + chunk].astype(F32)
     lane = lax.broadcasted_iota(jnp.int32, (POINTS, LANES), 1)
     head = lane < TAPS - 1
     edge = lane < EDGE
@@ -208,17 +219,17 @@
     )(received, station_row, after)
 
 
-def image_kernel(own_ref, other_ref, cos_ref, sin_ref, rows_ref, extra_ref, send_ref, real, imag):
-    count = rows_ref.shape[1]
+def chip_sums(own_ref, other_ref, real, imag):
+    pix = lax.axis_index("pix")
     lane = lax.broadcasted_iota(jnp.int32, (STATIONS, LANES), 1)
     contract = (((1,), (1,)), ((), ()))
-    pix = lax.axis_index("pix")
     upper_core = (pix & 1) == 1
-    second_chip = pix >= 2
     own_edge = own_ref[:, 2 * STATIONS :].astype(F32)
     other_edge = other_ref[:, 2 * STATIONS :].astype(F32)
     low = jnp.where(upper_core, other_edge, own_edge)
     high = jnp.where(upper_core, own_edge, other_edge)
+    outer = jnp.where(pix >= 2, pltpu.roll(low, LANES - 16, 1), high)
+    outer = jnp.where(lane < 16, outer, 0.0).T[0:16]
     inner = jnp.where(lane < 16, low + pltpu.roll(high, LANES - 16, 1), 0.0)
     turned = jnp.where(lane < 8, pltpu.roll(inner, LANES - 8, 1), -pltpu.roll(inner, 8, 1))
     turned = jnp.where(lane < 16, turned, 0.0).astype(BF16)
@@ -233,25 +244,17 @@
         + other_ref[:, STATIONS : 2 * STATIONS].astype(F32)
         + lax.dot_general(turned, inner, contract, preferred_element_type=F32)
     )
-    here = pl.ds(pl.multiple_of(pix * count, count), count)
-    across = pl.ds(pl.multiple_of((pix ^ 2) * count, count), count)
-    rows_ref[0] = real[here, :]
-    rows_ref[1] = imag[here, :]
-    send_ref[0:count, :] = real[across, :].astype(BF16)
-    send_ref[count : 2 * count, :] = imag[across, :].astype(BF16)
-
-    outer = jnp.where(second_chip, pltpu.roll(low, LANES - 16, 1), high)
-    outer = jnp.where(lane < 16, outer, 0.0).T[0:16]
-    edge_rows = outer[0:8] + pltpu.roll(outer[8:16], 4, 0)
-
+    return outer
+
+
+def partial_image(real, imag, outer, cos_ref, sin_ref, store):
     rows = lax.broadcasted_iota(jnp.int32, (STATIONS, STATIONS), 0)
     cols = lax.broadcasted_iota(jnp.int32, (STATIONS, STATIONS), 1)
     flag_real = jnp.where(rows == cols, 0.0, real[...]).astype(BF16)
     flag_real = jnp.concatenate([flag_real, outer.astype(BF16)], axis=0)
     flag_imag = jnp.where(rows == cols, 0.0, imag[...]).astype(BF16)
     width = STATIONS
-    groups = cos_ref.shape[1] // width // 2
-    for q in range(2 * groups):
+    for q in range(cos_ref.shape[1] // width):
         cosine = cos_ref[:, q * width : (q + 1) * width]
         sine = sin_ref[:, q * width : (q + 1) * width]
         by_cos = jnp.dot(flag_real, cosine, preferred_element_type=F32)
@@ -263,37 +266,72 @@
         )
         first = by_cos[STATIONS : STATIONS + 8] - by_sin[STATIONS + 8 :]
         second = by_cos[STATIONS + 8 :] + by_sin[STATIONS : STATIONS + 8]
-        beams = first + pltpu.roll(second, 4, 0)
-        if q < groups:
-            extra_ref[8 * q : 8 * q + 8, :] = beams
-            extra_ref[8 * groups + 8 + q : 8 * groups + 9 + q, :] = pixel
-        else:
-            at = 2 * count + 8 * (q - groups)
-            send_ref[at : at + 8, :] = beams.astype(BF16)
-            at = 2 * count + 8 * groups + 8 + q - groups
-            send_ref[at : at + 1, :] = pixel.astype(BF16)
-    extra_ref[8 * groups : 8 * groups + 8, :] = edge_rows
-    at = 2 * count + 8 * groups
-    send_ref[at : at + 8, :] = edge_rows.astype(BF16)
-    end = at + 8 + groups
-    send_ref[end:, :] = jnp.zeros((send_ref.shape[0] - end, width), BF16)
-
-
-def image_rows(own, other, cosine, sine, count):
-    groups = cosine.shape[1] // 512
-    return pl.pallas_call(
-        image_kernel,
+        store(q, first + pltpu.roll(second, 4, 0), pixel)
+
+
+def send_kernel(own_ref, other_ref, cos_ref, sin_ref, send_ref, real, imag):
+    groups = cos_ref.shape[1] // STATIONS
+    count = STATIONS // 4
+    outer = chip_sums(own_ref, other_ref, real, imag)
+    across = pl.ds(pl.multiple_of((lax.axis_index("pix") ^ 2) * count, count), count)
+    send_ref[0:count, :] = real[across, :].astype(BF16)
+    send_ref[count : 2 * count, :] = imag[across, :].astype(BF16)
+    base = 2 * count
+    edge = base + 8 * groups
+    send_ref[edge : edge + 8, :] = (outer[0:8] + pltpu.roll(outer[8:16], 4, 0)).astype(BF16)
+    send_ref[edge + 8 :, :] = jnp.zeros((send_ref.shape[0] - edge - 8, STATIONS), BF16)
+
+    def store(q, beams, pixel):
+        send_ref[base + 8 * q : base + 8 * q + 8, :] = beams.astype(BF16)
+        send_ref[edge + 8 + q : edge + 9 + q, :] = pixel.astype(BF16)
+
+    partial_image(real, imag, outer, cos_ref, sin_ref, store)
+
+
+def keep_kernel(own_ref, other_ref, cos_ref, sin_ref, after_ref, rows_ref, extra_ref, real, imag):
+    groups = cos_ref.shape[1] // STATIONS
+    count = rows_ref.shape[1]
+    outer = chip_sums(own_ref, other_ref, real, imag)
+    here = pl.ds(pl.multiple_of(lax.axis_index("pix") * count, count), count)
+    rows_ref[0] = real[here, :]
+    rows_ref[1] = imag[here, :]
+    edge = 8 * groups
+    extra_ref[edge : edge + 8, :] = outer[0:8] + pltpu.roll(outer[8:16], 4, 0)
+
+    def store(q, beams, pixel):
+        extra_ref[8 * q : 8 * q + 8, :] = beams
+        extra_ref[edge + 8 + q : edge + 9 + q, :] = pixel
+
+    partial_image(real, imag, outer, cos_ref, sin_ref, store)
+
+
+def send_part(own, other, cosine, sine, count):
+    groups = cosine.shape[1] // STATIONS
+    return pl.pallas_call(
+        send_kernel,
+        out_shape=jax.ShapeDtypeStruct((2 * count + 8 * groups + 16, STATIONS), BF16),
+        in_specs=[VMEM] * 4,
+        out_specs=VMEM,
+        scratch_shapes=[pltpu.VMEM((STATIONS, STATIONS), F32)] * 2,
+        name="send_part",
+        **params(6 * 256 * 256 * 1024, 1 << 20),
+    )(own, other, cosine, sine)
+
+
+def keep_part(own, other, cosine, sine, after, count):
+    groups = cosine.shape[1] // STATIONS
+    return pl.pallas_call(
+        keep_kernel,
         out_shape=(
             jax.ShapeDtypeStruct((2, count, STATIONS), F32),
             jax.ShapeDtypeStruct((9 * groups + 8, STATIONS), F32),
-            jax.ShapeDtypeStruct((2 * count + 8 * groups + 16, STATIONS), BF16),
         ),
-        in_specs=[VMEM] * 4,
-        out_specs=(VMEM, VMEM, VMEM),
+        in_specs=[VMEM] * 4 + [ANY],
+        out_specs=(VMEM, VMEM),
         scratch_shapes=[pltpu.VMEM((STATIONS, STATIONS), F32)] * 2,
-        name="image_rows",
-        **params(6 * 256 * 256 * 2048, 1 << 21),
-    )(own, other, cosine, sine)
+        name="keep_part",
+        **params(6 * 256 * 256 * 1024, 1 << 20),
+    )(own, other, cosine, sine, after)
 
 
 def finish_kernel(inv_total, image_scale, rows_ref, extra_ref, got_ref, vis_ref, image_ref, turn):
@@ -304,12 +342,10 @@
     edge = extra_ref[at : at + 8, :] + got_ref[2 * count + at : 2 * count + at + 8, :].astype(F32)
     swapped = pltpu.roll(edge, 4, 0)
     low = lax.broadcasted_iota(jnp.int32, (8, STATIONS), 0) < 4
-    swapped = jnp.where(low, swapped, -swapped)
-    blank = jnp.zeros((LANES - 16, STATIONS), F32)
-    turn[...] = jnp.concatenate([edge, swapped, blank], axis=0).T
+    turn[...] = jnp.concatenate([edge, jnp.where(low, swapped, -swapped)], axis=0).T
     left = turn[pl.ds(pl.multiple_of(pix * count, count), count), :]
-    right = jnp.concatenate([edge, edge, blank], axis=0).astype(BF16)
-    lane = lax.broadcasted_iota(jnp.int32, (count, LANES), 1)
+    right = jnp.concatenate([edge, edge], axis=0).astype(BF16)
+    lane = lax.broadcasted_iota(jnp.int32, left.shape, 1)
     for part in range(2):
         got = got_ref[part * count : (part + 1) * count, :].astype(F32)
         chosen = jnp.where((lane < 8) if part == 0 else (lane >= 8), left, 0.0).astype(BF16)
@@ -337,7 +373,7 @@
         ),
         in_specs=[VMEM] * 3,
         out_specs=(VMEM, VMEM),
-        scratch_shapes=[pltpu.VMEM((STATIONS, LANES), F32)],
+        scratch_shapes=[pltpu.VMEM((STATIONS, 16), F32)],
         name="finish",
         **params(1 << 20, 1 << 18),
     )(rows, extra, got)
@@ -361,19 +397,21 @@
         ]
     )[None]
     pixels = rows_l * pixel_m.shape[0]
-    cosine, sine = steering(
+    here_cos, here_sin, across_cos, across_sin = steering(
         lax.axis_index("chan")[None].astype(jnp.int32),
         station_u[None],
         station_v[None],
         block_l,
         jnp.concatenate([pixel_m, pixel_m])[None],
-        2 * pixels,
+        pixels,
     )
     station_row = station_of_slot.reshape(POINTS, 2).T.reshape(1, STATIONS)
-    own = gram(received.reshape(-1, 2, LANES), station_row, cosine)
+    own = gram(received.reshape(-1, LANES), station_row, here_cos)
     other = lax.ppermute(own, "pix", [(0, 1), (1, 0), (2, 3), (3, 2)])
-    rows, extra, send = image_rows(own, other, cosine, sine, STATIONS // pix_count)
+    count = STATIONS // pix_count
+    send = send_part(own, other, across_cos, across_sin, count)
     got = lax.ppermute(send, "pix", [(0, 2), (2, 0), (1, 3), (3, 1)])
+    rows, extra = keep_part(own, other, here_cos, here_sin, send, count)
     return finish(rows, extra, got, pixels, 1.0 / spectra_total, math.sqrt(spectra_total) / STATIONS)
 
 

time: 59.4 us -> 58 us (0.976)
  waiting for transfers between devices: 16.4 us -> 15.5 us
    ppermute x1, waiting for transfers between devices: 2.83 us -> 1.94 us  [on_device(): got = lax.ppermute(send, 'pix', [(0, 2), (2, 0), (1, 3), (3, 1)])]
    pallas_call x3 -> x4, Pallas kernels: 7.8 us -> 7.77 us  [the longest x1 3.35 us: steering(): pl.pallas_call(steering_kernel, out_shape=(out,) * 4, in_specs=[SMEM] + [...]
  transfers between devices with their start and end apart: 3 -> 3, of which waited for: 3 -> 3; matrix products, arithmetic and copies ran while one was open for 1% -> 1% of each run, Pallas kernels for 6% -> 7%
where the time goes in v5:
time: 58 us; the launch traced here: 57.7 us
  starting transfers between devices  29 us (50%)
  waiting for transfers between devices  15.5 us (27%)
  Pallas kernels  9.46 us (16%)
  local copies, waits for them, and re-layouts  2.96 us (5%)
  between operations  0.73 us (1%)
    all_to_all x1, starting transfers between devices, on_device(): lax.all_to_all(sent, 'chan', split_axis=0, concat_axis=0, tiled=True)  19.3 us
    all_to_all x1, waiting for transfers between devices, on_device(): lax.all_to_all(sent, 'chan', split_axis=0, concat_axis=0, tiled=True)  12.3 us
    ppermute x1, starting transfers between devices, on_device(): other = lax.ppermute(own, 'pix', [(0, 1), (1, 0), (2, 3), (3, 2)])  5.39 us
    ppermute x1, starting transfers between devices, on_device(): got = lax.ppermute(send, 'pix', [(0, 2), (2, 0), (1, 3), (3, 1)])  4.35 us
    pallas_call x1, Pallas kernels, steering(): pl.pallas_call(steering_kernel, out_shape=(out,) * 4, in_specs=[SMEM] + [...  3.35 us
    unnamed x10, local copies, waits for them, and re-layouts  2.69 us
    pallas_call x1, Pallas kernels, filter_bank(): pl.pallas_call(filter_kernel, out_shape=jax.ShapeDtypeStruct((rows, LANES...  2.65 us
    ppermute x1, waiting for transfers between devices, on_device(): got = lax.ppermute(send, 'pix', [(0, 2), (2, 0), (1, 3), (3, 1)])  1.94 us
  transfers between devices with their start and end apart: 3, of which 3 were waited for; matrix products, arithmetic and copies ran while one was open for 1% of the time, Pallas kernels for 7%

profile of v5, /device:TPU:1, one launch (start us, length us, event | category | flops | bytes accessed | tf_op | source)
XLA Modules:
  0.0 57.7 jit_solution(15238861752467061503)
XLA Ops:
  0.6 2.6 %filter_bank.1 = bf16[2304,128]{1,0:T(8,128)(2,1)} custom-call(bf16[2,512,256]{2,1,0:T(8,128)(2,1)} %v_hbm.1, f32[4,128]{1,0:T(4,128)} %taps_hbm.1, bf16[256,256]{1,0:T(8,128)(2,1)} %constant.24.dft_hbm), custom_call_target="tpu_custom_call" | custom-call | flops 134217728 | bytes 1048576 | tf_op jit(solution)/shard_map/filter_bank/pallas_call | solution.py:106
  3.3 19.3 %all-to-all-start = ((bf16[128,9,2,128]{3,2,1,0:T(2,128)(2,1)}), bf16[128,9,2,128]{3,2,1,0:T(2,128)(2,1)S(1)}, u32[]{:S(2)}, u32[]{:S(2)}) async-start(bf16[128,9,2,128]{3,2,1,0:T(2,128)(2,1)} %bitcast.15), calls=%async_computation | async-start | bytes 1179648 | tf_op jit(solution)/shard_map/all_to_all | solution.py:390
  22.6 0.0 copy-start.3
  22.6 0.7 %copy-done.3 = s32[256]{0:T(256)S(1)} copy-done((s32[256]{0:T(256)S(1)}, s32[256]{0:T(256)}, u32[]{:S(2)}) %copy-start.3) | copy-done | bytes 1048
  23.3 0.1 reshape.18
  23.4 0.0 copy-start.1
  23.4 0.1 copy.10
  23.5 0.0 copy-start.2
  23.5 0.7 %copy-done.2 = s32[64]{0:T(128)S(1)} copy-done((s32[64]{0:T(128)S(1)}, s32[64]{0:T(128)}, u32[]{:S(2)}) %copy-start.2) | copy-done | bytes 280
  24.2 0.1 fusion
  24.2 0.0 copy-start.4
  24.2 0.7 %copy-done.4 = s32[64]{0:T(128)S(1)} copy-done((s32[64]{0:T(128)S(1)}, s32[64]{0:T(128)}, u32[]{:S(2)}) %copy-start.4) | copy-done | bytes 280
  24.9 0.1 add_bitcast_fusion
  25.0 0.0 copy-start
  25.0 0.0 copy-done.1
  25.0 0.7 %copy-done = s32[256]{0:T(256)S(1)} copy-done((s32[256]{0:T(256)S(1)}, s32[256]{0:T(256)}, u32[]{:S(2)}) %copy-start) | copy-done | bytes 1048
  25.7 3.3 %steering.1 = (bf16[256,1024]{1,0:T(8,128)(2,1)S(1)}, bf16[256,1024]{1,0:T(8,128)(2,1)S(1)}, bf16[256,1024]{1,0:T(8,128)(2,1)S(1)}, bf16[256,1024]{1,0:T(8,128)(2,1)S(1)}) custom-call(s32[1]{0:T(128)} %bitcast.4.chan_ref, s32[1,256]{1,0:T(1,128)S(1)} %bitcast.13, s32[1,256]{1,0:T(1,128)S(1)} %bitcast.14, s32[1,128]{1,0:T(1,128)S(1)} %get-tuple-element.16.l_ref, ...), custom_call_target="tpu_custom_call" | custom-call | flops 3145728 | bytes 2097152 | tf_op jit(solution)/shard_map/steering/pallas_call | solution.py:155
  29.0 12.3 %all-to-all-done = bf16[128,9,2,128]{3,2,1,0:T(2,128)(2,1)S(1)} async-done(((bf16[128,9,2,128]{3,2,1,0:T(2,128)(2,1)}), bf16[128,9,2,128]{3,2,1,0:T(2,128)(2,1)S(1)}, u32[]{:S(2)}, u32[]{:S(2)}) %all-to-all-start) | async-done | bytes 589856 | tf_op jit(solution)/shard_map/all_to_all | solution.py:390
  41.3 0.8 %gram.1.own_ref = bf16[256,640]{1,0:T(8,128)(2,1)S(1)} custom-call(bf16[2304,128]{1,0:T(8,128)(2,1)S(1)} %bitcast.11, s32[1,256]{1,0:T(1,128)S(1)} %bitcast.12, bf16[256,1024]{1,0:T(8,128)(2,1)S(1)} %get-tuple-element.8.after_ref.cos_ref), custom_call_target="tpu_custom_call" | custom-call | flops 402653184 | bytes 1048576 | tf_op jit(solution)/shard_map/gram/pallas_call | solution.py:208
  42.1 5.4 %collective-permute-start = (bf16[256,640]{1,0:T(8,128)(2,1)S(1)}, bf16[256,640]{1,0:T(8,128)(2,1)S(1)}, u32[]{:S(2)}, u32[]{:S(2)}) collective-permute-start(bf16[256,640]{1,0:T(8,128)(2,1)S(1)} %gram.1.own_ref), channel_id=1, source_target_pairs={{0,1},{1,0},{2,3},{3,2},{4,5},{5,4},{6,7},{7,6},{8,9},{9,8},{10,11... | collective-permute-start | bytes 983048 | tf_op jit(solution)/shard_map/ppermute | solution.py:410
  47.5 1.2 %collective-permute-done.other_ref = bf16[256,640]{1,0:T(8,128)(2,1)S(1)} collective-permute-done((bf16[256,640]{1,0:T(8,128)(2,1)S(1)}, bf16[256,640]{1,0:T(8,128)(2,1)S(1)}, u32[]{:S(2)}, u32[]{:S(2)}) %collective-permute-start) | collective-permute-done | bytes 327712 | tf_op jit(solution)/shard_map/ppermute | solution.py:410
  48.8 0.9 %send_part.1.after_ref = bf16[176,256]{1,0:T(8,128)(2,1)S(1)} custom-call(bf16[256,640]{1,0:T(8,128)(2,1)S(1)} %gram.1.own_ref, bf16[256,640]{1,0:T(8,128)(2,1)S(1)} %collective-permute-done.other_ref, bf16[256,1024]{1,0:T(8,128)(2,1)S(1)} %get-tuple-element.10.cos_ref, bf16[256,1024]{1,0:T(8,128)(2,1)S(1)} %get-tuple-element.11.sin_ref), custom_call_target="tpu_custom_call" | custom-call | flops 402653184 | bytes 1048576 | tf_op jit(solution)/shard_map/send_part/pallas_call | solution.py:310
  49.6 4.3 %collective-permute-start.1 = (bf16[176,256]{1,0:T(8,128)(2,1)S(1)}, bf16[176,256]{1,0:T(8,128)(2,1)S(1)}, u32[]{:S(2)}, u32[]{:S(2)}) collective-permute-start(bf16[176,256]{1,0:T(8,128)(2,1)S(1)} %send_part.1.after_ref), channel_id=1, source_target_pairs={{0,2},{2,0},{1,3},{3,1},{4,6},{6,4},{5,7},{7,5},{8,10},{10,8},{9,1... | collective-permute-start | bytes 270344 | tf_op jit(solution)/shard_map/ppermute | solution.py:413
  54.0 0.9 %keep_part.1 = (f32[2,64,256]{2,1,0:T(8,128)S(1)}, f32[44,256]{1,0:T(8,128)S(1)}) custom-call(bf16[256,640]{1,0:T(8,128)(2,1)S(1)} %gram.1.own_ref, bf16[256,640]{1,0:T(8,128)(2,1)S(1)} %collective-permute-done.other_ref, bf16[256,1024]{1,0:T(8,128)(2,1)S(1)} %get-tuple-element.8.after_ref.cos_ref, bf16[256,1024]{1,0:T(8,128)(2,1)S(1)} %get-tuple-element.9.sin_ref, ...), custom_call_target="tpu_custom_call" | custom-call | flops 402653184 | bytes 1048576 | tf_op jit(solution)/shard_map/keep_part/pallas_call | solution.py:323
  54.9 1.9 %collective-permute-done.1.refs_2_ = bf16[176,256]{1,0:T(8,128)(2,1)S(1)} collective-permute-done((bf16[176,256]{1,0:T(8,128)(2,1)S(1)}, bf16[176,256]{1,0:T(8,128)(2,1)S(1)}, u32[]{:S(2)}, u32[]{:S(2)}) %collective-permute-start.1) | collective-permute-done | bytes 90144 | tf_op jit(solution)/shard_map/ppermute | solution.py:413
  56.8 0.9 %finish.1 = (f32[1,2,64,256]{3,2,1,0:T(8,128)}, f32[1,1024]{1,0:T(1,128)}) custom-call(f32[2,64,256]{2,1,0:T(8,128)S(1)} %get-tuple-element.12.refs_0_, f32[44,256]{1,0:T(8,128)S(1)} %get-tuple-element.13.refs_1_, bf16[176,256]{1,0:T(8,128)(2,1)S(1)} %collective-permute-done.1.refs_2_), custom_call_target="tpu_custom_call" | custom-call | flops 1048576 | bytes 262144 | tf_op jit(solution)/shard_map/finish/pallas_call | solution.py:368
  (1 shorter events, 0.0 us)
Async XLA Ops:
  3.3 38.1 %all-to-all-start = ((bf16[128,9,2,128]{3,2,1,0:T(2,128)(2,1)}), bf16[128,9,2,128]{3,2,1,0:T(2,128)(2,1)S(1)}, u32[]{:S(2)}, u32[]{:S(2)}) async-start(bf16[128,9,2,128]{3,2,1,0:T(2,128)(2,1)} %bitcast.15), calls=%async_computation | async-start | bytes 1179648 | tf_op jit(solution)/shard_map/all_to_all | solution.py:390
  22.6 0.7 %copy-start.3 = (s32[256]{0:T(256)S(1)}, s32[256]{0:T(256)}, u32[]{:S(2)}) copy-start(s32[256]{0:T(256)} %param.10) | copy-start | bytes 3076
  23.4 1.6 %copy-start.1 = (s32[256]{0:T(256)S(1)}, s32[256]{0:T(256)}, u32[]{:S(2)}) copy-start(s32[256]{0:T(256)} %param.12) | copy-start | bytes 3076
  23.5 0.7 %copy-start.2 = (s32[64]{0:T(128)S(1)}, s32[64]{0:T(128)}, u32[]{:S(2)}) copy-start(s32[64]{0:T(128)} %param.13) | copy-start | bytes 772
  24.2 0.7 %copy-start.4 = (s32[64]{0:T(128)S(1)}, s32[64]{0:T(128)}, u32[]{:S(2)}) copy-start(s32[64]{0:T(128)} %param.14) | copy-start | bytes 772
  25.0 0.7 %copy-start = (s32[256]{0:T(256)S(1)}, s32[256]{0:T(256)}, u32[]{:S(2)}) copy-start(s32[256]{0:T(256)} %param.11) | copy-start | bytes 3076
  42.1 6.6 %collective-permute-start = (bf16[256,640]{1,0:T(8,128)(2,1)S(1)}, bf16[256,640]{1,0:T(8,128)(2,1)S(1)}, u32[]{:S(2)}, u32[]{:S(2)}) collective-permute-start(bf16[256,640]{1,0:T(8,128)(2,1)S(1)} %gram.1.own_ref), channel_id=1, source_target_pairs={{0,1},{1,0},{2,3},{3,2},{4,5},{5,4},{6,7},{7,6},{8,9},{9,8},{10,11... | collective-permute-start | bytes 983048 | tf_op jit(solution)/shard_map/ppermute | solution.py:410
  49.6 7.2 %collective-permute-start.1 = (bf16[176,256]{1,0:T(8,128)(2,1)S(1)}, bf16[176,256]{1,0:T(8,128)(2,1)S(1)}, u32[]{:S(2)}, u32[]{:S(2)}) collective-permute-start(bf16[176,256]{1,0:T(8,128)(2,1)S(1)} %send_part.1.after_ref), channel_id=1, source_target_pairs={{0,2},{2,0},{1,3},{3,1},{4,6},{6,4},{5,7},{7,5},{8,10},{10,8},{9,1... | collective-permute-start | bytes 270344 | tf_op jit(solution)/shard_map/ppermute | solution.py:413

commit v6 on v5

--- a/solution.py
+++ b/solution.py
@@ -13,6 +13,7 @@
 GRID = 1024
 LANES = 128
 STATIONS = 256
+BACKWARDS = list(range(POINTS))[::-1]
 EDGE = 8
 ROWS = 18
 
@@ -29,6 +30,7 @@
     angle = np.mod(counter[:, None] * counter[None, :], points) * (2.0 * math.pi / points)
     cosine, sine = np.cos(angle), np.sin(angle)
     table = np.block([[cosine, sine], [-sine, cosine]]) * points ** (-0.5)
+    table = table.reshape(2, points, 2 * points)[:, ::-1].reshape(2 * points, 2 * points)
     return jnp.asarray(table, dtype=F32).astype(BF16)
 
 
@@ -387,7 +389,9 @@
     across = jnp.where(pix < 2, pix + 2, pix - 2)
     rows_l = pixel_l.shape[0] // pix_count
     sent = filter_bank(voltages, fir_taps).reshape(POINTS, ROWS // 2, 2, LANES)
-    received = lax.all_to_all(sent, "chan", split_axis=0, concat_axis=0, tiled=True)
+    received = lax.all_to_all(
+        sent, "chan", split_axis=0, concat_axis=0, tiled=True, axis_index_groups=[BACKWARDS]
+    )
 
     block_l = jnp.concatenate(
         [
@@ -405,7 +409,7 @@
         jnp.concatenate([pixel_m, pixel_m])[None],
         pixels,
     )
-    station_row = station_of_slot.reshape(POINTS, 2).T.reshape(1, STATIONS)
+    station_row = station_of_slot.reshape(POINTS, 2)[::-1].T.reshape(1, STATIONS)
     own = gram(received.reshape(-1, LANES), station_row, here_cos)
     other = lax.ppermute(own, "pix", [(0, 1), (1, 0), (2, 3), (3, 2)])
     count = STATIONS // pix_count

time: 58 us -> 53.8 us (0.928); the launches traced: 57.7 us -> 52.8 us
  waiting for transfers between devices: 15.5 us -> 10.3 us
    all_to_all x1, waiting for transfers between devices: 12.3 us -> 7.49 us  [on_device(): lax.all_to_all(sent, 'chan', split_axis=0, concat_axis=0, tiled=True, axi...]
  transfers between devices with their start and end apart: 3 -> 3, of which waited for: 3 -> 3; matrix products, arithmetic and copies ran while one was open for 1% -> 1% of each run, Pallas kernels for 7% -> 8%
where the time goes in v6:
time: 53.8 us; the launch traced here: 52.8 us
  starting transfers between devices  29.3 us (54%)
  waiting for transfers between devices  10.3 us (19%)
  Pallas kernels  9.44 us (18%)
  local copies, waits for them, and re-layouts  2.97 us (6%)
  between operations  0.73 us (1%)
    all_to_all x1, starting transfers between devices, on_device(): lax.all_to_all(sent, 'chan', split_axis=0, concat_axis=0, tiled=True, axi...  19.5 us
    all_to_all x1, waiting for transfers between devices, on_device(): lax.all_to_all(sent, 'chan', split_axis=0, concat_axis=0, tiled=True, axi...  7.49 us
    ppermute x1, starting transfers between devices, on_device(): other = lax.ppermute(own, 'pix', [(0, 1), (1, 0), (2, 3), (3, 2)])  5.14 us
    ppermute x1, starting transfers between devices, on_device(): got = lax.ppermute(send, 'pix', [(0, 2), (2, 0), (1, 3), (3, 1)])  4.68 us
    pallas_call x1, Pallas kernels, steering(): pl.pallas_call(steering_kernel, out_shape=(out,) * 4, in_specs=[SMEM] + [...  3.35 us
    unnamed x10, local copies, waits for them, and re-layouts  2.69 us
    pallas_call x1, Pallas kernels, filter_bank(): pl.pallas_call(filter_kernel, out_shape=jax.ShapeDtypeStruct((rows, LANES...  2.65 us
    ppermute x1, waiting for transfers between devices, on_device(): got = lax.ppermute(send, 'pix', [(0, 2), (2, 0), (1, 3), (3, 1)])  1.59 us
  transfers between devices with their start and end apart: 3, of which 3 were waited for; matrix products, arithmetic and copies ran while one was open for 1% of the time, Pallas kernels for 8%

profile of v6, /device:TPU:1, one launch (start us, length us, event | category | flops | bytes accessed | tf_op | source)
XLA Modules:
  0.0 52.8 jit_solution(12963360176900329646)
XLA Ops:
  0.6 2.6 %filter_bank.1 = bf16[2304,128]{1,0:T(8,128)(2,1)} custom-call(bf16[2,512,256]{2,1,0:T(8,128)(2,1)} %v_hbm.1, f32[4,128]{1,0:T(4,128)} %taps_hbm.1, bf16[256,256]{1,0:T(8,128)(2,1)} %constant.24.dft_hbm), custom_call_target="tpu_custom_call" | custom-call | flops 134217728 | bytes 1048576 | tf_op jit(solution)/shard_map/filter_bank/pallas_call | solution.py:108
  3.3 19.5 %all-to-all-start = ((bf16[128,9,2,128]{3,2,1,0:T(2,128)(2,1)}), bf16[128,9,2,128]{3,2,1,0:T(2,128)(2,1)S(1)}, u32[]{:S(2)}, u32[]{:S(2)}) async-start(bf16[128,9,2,128]{3,2,1,0:T(2,128)(2,1)} %bitcast.15), calls=%async_computation | async-start | bytes 1179648 | tf_op jit(solution)/shard_map/all_to_all | solution.py:392
  22.8 0.0 copy-start.3
  22.8 0.7 %copy-done.3 = s32[256]{0:T(256)S(1)} copy-done((s32[256]{0:T(256)S(1)}, s32[256]{0:T(256)}, u32[]{:S(2)}) %copy-start.3) | copy-done | bytes 1048
  23.4 0.1 reshape.18
  23.6 0.0 copy-start.1
  23.6 0.1 copy.10
  23.7 0.0 copy-start.2
  23.7 0.7 %copy-done.2 = s32[64]{0:T(128)S(1)} copy-done((s32[64]{0:T(128)S(1)}, s32[64]{0:T(128)}, u32[]{:S(2)}) %copy-start.2) | copy-done | bytes 280
  24.4 0.1 fusion
  24.4 0.0 copy-start.4
  24.4 0.7 %copy-done.4 = s32[64]{0:T(128)S(1)} copy-done((s32[64]{0:T(128)S(1)}, s32[64]{0:T(128)}, u32[]{:S(2)}) %copy-start.4) | copy-done | bytes 280
  25.1 0.1 add_bitcast_fusion
  25.2 0.0 copy-start
  25.2 0.0 copy-done.1
  25.2 0.7 %copy-done = s32[256]{0:T(256)S(1)} copy-done((s32[256]{0:T(256)S(1)}, s32[256]{0:T(256)}, u32[]{:S(2)}) %copy-start) | copy-done | bytes 1048
  25.8 3.3 %steering.1 = (bf16[256,1024]{1,0:T(8,128)(2,1)S(1)}, bf16[256,1024]{1,0:T(8,128)(2,1)S(1)}, bf16[256,1024]{1,0:T(8,128)(2,1)S(1)}, bf16[256,1024]{1,0:T(8,128)(2,1)S(1)}) custom-call(s32[1]{0:T(128)} %bitcast.4.chan_ref, s32[1,256]{1,0:T(1,128)S(1)} %bitcast.13, s32[1,256]{1,0:T(1,128)S(1)} %bitcast.14, s32[1,128]{1,0:T(1,128)S(1)} %get-tuple-element.16.l_ref, ...), custom_call_target="tpu_custom_call" | custom-call | flops 3145728 | bytes 2097152 | tf_op jit(solution)/shard_map/steering/pallas_call | solution.py:157
  29.2 7.5 %all-to-all-done = bf16[128,9,2,128]{3,2,1,0:T(2,128)(2,1)S(1)} async-done(((bf16[128,9,2,128]{3,2,1,0:T(2,128)(2,1)}), bf16[128,9,2,128]{3,2,1,0:T(2,128)(2,1)S(1)}, u32[]{:S(2)}, u32[]{:S(2)}) %all-to-all-start) | async-done | bytes 589856 | tf_op jit(solution)/shard_map/all_to_all | solution.py:392
  36.7 0.8 %gram.1.own_ref = bf16[256,640]{1,0:T(8,128)(2,1)S(1)} custom-call(bf16[2304,128]{1,0:T(8,128)(2,1)S(1)} %bitcast.11, s32[1,256]{1,0:T(1,128)S(1)} %bitcast.12, bf16[256,1024]{1,0:T(8,128)(2,1)S(1)} %get-tuple-element.8.after_ref.cos_ref), custom_call_target="tpu_custom_call" | custom-call | flops 402653184 | bytes 1048576 | tf_op jit(solution)/shard_map/gram/pallas_call | solution.py:210
  37.5 5.1 %collective-permute-start = (bf16[256,640]{1,0:T(8,128)(2,1)S(1)}, bf16[256,640]{1,0:T(8,128)(2,1)S(1)}, u32[]{:S(2)}, u32[]{:S(2)}) collective-permute-start(bf16[256,640]{1,0:T(8,128)(2,1)S(1)} %gram.1.own_ref), channel_id=1, source_target_pairs={{0,1},{1,0},{2,3},{3,2},{4,5},{5,4},{6,7},{7,6},{8,9},{9,8},{10,11... | collective-permute-start | bytes 983048 | tf_op jit(solution)/shard_map/ppermute | solution.py:414
  42.6 1.2 %collective-permute-done.other_ref = bf16[256,640]{1,0:T(8,128)(2,1)S(1)} collective-permute-done((bf16[256,640]{1,0:T(8,128)(2,1)S(1)}, bf16[256,640]{1,0:T(8,128)(2,1)S(1)}, u32[]{:S(2)}, u32[]{:S(2)}) %collective-permute-start) | collective-permute-done | bytes 327712 | tf_op jit(solution)/shard_map/ppermute | solution.py:414
  43.9 0.9 %send_part.1.after_ref = bf16[176,256]{1,0:T(8,128)(2,1)S(1)} custom-call(bf16[256,640]{1,0:T(8,128)(2,1)S(1)} %gram.1.own_ref, bf16[256,640]{1,0:T(8,128)(2,1)S(1)} %collective-permute-done.other_ref, bf16[256,1024]{1,0:T(8,128)(2,1)S(1)} %get-tuple-element.10.cos_ref, bf16[256,1024]{1,0:T(8,128)(2,1)S(1)} %get-tuple-element.11.sin_ref), custom_call_target="tpu_custom_call" | custom-call | flops 402653184 | bytes 1048576 | tf_op jit(solution)/shard_map/send_part/pallas_call | solution.py:312
  44.7 4.7 %collective-permute-start.1 = (bf16[176,256]{1,0:T(8,128)(2,1)S(1)}, bf16[176,256]{1,0:T(8,128)(2,1)S(1)}, u32[]{:S(2)}, u32[]{:S(2)}) collective-permute-start(bf16[176,256]{1,0:T(8,128)(2,1)S(1)} %send_part.1.after_ref), channel_id=1, source_target_pairs={{0,2},{2,0},{1,3},{3,1},{4,6},{6,4},{5,7},{7,5},{8,10},{10,8},{9,1... | collective-permute-start | bytes 270344 | tf_op jit(solution)/shard_map/ppermute | solution.py:417
  49.4 0.9 %keep_part.1 = (f32[2,64,256]{2,1,0:T(8,128)S(1)}, f32[44,256]{1,0:T(8,128)S(1)}) custom-call(bf16[256,640]{1,0:T(8,128)(2,1)S(1)} %gram.1.own_ref, bf16[256,640]{1,0:T(8,128)(2,1)S(1)} %collective-permute-done.other_ref, bf16[256,1024]{1,0:T(8,128)(2,1)S(1)} %get-tuple-element.8.after_ref.cos_ref, bf16[256,1024]{1,0:T(8,128)(2,1)S(1)} %get-tuple-element.9.sin_ref, ...), custom_call_target="tpu_custom_call" | custom-call | flops 402653184 | bytes 1048576 | tf_op jit(solution)/shard_map/keep_part/pallas_call | solution.py:325
  50.3 1.6 %collective-permute-done.1.refs_2_ = bf16[176,256]{1,0:T(8,128)(2,1)S(1)} collective-permute-done((bf16[176,256]{1,0:T(8,128)(2,1)S(1)}, bf16[176,256]{1,0:T(8,128)(2,1)S(1)}, u32[]{:S(2)}, u32[]{:S(2)}) %collective-permute-start.1) | collective-permute-done | bytes 90144 | tf_op jit(solution)/shard_map/ppermute | solution.py:417
  51.9 0.9 %finish.1 = (f32[1,2,64,256]{3,2,1,0:T(8,128)}, f32[1,1024]{1,0:T(1,128)}) custom-call(f32[2,64,256]{2,1,0:T(8,128)S(1)} %get-tuple-element.12.refs_0_, f32[44,256]{1,0:T(8,128)S(1)} %get-tuple-element.13.refs_1_, bf16[176,256]{1,0:T(8,128)(2,1)S(1)} %collective-permute-done.1.refs_2_), custom_call_target="tpu_custom_call" | custom-call | flops 1048576 | bytes 262144 | tf_op jit(solution)/shard_map/finish/pallas_call | solution.py:370
  (2 shorter events, 0.0 us)
Async XLA Ops:
  3.3 33.4 %all-to-all-start = ((bf16[128,9,2,128]{3,2,1,0:T(2,128)(2,1)}), bf16[128,9,2,128]{3,2,1,0:T(2,128)(2,1)S(1)}, u32[]{:S(2)}, u32[]{:S(2)}) async-start(bf16[128,9,2,128]{3,2,1,0:T(2,128)(2,1)} %bitcast.15), calls=%async_computation | async-start | bytes 1179648 | tf_op jit(solution)/shard_map/all_to_all | solution.py:392
  22.8 0.7 %copy-start.3 = (s32[256]{0:T(256)S(1)}, s32[256]{0:T(256)}, u32[]{:S(2)}) copy-start(s32[256]{0:T(256)} %param.10) | copy-start | bytes 3076
  23.6 1.6 %copy-start.1 = (s32[256]{0:T(256)S(1)}, s32[256]{0:T(256)}, u32[]{:S(2)}) copy-start(s32[256]{0:T(256)} %param.12) | copy-start | bytes 3076
  23.7 0.7 %copy-start.2 = (s32[64]{0:T(128)S(1)}, s32[64]{0:T(128)}, u32[]{:S(2)}) copy-start(s32[64]{0:T(128)} %param.13) | copy-start | bytes 772
  24.4 0.7 %copy-start.4 = (s32[64]{0:T(128)S(1)}, s32[64]{0:T(128)}, u32[]{:S(2)}) copy-start(s32[64]{0:T(128)} %param.14) | copy-start | bytes 772
  25.2 0.7 %copy-start = (s32[256]{0:T(256)S(1)}, s32[256]{0:T(256)}, u32[]{:S(2)}) copy-start(s32[256]{0:T(256)} %param.11) | copy-start | bytes 3076
  37.5 6.4 %collective-permute-start = (bf16[256,640]{1,0:T(8,128)(2,1)S(1)}, bf16[256,640]{1,0:T(8,128)(2,1)S(1)}, u32[]{:S(2)}, u32[]{:S(2)}) collective-permute-start(bf16[256,640]{1,0:T(8,128)(2,1)S(1)} %gram.1.own_ref), channel_id=1, source_target_pairs={{0,1},{1,0},{2,3},{3,2},{4,5},{5,4},{6,7},{7,6},{8,9},{9,8},{10,11... | collective-permute-start | bytes 983048 | tf_op jit(solution)/shard_map/ppermute | solution.py:414
  44.7 7.2 %collective-permute-start.1 = (bf16[176,256]{1,0:T(8,128)(2,1)S(1)}, bf16[176,256]{1,0:T(8,128)(2,1)S(1)}, u32[]{:S(2)}, u32[]{:S(2)}) collective-permute-start(bf16[176,256]{1,0:T(8,128)(2,1)S(1)} %send_part.1.after_ref), channel_id=1, source_target_pairs={{0,2},{2,0},{1,3},{3,1},{4,6},{6,4},{5,7},{7,5},{8,10},{10,8},{9,1... | collective-permute-start | bytes 270344 | tf_op jit(solution)/shard_map/ppermute | solution.py:417

commit v7 on v6

--- a/solution.py
+++ b/solution.py
@@ -197,10 +197,12 @@
     ordered = jnp.dot(select, slots[...], preferred_element_type=F32).astype(BF16)
     half = 4 * LANES
     spectra = ordered[:, : 2 * half]
-    turned = jnp.concatenate([ordered[:, half : 2 * half], -ordered[:, :half]], axis=1)
     contract = (((1,), (1,)), ((), ()))
+    cross = lax.dot_general(
+        ordered[:, half : 2 * half], ordered[:, :half], contract, preferred_element_type=F32
+    )
     real = lax.dot_general(spectra, spectra, contract, preferred_element_type=F32)
-    imag = lax.dot_general(turned, spectra, contract, preferred_element_type=F32)
+    imag = cross - cross.T
     out_ref[:, 0:STATIONS] = real.astype(BF16)
     out_ref[:, STATIONS : 2 * STATIONS] = imag.astype(BF16)
     out_ref[:, 2 * STATIONS :] = ordered[:, 2 * half :]

time: 53.8 us -> 53.8 us (level)
  no operation moved by 1% of the time
where the time goes in v7:
time: 53.8 us; the launch traced here: 52.8 us
  starting transfers between devices  29.3 us (54%)
  waiting for transfers between devices  10.3 us (19%)
  Pallas kernels  9.42 us (18%)
  local copies, waits for them, and re-layouts  2.97 us (6%)
  between operations  0.73 us (1%)
    all_to_all x1, starting transfers between devices, on_device(): lax.all_to_all(sent, 'chan', split_axis=0, concat_axis=0, tiled=True, axi...  19.5 us
    all_to_all x1, waiting for transfers between devices, on_device(): lax.all_to_all(sent, 'chan', split_axis=0, concat_axis=0, tiled=True, axi...  7.49 us
    ppermute x1, starting transfers between devices, on_device(): other = lax.ppermute(own, 'pix', [(0, 1), (1, 0), (2, 3), (3, 2)])  5.15 us
    ppermute x1, starting transfers between devices, on_device(): got = lax.ppermute(send, 'pix', [(0, 2), (2, 0), (1, 3), (3, 1)])  4.66 us
    pallas_call x1, Pallas kernels, steering(): pl.pallas_call(steering_kernel, out_shape=(out,) * 4, in_specs=[SMEM] + [...  3.35 us
    unnamed x10, local copies, waits for them, and re-layouts  2.69 us
    pallas_call x1, Pallas kernels, filter_bank(): pl.pallas_call(filter_kernel, out_shape=jax.ShapeDtypeStruct((rows, LANES...  2.65 us
    ppermute x1, waiting for transfers between devices, on_device(): got = lax.ppermute(send, 'pix', [(0, 2), (2, 0), (1, 3), (3, 1)])  1.61 us
  transfers between devices with their start and end apart: 3, of which 3 were waited for; matrix products, arithmetic and copies ran while one was open for 1% of the time, Pallas kernels for 8%

profile of v7, /device:TPU:1, one launch (start us, length us, event | category | flops | bytes accessed | tf_op | source)
XLA Modules:
  0.0 52.8 jit_solution(17629337224279235450)
XLA Ops:
  0.6 2.6 %filter_bank.1 = bf16[2304,128]{1,0:T(8,128)(2,1)} custom-call(bf16[2,512,256]{2,1,0:T(8,128)(2,1)} %v_hbm.1, f32[4,128]{1,0:T(4,128)} %taps_hbm.1, bf16[256,256]{1,0:T(8,128)(2,1)} %constant.24.dft_hbm), custom_call_target="tpu_custom_call" | custom-call | flops 134217728 | bytes 1048576 | tf_op jit(solution)/shard_map/filter_bank/pallas_call | solution.py:108
  3.3 19.5 %all-to-all-start = ((bf16[128,9,2,128]{3,2,1,0:T(2,128)(2,1)}), bf16[128,9,2,128]{3,2,1,0:T(2,128)(2,1)S(1)}, u32[]{:S(2)}, u32[]{:S(2)}) async-start(bf16[128,9,2,128]{3,2,1,0:T(2,128)(2,1)} %bitcast.15), calls=%async_computation | async-start | bytes 1179648 | tf_op jit(solution)/shard_map/all_to_all | solution.py:394
  22.8 0.0 copy-start.3
  22.8 0.7 %copy-done.3 = s32[256]{0:T(256)S(1)} copy-done((s32[256]{0:T(256)S(1)}, s32[256]{0:T(256)}, u32[]{:S(2)}) %copy-start.3) | copy-done | bytes 1048
  23.4 0.1 reshape.18
  23.6 0.0 copy-start.1
  23.6 0.1 copy.10
  23.7 0.0 copy-start.2
  23.7 0.7 %copy-done.2 = s32[64]{0:T(128)S(1)} copy-done((s32[64]{0:T(128)S(1)}, s32[64]{0:T(128)}, u32[]{:S(2)}) %copy-start.2) | copy-done | bytes 280
  24.4 0.1 fusion
  24.4 0.0 copy-start.4
  24.4 0.7 %copy-done.4 = s32[64]{0:T(128)S(1)} copy-done((s32[64]{0:T(128)S(1)}, s32[64]{0:T(128)}, u32[]{:S(2)}) %copy-start.4) | copy-done | bytes 280
  25.1 0.1 add_bitcast_fusion
  25.2 0.0 copy-start
  25.2 0.0 copy-done.1
  25.2 0.7 %copy-done = s32[256]{0:T(256)S(1)} copy-done((s32[256]{0:T(256)S(1)}, s32[256]{0:T(256)}, u32[]{:S(2)}) %copy-start) | copy-done | bytes 1048
  25.8 3.3 %steering.1 = (bf16[256,1024]{1,0:T(8,128)(2,1)S(1)}, bf16[256,1024]{1,0:T(8,128)(2,1)S(1)}, bf16[256,1024]{1,0:T(8,128)(2,1)S(1)}, bf16[256,1024]{1,0:T(8,128)(2,1)S(1)}) custom-call(s32[1]{0:T(128)} %bitcast.4.chan_ref, s32[1,256]{1,0:T(1,128)S(1)} %bitcast.13, s32[1,256]{1,0:T(1,128)S(1)} %bitcast.14, s32[1,128]{1,0:T(1,128)S(1)} %get-tuple-element.16.l_ref, ...), custom_call_target="tpu_custom_call" | custom-call | flops 3145728 | bytes 2097152 | tf_op jit(solution)/shard_map/steering/pallas_call | solution.py:157
  29.2 7.5 %all-to-all-done = bf16[128,9,2,128]{3,2,1,0:T(2,128)(2,1)S(1)} async-done(((bf16[128,9,2,128]{3,2,1,0:T(2,128)(2,1)}), bf16[128,9,2,128]{3,2,1,0:T(2,128)(2,1)S(1)}, u32[]{:S(2)}, u32[]{:S(2)}) %all-to-all-start) | async-done | bytes 589856 | tf_op jit(solution)/shard_map/all_to_all | solution.py:394
  36.7 0.8 %gram.1.own_ref = bf16[256,640]{1,0:T(8,128)(2,1)S(1)} custom-call(bf16[2304,128]{1,0:T(8,128)(2,1)S(1)} %bitcast.11, s32[1,256]{1,0:T(1,128)S(1)} %bitcast.12, bf16[256,1024]{1,0:T(8,128)(2,1)S(1)} %get-tuple-element.8.after_ref.cos_ref), custom_call_target="tpu_custom_call" | custom-call | flops 402653184 | bytes 1048576 | tf_op jit(solution)/shard_map/gram/pallas_call | solution.py:212
  37.5 5.1 %collective-permute-start = (bf16[256,640]{1,0:T(8,128)(2,1)S(1)}, bf16[256,640]{1,0:T(8,128)(2,1)S(1)}, u32[]{:S(2)}, u32[]{:S(2)}) collective-permute-start(bf16[256,640]{1,0:T(8,128)(2,1)S(1)} %gram.1.own_ref), channel_id=1, source_target_pairs={{0,1},{1,0},{2,3},{3,2},{4,5},{5,4},{6,7},{7,6},{8,9},{9,8},{10,11... | collective-permute-start | bytes 983048 | tf_op jit(solution)/shard_map/ppermute | solution.py:416
  42.6 1.2 %collective-permute-done.other_ref = bf16[256,640]{1,0:T(8,128)(2,1)S(1)} collective-permute-done((bf16[256,640]{1,0:T(8,128)(2,1)S(1)}, bf16[256,640]{1,0:T(8,128)(2,1)S(1)}, u32[]{:S(2)}, u32[]{:S(2)}) %collective-permute-start) | collective-permute-done | bytes 327712 | tf_op jit(solution)/shard_map/ppermute | solution.py:416
  43.8 0.9 %send_part.1.after_ref = bf16[176,256]{1,0:T(8,128)(2,1)S(1)} custom-call(bf16[256,640]{1,0:T(8,128)(2,1)S(1)} %gram.1.own_ref, bf16[256,640]{1,0:T(8,128)(2,1)S(1)} %collective-permute-done.other_ref, bf16[256,1024]{1,0:T(8,128)(2,1)S(1)} %get-tuple-element.10.cos_ref, bf16[256,1024]{1,0:T(8,128)(2,1)S(1)} %get-tuple-element.11.sin_ref), custom_call_target="tpu_custom_call" | custom-call | flops 402653184 | bytes 1048576 | tf_op jit(solution)/shard_map/send_part/pallas_call | solution.py:314
  44.7 4.7 %collective-permute-start.1 = (bf16[176,256]{1,0:T(8,128)(2,1)S(1)}, bf16[176,256]{1,0:T(8,128)(2,1)S(1)}, u32[]{:S(2)}, u32[]{:S(2)}) collective-permute-start(bf16[176,256]{1,0:T(8,128)(2,1)S(1)} %send_part.1.after_ref), channel_id=1, source_target_pairs={{0,2},{2,0},{1,3},{3,1},{4,6},{6,4},{5,7},{7,5},{8,10},{10,8},{9,1... | collective-permute-start | bytes 270344 | tf_op jit(solution)/shard_map/ppermute | solution.py:419
  49.4 0.9 %keep_part.1 = (f32[2,64,256]{2,1,0:T(8,128)S(1)}, f32[44,256]{1,0:T(8,128)S(1)}) custom-call(bf16[256,640]{1,0:T(8,128)(2,1)S(1)} %gram.1.own_ref, bf16[256,640]{1,0:T(8,128)(2,1)S(1)} %collective-permute-done.other_ref, bf16[256,1024]{1,0:T(8,128)(2,1)S(1)} %get-tuple-element.8.after_ref.cos_ref, bf16[256,1024]{1,0:T(8,128)(2,1)S(1)} %get-tuple-element.9.sin_ref, ...), custom_call_target="tpu_custom_call" | custom-call | flops 402653184 | bytes 1048576 | tf_op jit(solution)/shard_map/keep_part/pallas_call | solution.py:327
  50.3 1.6 %collective-permute-done.1.refs_2_ = bf16[176,256]{1,0:T(8,128)(2,1)S(1)} collective-permute-done((bf16[176,256]{1,0:T(8,128)(2,1)S(1)}, bf16[176,256]{1,0:T(8,128)(2,1)S(1)}, u32[]{:S(2)}, u32[]{:S(2)}) %collective-permute-start.1) | collective-permute-done | bytes 90144 | tf_op jit(solution)/shard_map/ppermute | solution.py:419
  51.9 0.9 %finish.1 = (f32[1,2,64,256]{3,2,1,0:T(8,128)}, f32[1,1024]{1,0:T(1,128)}) custom-call(f32[2,64,256]{2,1,0:T(8,128)S(1)} %get-tuple-element.12.refs_0_, f32[44,256]{1,0:T(8,128)S(1)} %get-tuple-element.13.refs_1_, bf16[176,256]{1,0:T(8,128)(2,1)S(1)} %collective-permute-done.1.refs_2_), custom_call_target="tpu_custom_call" | custom-call | flops 1048576 | bytes 262144 | tf_op jit(solution)/shard_map/finish/pallas_call | solution.py:372
  (2 shorter events, 0.0 us)
Async XLA Ops:
  3.3 33.4 %all-to-all-start = ((bf16[128,9,2,128]{3,2,1,0:T(2,128)(2,1)}), bf16[128,9,2,128]{3,2,1,0:T(2,128)(2,1)S(1)}, u32[]{:S(2)}, u32[]{:S(2)}) async-start(bf16[128,9,2,128]{3,2,1,0:T(2,128)(2,1)} %bitcast.15), calls=%async_computation | async-start | bytes 1179648 | tf_op jit(solution)/shard_map/all_to_all | solution.py:394
  22.8 0.7 %copy-start.3 = (s32[256]{0:T(256)S(1)}, s32[256]{0:T(256)}, u32[]{:S(2)}) copy-start(s32[256]{0:T(256)} %param.10) | copy-start | bytes 3076
  23.6 1.6 %copy-start.1 = (s32[256]{0:T(256)S(1)}, s32[256]{0:T(256)}, u32[]{:S(2)}) copy-start(s32[256]{0:T(256)} %param.12) | copy-start | bytes 3076
  23.7 0.7 %copy-start.2 = (s32[64]{0:T(128)S(1)}, s32[64]{0:T(128)}, u32[]{:S(2)}) copy-start(s32[64]{0:T(128)} %param.13) | copy-start | bytes 772
  24.4 0.7 %copy-start.4 = (s32[64]{0:T(128)S(1)}, s32[64]{0:T(128)}, u32[]{:S(2)}) copy-start(s32[64]{0:T(128)} %param.14) | copy-start | bytes 772
  25.2 0.7 %copy-start = (s32[256]{0:T(256)S(1)}, s32[256]{0:T(256)}, u32[]{:S(2)}) copy-start(s32[256]{0:T(256)} %param.11) | copy-start | bytes 3076
  37.5 6.4 %collective-permute-start = (bf16[256,640]{1,0:T(8,128)(2,1)S(1)}, bf16[256,640]{1,0:T(8,128)(2,1)S(1)}, u32[]{:S(2)}, u32[]{:S(2)}) collective-permute-start(bf16[256,640]{1,0:T(8,128)(2,1)S(1)} %gram.1.own_ref), channel_id=1, source_target_pairs={{0,1},{1,0},{2,3},{3,2},{4,5},{5,4},{6,7},{7,6},{8,9},{9,8},{10,11... | collective-permute-start | bytes 983048 | tf_op jit(solution)/shard_map/ppermute | solution.py:416
  44.7 7.2 %collective-permute-start.1 = (bf16[176,256]{1,0:T(8,128)(2,1)S(1)}, bf16[176,256]{1,0:T(8,128)(2,1)S(1)}, u32[]{:S(2)}, u32[]{:S(2)}) collective-permute-start(bf16[176,256]{1,0:T(8,128)(2,1)S(1)} %send_part.1.after_ref), channel_id=1, source_target_pairs={{0,2},{2,0},{1,3},{3,1},{4,6},{6,4},{5,7},{7,5},{8,10},{10,8},{9,1... | collective-permute-start | bytes 270344 | tf_op jit(solution)/shard_map/ppermute | solution.py:419

commit v8 on v7

--- a/solution.py
+++ b/solution.py
@@ -77,11 +77,10 @@
                 ext[s, half, EDGE : EDGE + spec_dev, :] = v_ref[
                     s, :, half * POINTS : (half + 1) * POINTS
                 ].astype(F32)
+        samples = filtered(s, t, step)
         if i == 0:
             copies[3].wait()
-        spectra = lax.dot_general(
-            dft_ref[...], filtered(s, t, step), contract, preferred_element_type=F32
-        )
+        spectra = lax.dot_general(dft_ref[...], samples, contract, preferred_element_type=F32)
         for r in range(2):
             for part in range(step // LANES):
                 row = s * 8 + r * 4 + t // LANES + part

time: 53.8 us -> 53.8 us (level)
  no operation moved by 1% of the time
where the time goes in v8:
time: 53.8 us; the launch traced here: 52.8 us
  starting transfers between devices  29.3 us (54%)
  waiting for transfers between devices  10.3 us (19%)
  Pallas kernels  9.45 us (18%)
  local copies, waits for them, and re-layouts  2.97 us (6%)
  between operations  0.73 us (1%)
    all_to_all x1, starting transfers between devices, on_device(): lax.all_to_all(sent, 'chan', split_axis=0, concat_axis=0, tiled=True, axi...  19.5 us
    all_to_all x1, waiting for transfers between devices, on_device(): lax.all_to_all(sent, 'chan', split_axis=0, concat_axis=0, tiled=True, axi...  7.49 us
    ppermute x1, starting transfers between devices, on_device(): other = lax.ppermute(own, 'pix', [(0, 1), (1, 0), (2, 3), (3, 2)])  5.15 us
    ppermute x1, starting transfers between devices, on_device(): got = lax.ppermute(send, 'pix', [(0, 2), (2, 0), (1, 3), (3, 1)])  4.66 us
    pallas_call x1, Pallas kernels, steering(): pl.pallas_call(steering_kernel, out_shape=(out,) * 4, in_specs=[SMEM] + [...  3.35 us
    unnamed x10, local copies, waits for them, and re-layouts  2.69 us
    pallas_call x1, Pallas kernels, filter_bank(): pl.pallas_call(filter_kernel, out_shape=jax.ShapeDtypeStruct((rows, LANES...  2.67 us
    ppermute x1, waiting for transfers between devices, on_device(): got = lax.ppermute(send, 'pix', [(0, 2), (2, 0), (1, 3), (3, 1)])  1.6 us
  transfers between devices with their start and end apart: 3, of which 3 were waited for; matrix products, arithmetic and copies ran while one was open for 1% of the time, Pallas kernels for 8%

profile of v8, /device:TPU:1, one launch (start us, length us, event | category | flops | bytes accessed | tf_op | source)
XLA Modules:
  0.0 52.8 jit_solution(5350330145776102431)
XLA Ops:
  0.6 2.7 %filter_bank.1 = bf16[2304,128]{1,0:T(8,128)(2,1)} custom-call(bf16[2,512,256]{2,1,0:T(8,128)(2,1)} %v_hbm.1, f32[4,128]{1,0:T(4,128)} %taps_hbm.1, bf16[256,256]{1,0:T(8,128)(2,1)} %constant.24.dft_hbm), custom_call_target="tpu_custom_call" | custom-call | flops 134217728 | bytes 1048576 | tf_op jit(solution)/shard_map/filter_bank/pallas_call | solution.py:107
  3.3 19.5 %all-to-all-start = ((bf16[128,9,2,128]{3,2,1,0:T(2,128)(2,1)}), bf16[128,9,2,128]{3,2,1,0:T(2,128)(2,1)S(1)}, u32[]{:S(2)}, u32[]{:S(2)}) async-start(bf16[128,9,2,128]{3,2,1,0:T(2,128)(2,1)} %bitcast.15), calls=%async_computation | async-start | bytes 1179648 | tf_op jit(solution)/shard_map/all_to_all | solution.py:393
  22.8 0.0 copy-start.3
  22.8 0.7 %copy-done.3 = s32[256]{0:T(256)S(1)} copy-done((s32[256]{0:T(256)S(1)}, s32[256]{0:T(256)}, u32[]{:S(2)}) %copy-start.3) | copy-done | bytes 1048
  23.5 0.1 reshape.18
  23.6 0.0 copy-start.1
  23.6 0.1 copy.10
  23.7 0.0 copy-start.2
  23.7 0.7 %copy-done.2 = s32[64]{0:T(128)S(1)} copy-done((s32[64]{0:T(128)S(1)}, s32[64]{0:T(128)}, u32[]{:S(2)}) %copy-start.2) | copy-done | bytes 280
  24.4 0.1 fusion
  24.5 0.0 copy-start.4
  24.5 0.7 %copy-done.4 = s32[64]{0:T(128)S(1)} copy-done((s32[64]{0:T(128)S(1)}, s32[64]{0:T(128)}, u32[]{:S(2)}) %copy-start.4) | copy-done | bytes 280
  25.1 0.1 add_bitcast_fusion
  25.2 0.0 copy-start
  25.2 0.0 copy-done.1
  25.2 0.7 %copy-done = s32[256]{0:T(256)S(1)} copy-done((s32[256]{0:T(256)S(1)}, s32[256]{0:T(256)}, u32[]{:S(2)}) %copy-start) | copy-done | bytes 1048
  25.9 3.3 %steering.1 = (bf16[256,1024]{1,0:T(8,128)(2,1)S(1)}, bf16[256,1024]{1,0:T(8,128)(2,1)S(1)}, bf16[256,1024]{1,0:T(8,128)(2,1)S(1)}, bf16[256,1024]{1,0:T(8,128)(2,1)S(1)}) custom-call(s32[1]{0:T(128)} %bitcast.4.chan_ref, s32[1,256]{1,0:T(1,128)S(1)} %bitcast.13, s32[1,256]{1,0:T(1,128)S(1)} %bitcast.14, s32[1,128]{1,0:T(1,128)S(1)} %get-tuple-element.16.l_ref, ...), custom_call_target="tpu_custom_call" | custom-call | flops 3145728 | bytes 2097152 | tf_op jit(solution)/shard_map/steering/pallas_call | solution.py:156
  29.2 7.5 %all-to-all-done = bf16[128,9,2,128]{3,2,1,0:T(2,128)(2,1)S(1)} async-done(((bf16[128,9,2,128]{3,2,1,0:T(2,128)(2,1)}), bf16[128,9,2,128]{3,2,1,0:T(2,128)(2,1)S(1)}, u32[]{:S(2)}, u32[]{:S(2)}) %all-to-all-start) | async-done | bytes 589856 | tf_op jit(solution)/shard_map/all_to_all | solution.py:393
  36.7 0.8 %gram.1.own_ref = bf16[256,640]{1,0:T(8,128)(2,1)S(1)} custom-call(bf16[2304,128]{1,0:T(8,128)(2,1)S(1)} %bitcast.11, s32[1,256]{1,0:T(1,128)S(1)} %bitcast.12, bf16[256,1024]{1,0:T(8,128)(2,1)S(1)} %get-tuple-element.8.after_ref.cos_ref), custom_call_target="tpu_custom_call" | custom-call | flops 402653184 | bytes 1048576 | tf_op jit(solution)/shard_map/gram/pallas_call | solution.py:211
  37.5 5.1 %collective-permute-start = (bf16[256,640]{1,0:T(8,128)(2,1)S(1)}, bf16[256,640]{1,0:T(8,128)(2,1)S(1)}, u32[]{:S(2)}, u32[]{:S(2)}) collective-permute-start(bf16[256,640]{1,0:T(8,128)(2,1)S(1)} %gram.1.own_ref), channel_id=1, source_target_pairs={{0,1},{1,0},{2,3},{3,2},{4,5},{5,4},{6,7},{7,6},{8,9},{9,8},{10,11... | collective-permute-start | bytes 983048 | tf_op jit(solution)/shard_map/ppermute | solution.py:415
  42.6 1.2 %collective-permute-done.other_ref = bf16[256,640]{1,0:T(8,128)(2,1)S(1)} collective-permute-done((bf16[256,640]{1,0:T(8,128)(2,1)S(1)}, bf16[256,640]{1,0:T(8,128)(2,1)S(1)}, u32[]{:S(2)}, u32[]{:S(2)}) %collective-permute-start) | collective-permute-done | bytes 327712 | tf_op jit(solution)/shard_map/ppermute | solution.py:415
  43.9 0.9 %send_part.1.after_ref = bf16[176,256]{1,0:T(8,128)(2,1)S(1)} custom-call(bf16[256,640]{1,0:T(8,128)(2,1)S(1)} %gram.1.own_ref, bf16[256,640]{1,0:T(8,128)(2,1)S(1)} %collective-permute-done.other_ref, bf16[256,1024]{1,0:T(8,128)(2,1)S(1)} %get-tuple-element.10.cos_ref, bf16[256,1024]{1,0:T(8,128)(2,1)S(1)} %get-tuple-element.11.sin_ref), custom_call_target="tpu_custom_call" | custom-call | flops 402653184 | bytes 1048576 | tf_op jit(solution)/shard_map/send_part/pallas_call | solution.py:313
  44.7 4.7 %collective-permute-start.1 = (bf16[176,256]{1,0:T(8,128)(2,1)S(1)}, bf16[176,256]{1,0:T(8,128)(2,1)S(1)}, u32[]{:S(2)}, u32[]{:S(2)}) collective-permute-start(bf16[176,256]{1,0:T(8,128)(2,1)S(1)} %send_part.1.after_ref), channel_id=1, source_target_pairs={{0,2},{2,0},{1,3},{3,1},{4,6},{6,4},{5,7},{7,5},{8,10},{10,8},{9,1... | collective-permute-start | bytes 270344 | tf_op jit(solution)/shard_map/ppermute | solution.py:418
  49.4 0.9 %keep_part.1 = (f32[2,64,256]{2,1,0:T(8,128)S(1)}, f32[44,256]{1,0:T(8,128)S(1)}) custom-call(bf16[256,640]{1,0:T(8,128)(2,1)S(1)} %gram.1.own_ref, bf16[256,640]{1,0:T(8,128)(2,1)S(1)} %collective-permute-done.other_ref, bf16[256,1024]{1,0:T(8,128)(2,1)S(1)} %get-tuple-element.8.after_ref.cos_ref, bf16[256,1024]{1,0:T(8,128)(2,1)S(1)} %get-tuple-element.9.sin_ref, ...), custom_call_target="tpu_custom_call" | custom-call | flops 402653184 | bytes 1048576 | tf_op jit(solution)/shard_map/keep_part/pallas_call | solution.py:326
  50.3 1.6 %collective-permute-done.1.refs_2_ = bf16[176,256]{1,0:T(8,128)(2,1)S(1)} collective-permute-done((bf16[176,256]{1,0:T(8,128)(2,1)S(1)}, bf16[176,256]{1,0:T(8,128)(2,1)S(1)}, u32[]{:S(2)}, u32[]{:S(2)}) %collective-permute-start.1) | collective-permute-done | bytes 90144 | tf_op jit(solution)/shard_map/ppermute | solution.py:418
  51.9 0.9 %finish.1 = (f32[1,2,64,256]{3,2,1,0:T(8,128)}, f32[1,1024]{1,0:T(1,128)}) custom-call(f32[2,64,256]{2,1,0:T(8,128)S(1)} %get-tuple-element.12.refs_0_, f32[44,256]{1,0:T(8,128)S(1)} %get-tuple-element.13.refs_1_, bf16[176,256]{1,0:T(8,128)(2,1)S(1)} %collective-permute-done.1.refs_2_), custom_call_target="tpu_custom_call" | custom-call | flops 1048576 | bytes 262144 | tf_op jit(solution)/shard_map/finish/pallas_call | solution.py:371
  (2 shorter events, 0.0 us)
Async XLA Ops:
  3.3 33.4 %all-to-all-start = ((bf16[128,9,2,128]{3,2,1,0:T(2,128)(2,1)}), bf16[128,9,2,128]{3,2,1,0:T(2,128)(2,1)S(1)}, u32[]{:S(2)}, u32[]{:S(2)}) async-start(bf16[128,9,2,128]{3,2,1,0:T(2,128)(2,1)} %bitcast.15), calls=%async_computation | async-start | bytes 1179648 | tf_op jit(solution)/shard_map/all_to_all | solution.py:393
  22.8 0.7 %copy-start.3 = (s32[256]{0:T(256)S(1)}, s32[256]{0:T(256)}, u32[]{:S(2)}) copy-start(s32[256]{0:T(256)} %param.10) | copy-start | bytes 3076
  23.6 1.6 %copy-start.1 = (s32[256]{0:T(256)S(1)}, s32[256]{0:T(256)}, u32[]{:S(2)}) copy-start(s32[256]{0:T(256)} %param.12) | copy-start | bytes 3076
  23.7 0.7 %copy-start.2 = (s32[64]{0:T(128)S(1)}, s32[64]{0:T(128)}, u32[]{:S(2)}) copy-start(s32[64]{0:T(128)} %param.13) | copy-start | bytes 772
  24.5 0.7 %copy-start.4 = (s32[64]{0:T(128)S(1)}, s32[64]{0:T(128)}, u32[]{:S(2)}) copy-start(s32[64]{0:T(128)} %param.14) | copy-start | bytes 772
  25.2 0.7 %copy-start = (s32[256]{0:T(256)S(1)}, s32[256]{0:T(256)}, u32[]{:S(2)}) copy-start(s32[256]{0:T(256)} %param.11) | copy-start | bytes 3076
  37.5 6.4 %collective-permute-start = (bf16[256,640]{1,0:T(8,128)(2,1)S(1)}, bf16[256,640]{1,0:T(8,128)(2,1)S(1)}, u32[]{:S(2)}, u32[]{:S(2)}) collective-permute-start(bf16[256,640]{1,0:T(8,128)(2,1)S(1)} %gram.1.own_ref), channel_id=1, source_target_pairs={{0,1},{1,0},{2,3},{3,2},{4,5},{5,4},{6,7},{7,6},{8,9},{9,8},{10,11... | collective-permute-start | bytes 983048 | tf_op jit(solution)/shard_map/ppermute | solution.py:415
  44.7 7.2 %collective-permute-start.1 = (bf16[176,256]{1,0:T(8,128)(2,1)S(1)}, bf16[176,256]{1,0:T(8,128)(2,1)S(1)}, u32[]{:S(2)}, u32[]{:S(2)}) collective-permute-start(bf16[176,256]{1,0:T(8,128)(2,1)S(1)} %send_part.1.after_ref), channel_id=1, source_target_pairs={{0,2},{2,0},{1,3},{3,1},{4,6},{6,4},{5,7},{7,5},{8,10},{10,8},{9,1... | collective-permute-start | bytes 270344 | tf_op jit(solution)/shard_map/ppermute | solution.py:418
